TPU v7x, 128 devices: a whole 4x4x4 slice. The times are simulated.
128 devices in a mesh: row: 4 (over x_lo, core), col: 8 (over x_hi, y), tm: 4 (over z).
Axes of the slice: x: 4 (x_hi: 2, x_lo: 2; x = x_hi * 2 + x_lo), y: 4, z: 4, core: 2. Of those that a mesh axis runs over, the one named last changes fastest.
Arguments:
- right_sides: bfloat16 [8, 256, 16384], P(None, 'tm', ('row', 'col')), may hold values from -6 to 6
- eigen_basis: bfloat16 [16384, 16384], P('row', 'col'), may hold values from -0.046875 to 0.046875
- space_values: float32 [16384], P('col'), may hold values from 0.02 to 4
- time_basis: bfloat16 [256, 256], replicated, may hold values from -0.375 to 0.375
- time_values: float32 [256], replicated, may hold values from 0.05 to 4
- noise_level: float32 [1], replicated, may hold values from 0.05 to 0.5
Outputs:
- solved: float32 [8, 256, 16384], P(None, 'tm', ('row', 'col'))
All inputs are finite; a program needn't handle non-finite values.
Results may differ from a plain program's by a relative error of at most 0.0037.
Values may be sent and summed in bfloat16 or wider, within the bound.
No kernel may reach another device: no remote copies, remote signals or barrier semaphores. Data moves between devices by JAX's collectives and lax.ppermute only.
A program may use at most 128 MiB of HBM per device.

v0:
```python
import jax
import jax.numpy as jnp
from jax import lax
from jax.sharding import PartitionSpec as P


def shards(right_sides, eigen_basis, space_values, time_basis, time_values, noise_level):
    span = space_values.shape[0] // lax.axis_size("tm")
    value_part = lax.dynamic_slice_in_dim(space_values, lax.axis_index("tm") * span, span, 0)
    partial_value = jnp.einsum(
        "rts,si->rti",
        lax.all_gather(right_sides, "col", axis=2, tiled=True),
        eigen_basis,
        preferred_element_type=jnp.float32,
    )
    spectral = lax.psum(partial_value, "row").astype(jnp.bfloat16)
    mixed = jnp.einsum(
        "tj,kti->kji",
        time_basis,
        lax.all_to_all(spectral, "tm", split_axis=2, concat_axis=1, tiled=True),
        preferred_element_type=jnp.float32,
    )
    denom = value_part[None, None, :] * time_values[None, :, None] + noise_level[0]
    scaled = (mixed / denom).astype(jnp.bfloat16)
    own_part = lax.all_to_all(
        jnp.einsum("tj,kji->kti", time_basis, scaled, preferred_element_type=jnp.float32).astype(
            jnp.bfloat16
        ),
        "tm",
        split_axis=1,
        concat_axis=2,
        tiled=True,
    )
    terms = jnp.einsum("rti,si->rts", own_part, eigen_basis, preferred_element_type=jnp.float32)
    return lax.psum_scatter(terms, "col", scatter_dimension=2, tiled=True)


def solution(mesh):
    placed = (P(None, "tm", ("row", "col")), P("row", "col"), P("col"), P(), P(), P())
    return jax.shard_map(
        shards, mesh=mesh, in_specs=placed, out_specs=P(None, "tm", ("row", "col")), check_vma=False
    )
```

profile of v0, /device:TPU:0, one launch (start us, length us, event | category | flops | bytes accessed | tf_op | source)
XLA Modules:
  0.0 404.0 jit_solution(12070897886368147849)
XLA Ops:
  6.5 0.0 copy-start
  6.5 0.0 all-gather.2.cloned.1.call-start
  6.5 0.7 all-gather.2.cloned.1.call-update
  7.3 78.3 %all-gather.2.cloned.1.call-done = bf16[8,64,4096]{2,1,0:T(8,128)(2,1)} async-done(((bf16[8,64,512]{2,1,0:T(8,128)(2,1)}), bf16[8,64,4096]{2,1,0:T(8,128)(2,1)}) %all-gather.2.cloned.1.call-update) | async-done | bytes 4194320 | tf_op jit(solution)/shard_map/all_gather | solution.py:12
  85.6 15.0 %fusion.2 = f32[8,64,2048]{2,1,0:T(8,128)} fusion(bf16[8,64,4096]{2,1,0:T(8,128)(2,1)} %all-gather.2.cloned.1.call-done, bf16[4096,2048]{1,0:T(8,128)(2,1)} %param.7), kind=kOutput, calls=%fused_computation.2 | convolution fusion | flops 8589934592 | bytes 25165824 | tf_op jit(solution)/shard_map/rts,si->rti/dot_general | solution.py:10
  100.6 76.4 %all-reduce.1 = bf16[8,64,2048]{2,1,0:T(8,128)(2,1)S(1)} all-reduce(f32[8,64,2048]{2,1,0:T(8,128)} %fusion.2), channel_id=1, replica_groups=mesh['row'=4,'col'=8,'tm'=4] {'row'}, use_global_device_ids=true, to_apply=%region_0.0 | all-reduce | flops 1048576 | bytes 6291456 | tf_op jit(solution)/shard_map/psum | solution.py:16
  177.0 4.3 %copy.16 = bf16[8,64,2048]{1,0,2:T(8,128)(2,1)} copy(bf16[8,64,2048]{2,1,0:T(8,128)(2,1)S(1)} %all-reduce.1) | data formatting | bytes 4194304 | tf_op jit(solution)/shard_map/convert_element_type | solution.py:16
  181.3 0.0 copy-start.1
  181.3 5.9 %reshape.36 = bf16[4,2,131072]{2,1,0:T(2,128)(2,1)} reshape(bf16[2048,8,64]{2,1,0:T(8,128)(2,1)} %bitcast.30) | data formatting | bytes 4194304
  187.2 4.4 %all-to-all-start = ((bf16[4,2,131072]{2,1,0:T(2,128)(2,1)}), bf16[4,2,131072]{2,1,0:T(2,128)(2,1)S(1)}, u32[]{:S(2)}, u32[]{:S(2)}) async-start(bf16[4,2,131072]{2,1,0:T(2,128)(2,1)} %reshape.36), calls=%async_computation | async-start | bytes 4194304 | tf_op jit(solution)/shard_map/all_to_all | solution.py:20
  191.7 0.0 reduce-scatter.2.cloned.1.call-start
  192.3 0.8 dynamic_slice.3
  193.1 0.0 copy-done.1
  193.1 0.1 multiply_add_fusion
  193.2 25.3 %all-to-all-done = bf16[4,2,131072]{2,1,0:T(2,128)(2,1)S(1)} async-done(((bf16[4,2,131072]{2,1,0:T(2,128)(2,1)}), bf16[4,2,131072]{2,1,0:T(2,128)(2,1)S(1)}, u32[]{:S(2)}, u32[]{:S(2)}) %all-to-all-start) | async-done | bytes 2097184 | tf_op jit(solution)/shard_map/all_to_all | solution.py:20
  218.5 4.0 reshape.37
  222.5 5.2 %copy.24 = bf16[8,64,4,512]{3,2,1,0:T(4,128)(2,1)S(1)} copy(bf16[8,64,4,512]{1,0,3,2:T(8,128)(2,1)} %bitcast.31) | data formatting | bytes 4194304 | tf_op jit(solution)/shard_map/all_to_all | solution.py:20
  227.7 1.9 copy.18
  229.5 0.0 copy-done
  229.5 5.0 %convert_bitcast_fusion = bf16[8,256,512]{1,2,0:T(8,128)(2,1)} fusion(bf16[8,256,512]{2,1,0:T(8,128)(2,1)} %bitcast.34, f32[256,512]{0,1:T(8,128)S(1)} %multiply_add_fusion, bf16[256,256]{1,0:T(8,128)(2,1)S(1)} %copy-done), kind=kOutput, calls=%fused_computation.6 | convolution fusion | flops 1076887552 | bytes 4849664 | tf_op jit(solution)/shard_map/tj,kji->kti/dot_general | solution.py:26
  234.5 3.4 copy.20
  237.9 28.5 %all_to_all.36 = bf16[8,256,512]{2,0,1:T(8,128)(2,1)S(1)} all-to-all(bf16[8,256,512]{2,0,1:T(8,128)(2,1)S(1)} %copy.20), channel_id=1, replica_groups=mesh['row'=4,'col'=8,'tm'=4] {'tm'}, dimensions={1} | all-to-all | bytes 4194304 | tf_op jit(solution)/shard_map/all_to_all | solution.py:25
  266.4 1.6 copy.22
  268.0 2.8 all_to_all.33
  270.8 15.1 %fusion = f32[8,64,4096]{2,1,0:T(8,128)} fusion(bf16[8,64,2048]{2,1,0:T(8,128)(2,1)} %all_to_all.33, bf16[4096,2048]{1,0:T(8,128)(2,1)} %param.7), kind=kOutput, calls=%fused_computation | convolution fusion | flops 8589934592 | bytes 27262976 | tf_op jit(solution)/shard_map/rti,si->rts/dot_general | solution.py:34
  285.9 0.0 reduce-scatter.2.cloned.1.call-update
  285.9 111.2 %reduce-scatter.2.cloned.1.call-done = f32[8,64,512]{2,1,0:T(8,128)} async-done(((f32[8,64,4096]{2,1,0:T(8,128)}), f32[8,64,512]{2,1,0:T(8,128)}) %reduce-scatter.2.cloned.1.call-update) | async-done | bytes 1048592 | tf_op jit(solution)/shard_map/reduce_scatter | solution.py:35
Async XLA Ops:
  6.5 223.0 %copy-start = (bf16[256,256]{1,0:T(8,128)(2,1)S(1)}, bf16[256,256]{1,0:T(8,128)(2,1)}, u32[]{:S(2)}) copy-start(bf16[256,256]{1,0:T(8,128)(2,1)} %param.9) | copy-start | bytes 393220
  6.5 79.1 %all-gather.2.cloned.1.call-start = ((), (), s32[]{:S(2)}) async-start(), calls=%async_computation.3 | async-start | bytes 4718592 | tf_op jit(solution)/shard_map/all_gather | solution.py:12
  181.3 11.8 %copy-start.1 = (f32[256]{0:T(256)S(1)}, f32[256]{0:T(256)}, u32[]{:S(2)}) copy-start(f32[256]{0:T(256)} %param.10) | copy-start | bytes 3076
  187.2 31.3 %all-to-all-start = ((bf16[4,2,131072]{2,1,0:T(2,128)(2,1)}), bf16[4,2,131072]{2,1,0:T(2,128)(2,1)S(1)}, u32[]{:S(2)}, u32[]{:S(2)}) async-start(bf16[4,2,131072]{2,1,0:T(2,128)(2,1)} %reshape.36), calls=%async_computation | async-start | bytes 4194304 | tf_op jit(solution)/shard_map/all_to_all | solution.py:20
  191.7 205.5 %reduce-scatter.2.cloned.1.call-start = ((), (), s32[]{:S(2)}) async-start(), calls=%async_computation.4 | async-start | bytes 9437184 | tf_op jit(solution)/shard_map/reduce_scatter | solution.py:35
Sparse Core Ops, SparseCore 0:
  9.5 76.0 all-gather.1
  286.1 111.0 reduce-scatter.1
where the time goes:
time: 405 us; the launch traced here: 404 us
  waiting for transfers between devices  216 us (53%)
  blocking collectives  105 us (26%)
  matrix products  35.1 us (9%)
  local copies, waits for them, and re-layouts  29.8 us (7%)
  between operations  14.1 us (3%)
  starting transfers between devices  4.42 us (1%)
    reduce_scatter x1, waiting for transfers between devices, shards(): return lax.psum_scatter(terms, 'col', scatter_dimension=2, tiled=True)  111 us
    all_gather x1, waiting for transfers between devices, shards(): lax.all_gather(right_sides, 'col', axis=2, tiled=True)  78.3 us
    psum x1, blocking collectives, shards(): spectral = lax.psum(partial_value, 'row').astype(jnp.bfloat16)  76.4 us
    all_to_all x1, blocking collectives, shards(): lax.all_to_all(jnp.einsum('tj,kji->kti', time_basis, scaled, preferred_el...  28.5 us
    all_to_all x1, waiting for transfers between devices, shards(): lax.all_to_all(spectral, 'tm', split_axis=2, concat_axis=1, tiled=True)  25.3 us
    dot_general x1, matrix products, shards(): jnp.einsum('rti,si->rts', own_part, eigen_basis, preferred_element_type=j...  15.1 us
    dot_general x1, matrix products, shards(): jnp.einsum('rts,si->rti', lax.all_gather(right_sides, 'col', axis=2, tile...  15 us
    unnamed x6, local copies, waits for them, and re-layouts  9.92 us
  transfers between devices with their start and end apart: 3, of which 3 were waited for; matrix products, arithmetic and copies ran while one was open for 0% of the time, Pallas kernels for 0%

commit v1 on v0

v1 whole, which is shorter than its diff:
```python
import jax
import jax.numpy as jnp
from jax import lax
from jax.sharding import PartitionSpec as P

F32, BF16 = jnp.float32, jnp.bfloat16


def shards(right_sides, eigen_basis, space_values, time_basis, time_values, noise_level):
    rhs, nt, ns = right_sides.shape
    rows = rhs * nt
    basis = space_values.shape[0]
    row, col, tm = lax.axis_index("row"), lax.axis_index("col"), lax.axis_index("tm")
    x_lo, core, x_hi, y = row // 2, row % 2, col // 4, col % 4
    quarter = basis // 4

    def across_x(a):
        return lax.ppermute(a, "col", [(c, c ^ 4) for c in range(8)])

    def along_y(a, k):
        return lax.ppermute(a, "col", [(c, (c & 4) | ((c + k) & 3)) for c in range(8)])

    def along_z(a, k):
        return lax.ppermute(a, "tm", [(z, (z + k) & 3) for z in range(4)])

    def other_core(a):
        return lax.ppermute(a, "row", [(r, r ^ 1) for r in range(4)])

    def other_x(a):
        return lax.ppermute(a, "row", [(r, r ^ 2) for r in range(4)])

    def block(flip, step):
        at = (x_hi ^ flip) * 4 + ((y + step) & 3)
        return lax.dynamic_slice_in_dim(eigen_basis, at * ns, ns, 0)

    def project(a, flip, step):
        return lax.dot_general(
            a, block(flip, step), (((1,), (0,)), ((), ())), preferred_element_type=F32
        )

    own = right_sides.reshape(rows, ns)
    x0 = across_x(own)
    up, down = along_y(own, 1), along_y(own, -1)
    far = along_y(own, 2)
    total = project(own, 0, 0)
    total = total + project(up, 0, -1)
    total = total + project(down, 0, 1)
    x_up, x_down = along_y(x0, 1), along_y(x0, -1)
    total = total + project(x0, 1, 0)
    total = total + project(far, 0, 2)
    x_far = across_x(far)
    total = total + project(x_up, 1, -1)
    total = total + project(x_down, 1, 1)
    total = total + project(x_far, 1, 2)

    parts = total.reshape(2, 2, rhs // 4, nt, basis)
    pick = lax.dynamic_index_in_dim
    got = other_core(pick(parts, 1 - core, 1, False).astype(BF16))
    pair = pick(parts, core, 1, False) + got.astype(F32)
    got = other_x(pick(pair, 1 - x_lo, 0, False).astype(BF16))
    spectral = (pick(pair, x_lo, 0, False) + got.astype(F32)).astype(BF16)

    def lanes(a, z):
        return lax.dynamic_slice_in_dim(a, (z & 3) * quarter, quarter, a.ndim - 1)

    times = [lanes(spectral, tm)] + [along_z(lanes(spectral, tm + k), k) for k in (1, 2, 3)]
    times = jnp.concatenate(times, axis=1)
    turned = jnp.concatenate(
        [lax.dynamic_slice_in_dim(time_basis, ((tm - k) & 3) * nt, nt, 0) for k in range(4)], axis=0
    )
    mixed = jnp.einsum("tj,kti->kji", turned, times, preferred_element_type=F32)
    denom = lanes(space_values, tm)[None, None, :] * time_values[None, :, None] + noise_level[0]
    scaled = (mixed / denom).astype(BF16)
    back = jnp.einsum("tj,kji->kti", turned, scaled, preferred_element_type=F32).astype(BF16)
    pieces = [back[:, :nt]] + [along_z(back[:, k * nt : (k + 1) * nt], -k) for k in (1, 2, 3)]
    mine = jnp.zeros(spectral.shape, BF16)
    for k in range(4):
        mine = lax.dynamic_update_slice_in_dim(mine, pieces[k], ((tm + k) & 3) * quarter, 2)

    c1, c2 = other_core(mine), other_x(mine)
    c3 = other_core(c2)
    fields = jnp.zeros((4,) + mine.shape, BF16)
    for a, at in ((mine, row), (c1, row ^ 1), (c2, row ^ 2), (c3, row ^ 3)):
        fields = lax.dynamic_update_index_in_dim(fields, a, at, 0)
    fields = fields.reshape(rows, basis)

    def expand(flip, step):
        return lax.dot_general(
            fields, block(flip, step), (((1,), (1,)), ((), ())), preferred_element_type=F32
        )

    s_up = along_y(expand(1, 1).astype(BF16), 1)
    s_down = along_y(expand(1, -1).astype(BF16), -1)
    s_far = across_x(expand(1, 2).astype(BF16))
    o_up = along_y(expand(0, 1).astype(BF16), 1)
    o_down = along_y(expand(0, -1).astype(BF16), -1)
    o_x = across_x((expand(1, 0) + s_up.astype(F32) + s_down.astype(F32)).astype(BF16))
    o_far = along_y((expand(0, 2) + s_far.astype(F32)).astype(BF16), 2)
    out = expand(0, 0)
    for a in (o_up, o_down, o_x, o_far):
        out = out + a.astype(F32)
    return out.reshape(rhs, nt, ns)


def solution(mesh):
    placed = (P(None, "tm", ("row", "col")), P("row", "col"), P("col"), P(), P(), P())
    return jax.shard_map(
        shards, mesh=mesh, in_specs=placed, out_specs=P(None, "tm", ("row", "col")), check_vma=False
    )
```

time: 405 us -> 169 us (0.42)
  waiting for transfers between devices: 216 us -> 64.2 us
  blocking collectives: 105 us -> 0 us
  starting transfers between devices: 4.42 us -> 35.8 us
  matrix products: 35.1 us -> 62.8 us
  local copies, waits for them, and re-layouts: 29.8 us -> 3.23 us
  between operations: 14.1 us -> 0.96 us
    reduce_scatter x1 -> x0, waiting for transfers between devices: 111 us -> none  [shards(): return lax.psum_scatter(terms, 'col', scatter_dimension=2, tiled=True)]
    all_gather x1 -> x0, waiting for transfers between devices: 78.3 us -> none  [shards(): lax.all_gather(right_sides, 'col', axis=2, tiled=True)]
    psum x1 -> x0, blocking collectives: 76.4 us -> none  [shards(): spectral = lax.psum(partial_value, 'row').astype(jnp.bfloat16)]
    ppermute x0 -> x25, waiting for transfers between devices: none -> 64.2 us  [the longest x2 24.3 us: other_x(): return lax.ppermute(a, 'row', [(r, r ^ 2) for r in range(4)])]
    ppermute x0 -> x25, starting transfers between devices: none -> 35.8 us  [the longest x10 17.1 us: along_y(): return lax.ppermute(a, 'col', [(c, c & 4 | c + k & 3) for c in range(8)])]
    all_to_all x1 -> x0, blocking collectives: 28.5 us -> none  [shards(): lax.all_to_all(jnp.einsum('tj,kji->kti', time_basis, scaled, preferred_el...]
    dot_general x3 -> x17, matrix products: 35.1 us -> 62.8 us  [the longest x8 43.9 us: project(): lax.dot_general(a, block(flip, step), (((1,), (0,)), ((), ())), preferred...]
    all_to_all x1 -> x0, waiting for transfers between devices: 25.3 us -> none  [shards(): lax.all_to_all(spectral, 'tm', split_axis=2, concat_axis=1, tiled=True)]
  transfers between devices with their start and end apart: 3 -> 25, of which waited for: 3 -> 20; matrix products, arithmetic and copies ran while one was open for 0% -> 23% of each run, Pallas kernels for 0% -> 0%
where the time goes in v1:
time: 169 us
  waiting for transfers between devices  64.2 us (38%)
  matrix products  62.8 us (37%)
  starting transfers between devices  35.8 us (21%)
  local copies, waits for them, and re-layouts  3.23 us (2%)
  other arithmetic  2.05 us (1%)
    dot_general x8, matrix products, project(): lax.dot_general(a, block(flip, step), (((1,), (0,)), ((), ())), preferred...  43.9 us
    ppermute x2, waiting for transfers between devices, other_x(): return lax.ppermute(a, 'row', [(r, r ^ 2) for r in range(4)])  24.3 us
    dot_general x8, matrix products, expand(): lax.dot_general(fields, block(flip, step), (((1,), (1,)), ((), ())), pref...  18.3 us
    ppermute x10, starting transfers between devices, along_y(): return lax.ppermute(a, 'col', [(c, c & 4 | c + k & 3) for c in range(8)])  17.1 us
    ppermute x10, waiting for transfers between devices, along_y(): return lax.ppermute(a, 'col', [(c, c & 4 | c + k & 3) for c in range(8)])  13.9 us
    ppermute x6, waiting for transfers between devices, along_z(): return lax.ppermute(a, 'tm', [(z, z + k & 3) for z in range(4)])  12.1 us
    ppermute x6, starting transfers between devices, along_z(): return lax.ppermute(a, 'tm', [(z, z + k & 3) for z in range(4)])  9.61 us
    ppermute x4, waiting for transfers between devices, across_x(): return lax.ppermute(a, 'col', [(c, c ^ 4) for c in range(8)])  9.55 us
  transfers between devices with their start and end apart: 25, of which 20 were waited for; matrix products, arithmetic and copies ran while one was open for 23% of the time, Pallas kernels for 0%

profile of v1, /device:TPU:0, one launch (start us, length us, event | category | flops | bytes accessed | tf_op | source)
XLA Modules:
  0.0 169.1 jit_solution(409569345175697191)
XLA Ops:
  0.0 3.1 %collective-permute-start.2 = (bf16[512,512]{1,0:T(8,128)(2,1)}, bf16[512,512]{1,0:T(8,128)(2,1)}, u32[]{:S(2)}, u32[]{:S(2)}) collective-permute-start(bf16[512,512]{1,0:T(8,128)(2,1)} %bitcast.68), channel_id=1, source_target_pairs={{0,16},{4,20},{8,24},{12,28},{16,0},{20,4},{24,8},{28,12},{1,17},{... | collective-permute-start | bytes 1572872 | tf_op jit(solution)/shard_map/ppermute | solution.py:18
  3.1 3.2 %collective-permute-start.3 = (bf16[512,512]{1,0:T(8,128)(2,1)}, bf16[512,512]{1,0:T(8,128)(2,1)S(1)}, u32[]{:S(2)}, u32[]{:S(2)}) collective-permute-start(bf16[512,512]{1,0:T(8,128)(2,1)} %bitcast.69), channel_id=1, source_target_pairs={{0,8},{4,12},{8,0},{12,4},{16,24},{20,28},{24,16},{28,20},{1,9},{5... | collective-permute-start | bytes 1572872 | tf_op jit(solution)/shard_map/ppermute | solution.py:21
  8.3 5.3 %fusion.32 = f32[2048,512]{0,1:T(8,128)} fusion(bf16[512,512]{1,0:T(8,128)(2,1)} %bitcast.72, bf16[4096,2048]{1,0:T(8,128)(2,1)} %param.7, s32[]{:T(128)S(6)} %select_n.108), kind=kOutput, calls=%fused_computation.33 | convolution fusion | flops 1073741824 | bytes 6815748 | tf_op jit(solution)/shard_map/dot_general | solution.py:37
  13.6 1.7 %collective-permute-done.2 = bf16[512,512]{1,0:T(8,128)(2,1)} collective-permute-done((bf16[512,512]{1,0:T(8,128)(2,1)}, bf16[512,512]{1,0:T(8,128)(2,1)}, u32[]{:S(2)}, u32[]{:S(2)}) %collective-permute-start.2) | collective-permute-done | bytes 524320 | tf_op jit(solution)/shard_map/ppermute | solution.py:18
  15.3 1.8 %collective-permute-start.4 = (bf16[512,512]{1,0:T(8,128)(2,1)}, bf16[512,512]{1,0:T(8,128)(2,1)S(1)}, u32[]{:S(2)}, u32[]{:S(2)}) collective-permute-start(bf16[512,512]{1,0:T(8,128)(2,1)} %collective-permute-done.2), channel_id=1, source_target_pairs={{0,4},{4,8},{8,12},{12,0},{16,20},{20,24},{24,28},{28,16},{1,5},{5... | collective-permute-start | bytes 1572872 | tf_op jit(solution)/shard_map/ppermute | solution.py:21
  17.1 1.4 collective-permute-start.5
  18.6 1.1 collective-permute-done.3
  19.7 2.1 %collective-permute-start.6 = (bf16[512,512]{1,0:T(8,128)(2,1)S(1)}, bf16[512,512]{1,0:T(8,128)(2,1)S(1)}, u32[]{:S(2)}, u32[]{:S(2)}) collective-permute-start(bf16[512,512]{1,0:T(8,128)(2,1)S(1)} %collective-permute-done.3), channel_id=1, source_target_pairs={{0,16},{4,20},{8,24},{12,28},{16,0},{20,4},{24,8},{28,12},{1,17},{... | collective-permute-start | bytes 1572872 | tf_op jit(solution)/shard_map/ppermute | solution.py:18
  21.8 4.9 %fusion.16 = f32[2048,512]{0,1:T(8,128)} fusion(bf16[512,512]{1,0:T(8,128)(2,1)S(1)} %collective-permute-done.3, bf16[4096,2048]{1,0:T(8,128)(2,1)} %param.7, s32[]{:T(128)S(6)} %select_n.112), kind=kOutput, calls=%fused_computation.17 | convolution fusion | flops 1073741824 | bytes 6815748 | tf_op jit(solution)/shard_map/dot_general | solution.py:37
  26.7 5.0 %fusion.20 = f32[2048,512]{0,1:T(8,128)} fusion(bf16[512,512]{1,0:T(8,128)(2,1)} %collective-permute-done.2, bf16[4096,2048]{1,0:T(8,128)(2,1)} %param.7, s32[]{:T(128)S(6)} %select_n.111), kind=kOutput, calls=%fused_computation.21 | convolution fusion | flops 1073741824 | bytes 6815748 | tf_op jit(solution)/shard_map/dot_general | solution.py:37
  31.7 4.3 %fusion.24 = f32[2048,512]{0,1:T(8,128)} fusion(bf16[512,512]{1,0:T(8,128)(2,1)} %collective-permute-done.1, bf16[4096,2048]{1,0:T(8,128)(2,1)S(1)} %copy-done, s32[]{:T(128)S(6)} %select_n.110), kind=kOutput, calls=%fused_computation.25 | convolution fusion | flops 1073741824 | bytes 6815748 | tf_op jit(solution)/shard_map/dot_general | solution.py:37
  36.1 4.3 %fusion.28 = f32[2048,512]{0,1:T(8,128)} fusion(bf16[512,512]{1,0:T(8,128)(2,1)} %collective-permute-done, bf16[4096,2048]{1,0:T(8,128)(2,1)S(1)} %copy-done, s32[]{:T(128)S(6)} %select_n.109), kind=kOutput, calls=%fused_computation.29 | convolution fusion | flops 1073741824 | bytes 6815748 | tf_op jit(solution)/shard_map/dot_general | solution.py:37
  40.7 3.3 %fusion.12 = f32[2048,512]{0,1:T(8,128)} fusion(bf16[512,512]{1,0:T(8,128)(2,1)S(1)} %collective-permute-done.4, bf16[4096,2048]{1,0:T(8,128)(2,1)S(1)} %copy-done, s32[]{:T(128)S(6)} %select_n.113), kind=kOutput, calls=%fused_computation.13 | convolution fusion | flops 1073741824 | bytes 6815748 | tf_op jit(solution)/shard_map/dot_general | solution.py:37
  44.0 3.3 %fusion.8 = f32[2048,512]{0,1:T(8,128)} fusion(bf16[512,512]{1,0:T(8,128)(2,1)S(1)} %collective-permute-done.5, bf16[4096,2048]{1,0:T(8,128)(2,1)S(1)} %copy-done, s32[]{:T(128)S(6)} %select_n.114), kind=kOutput, calls=%fused_computation.9 | convolution fusion | flops 1073741824 | bytes 6815748 | tf_op jit(solution)/shard_map/dot_general | solution.py:37
  47.2 13.5 %add_add_fusion = f32[2048,512]{0,1:T(8,128)} fusion(f32[2048,512]{0,1:T(8,128)} %fusion.8, f32[2048,512]{0,1:T(8,128)} %fusion.12, f32[2048,512]{0,1:T(8,128)} %fusion.16, f32[2048,512]{0,1:T(8,128)} %fusion.20, f32[2048,512]{0,1:T(8,128)} %fusion.24, f32[2048,512]{0,1:T(8,128)} %fusion.32, f32[2048,512]{0,1:T(8,128)} %fusion.28, ...), kind=kOutput, calls=%fused_computation | convolution fusion | flops 1081081856 | bytes 36175876 | tf_op jit(solution)/shard_map/dot_general | solution.py:37
  60.8 1.7 %fusion.79 = bf16[2,2,64,2048]{3,2,1,0:T(8,128)(2,1)S(1)} fusion(f32[2,2,2,64,2048]{4,3,2,1,0:T(8,128)} %bitcast.58, s32[]{:T(128)S(6)} %select_n.118), kind=kLoop, calls=%fused_computation.54 | loop fusion | bytes 2097156 | tf_op jit(solution)/shard_map/convert_element_type | solution.py:58
  62.6 2.6 %collective-permute-done.7 = bf16[2,2,64,2048]{3,2,1,0:T(8,128)(2,1)S(1)} collective-permute-done((bf16[2,2,64,2048]{3,2,1,0:T(8,128)(2,1)S(1)}, bf16[2,2,64,2048]{3,2,1,0:T(8,128)(2,1)S(1)}, u32[]{:S(2)}, u32[]{:S(2)}) %collective-permute-start.7) | collective-permute-done | bytes 1048608 | tf_op jit(solution)/shard_map/ppermute | solution.py:27
  65.3 1.8 %bitcast_add_fusion = f32[2,2,64,2048]{3,2,1,0:T(8,128)S(1)} fusion(bf16[2,2,64,2048]{3,2,1,0:T(8,128)(2,1)S(1)} %collective-permute-done.7, f32[2,2,2,64,2048]{4,3,2,1,0:T(8,128)} %bitcast.59, s32[]{:T(128)S(6)} %select_n.117), kind=kLoop, calls=%fused_computation.1 | loop fusion | flops 1048576 | bytes 5242884 | tf_op jit(solution)/shard_map/add | solution.py:59
  69.5 11.9 %collective-permute-done.8 = bf16[2,64,2048]{2,1,0:T(8,128)(2,1)S(1)} collective-permute-done((bf16[2,64,2048]{2,1,0:T(8,128)(2,1)S(1)}, bf16[2,64,2048]{2,1,0:T(8,128)(2,1)S(1)}, u32[]{:S(2)}, u32[]{:S(2)}) %collective-permute-start.8) | collective-permute-done | bytes 524320 | tf_op jit(solution)/shard_map/ppermute | solution.py:30
  81.6 4.0 %collective-permute-start.10 = (bf16[2,64,512]{2,1,0:T(8,128)(2,1)S(1)}, bf16[2,64,512]{2,1,0:T(8,128)(2,1)S(1)}, u32[]{:S(2)}, u32[]{:S(2)}) collective-permute-start(bf16[2,64,512]{2,1,0:T(8,128)(2,1)S(1)} %get-tuple-element.11), channel_id=1, source_target_pairs={{0,2},{1,3},{2,0},{3,1},{4,6},{5,7},{6,4},{7,5},{8,10},{9,11},{10,... | collective-permute-start | bytes 393224 | tf_op jit(solution)/shard_map/ppermute | solution.py:24
  86.3 1.3 collective-permute-start.9
  87.8 1.5 collective-permute-done.10
  89.3 2.9 %collective-permute-done.11 = bf16[2,64,512]{2,1,0:T(8,128)(2,1)S(1)} collective-permute-done((bf16[2,64,512]{2,1,0:T(8,128)(2,1)S(1)}, bf16[2,64,512]{2,1,0:T(8,128)(2,1)S(1)}, u32[]{:S(2)}, u32[]{:S(2)}) %collective-permute-start.11) | collective-permute-done | bytes 131104 | tf_op jit(solution)/shard_map/ppermute | solution.py:24
  93.1 2.3 %collective-permute-start.12 = (bf16[2,64,512]{2,1,0:T(8,128)(2,1)S(1)}, bf16[2,64,512]{2,1,0:T(8,128)(2,1)S(1)}, u32[]{:S(2)}, u32[]{:S(2)}) collective-permute-start(bf16[2,64,512]{2,1,0:T(8,128)(2,1)S(1)} %get-tuple-element.7), channel_id=1, source_target_pairs={{0,3},{1,0},{2,1},{3,2},{4,7},{5,4},{6,5},{7,6},{8,11},{9,8},{10,9... | collective-permute-start | bytes 393224 | tf_op jit(solution)/shard_map/ppermute | solution.py:24
  96.8 4.1 %collective-permute-done.12 = bf16[2,64,512]{2,1,0:T(8,128)(2,1)S(1)} collective-permute-done((bf16[2,64,512]{2,1,0:T(8,128)(2,1)S(1)}, bf16[2,64,512]{2,1,0:T(8,128)(2,1)S(1)}, u32[]{:S(2)}, u32[]{:S(2)}) %collective-permute-start.12) | collective-permute-done | bytes 131104 | tf_op jit(solution)/shard_map/ppermute | solution.py:24
  100.9 2.3 %collective-permute-done.13 = bf16[2,64,512]{2,1,0:T(8,128)(2,1)S(1)} collective-permute-done((bf16[2,64,512]{2,1,0:T(8,128)(2,1)S(1)}, bf16[2,64,512]{2,1,0:T(8,128)(2,1)S(1)}, u32[]{:S(2)}, u32[]{:S(2)}) %collective-permute-start.13) | collective-permute-done | bytes 131104 | tf_op jit(solution)/shard_map/ppermute | solution.py:24
  105.3 12.3 %collective-permute-done.16 = bf16[2,64,2048]{2,1,0:T(8,128)(2,1)S(1)} collective-permute-done((bf16[2,64,2048]{2,1,0:T(8,128)(2,1)S(1)}, bf16[2,64,2048]{2,1,0:T(8,128)(2,1)S(1)}, u32[]{:S(2)}, u32[]{:S(2)}) %collective-permute-start.16) | collective-permute-done | bytes 524320 | tf_op jit(solution)/shard_map/ppermute | solution.py:30
  117.7 1.8 %collective-permute-done.17 = bf16[2,64,2048]{2,1,0:T(8,128)(2,1)S(1)} collective-permute-done((bf16[2,64,2048]{2,1,0:T(8,128)(2,1)S(1)}, bf16[2,64,2048]{2,1,0:T(8,128)(2,1)S(1)}, u32[]{:S(2)}, u32[]{:S(2)}) %collective-permute-start.17) | collective-permute-done | bytes 524320 | tf_op jit(solution)/shard_map/ppermute | solution.py:27
  119.5 3.0 %fusion.68 = bf16[512,512]{1,0:T(8,128)(2,1)S(1)} fusion(bf16[512,2048]{1,0:T(8,128)(2,1)S(1)} %bitcast.60, bf16[4096,2048]{1,0:T(8,128)(2,1)} %param.7, s32[]{:T(128)S(6)} %select_n.114), kind=kOutput, calls=%fused_computation.48 | convolution fusion | flops 1074003968 | bytes 4718596 | tf_op jit(solution)/shard_map/dot_general | solution.py:88
  122.6 3.0 %fusion.65 = bf16[512,512]{1,0:T(8,128)(2,1)S(1)} fusion(bf16[512,2048]{1,0:T(8,128)(2,1)S(1)} %bitcast.61, bf16[4096,2048]{1,0:T(8,128)(2,1)} %param.7, s32[]{:T(128)S(6)} %select_n.113), kind=kOutput, calls=%fused_computation.47 | convolution fusion | flops 1074003968 | bytes 4718596 | tf_op jit(solution)/shard_map/dot_general | solution.py:88
  125.7 3.0 %fusion.71 = bf16[512,512]{1,0:T(8,128)(2,1)S(1)} fusion(bf16[512,2048]{1,0:T(8,128)(2,1)S(1)} %bitcast.62, bf16[4096,2048]{1,0:T(8,128)(2,1)} %param.7, s32[]{:T(128)S(6)} %select_n.115), kind=kOutput, calls=%fused_computation.49 | convolution fusion | flops 1074003968 | bytes 4718596 | tf_op jit(solution)/shard_map/dot_general | solution.py:88
  128.7 1.8 %collective-permute-start.20 = (bf16[512,512]{1,0:T(8,128)(2,1)S(1)}, bf16[512,512]{1,0:T(8,128)(2,1)S(1)}, u32[]{:S(2)}, u32[]{:S(2)}) collective-permute-start(bf16[512,512]{1,0:T(8,128)(2,1)S(1)} %fusion.68), channel_id=1, source_target_pairs={{0,4},{4,8},{8,12},{12,0},{16,20},{20,24},{24,28},{28,16},{1,5},{5... | collective-permute-start | bytes 1572872 | tf_op jit(solution)/shard_map/ppermute | solution.py:21
  130.5 1.5 collective-permute-start.21
  132.0 2.9 %fusion.62 = bf16[512,512]{1,0:T(8,128)(2,1)S(1)} fusion(bf16[512,2048]{1,0:T(8,128)(2,1)S(1)} %bitcast.63, bf16[4096,2048]{1,0:T(8,128)(2,1)} %param.7, s32[]{:T(128)S(6)} %select_n.110), kind=kOutput, calls=%fused_computation.46 | convolution fusion | flops 1074003968 | bytes 4718596 | tf_op jit(solution)/shard_map/dot_general | solution.py:88
  134.9 1.2 collective-permute-start.23
  136.1 1.3 fusion.59
  137.9 2.9 %collective-permute-start.19 = (bf16[512,512]{1,0:T(8,128)(2,1)S(1)}, bf16[512,512]{1,0:T(8,128)(2,1)S(1)}, u32[]{:S(2)}, u32[]{:S(2)}) collective-permute-start(bf16[512,512]{1,0:T(8,128)(2,1)S(1)} %fusion.59), channel_id=1, source_target_pairs={{0,12},{4,0},{8,4},{12,8},{16,28},{20,16},{24,20},{28,24},{1,13},{... | collective-permute-start | bytes 1572872 | tf_op jit(solution)/shard_map/ppermute | solution.py:21
  140.7 4.0 %collective-permute-done.20 = bf16[512,512]{1,0:T(8,128)(2,1)S(1)} collective-permute-done((bf16[512,512]{1,0:T(8,128)(2,1)S(1)}, bf16[512,512]{1,0:T(8,128)(2,1)S(1)}, u32[]{:S(2)}, u32[]{:S(2)}) %collective-permute-start.20) | collective-permute-done | bytes 524320 | tf_op jit(solution)/shard_map/ppermute | solution.py:21
  145.3 1.3 fusion.56
  146.6 1.1 collective-permute-start.22
  147.7 3.3 %collective-permute-done.23 = bf16[512,512]{1,0:T(8,128)(2,1)S(1)} collective-permute-done((bf16[512,512]{1,0:T(8,128)(2,1)S(1)}, bf16[512,512]{1,0:T(8,128)(2,1)S(1)}, u32[]{:S(2)}, u32[]{:S(2)}) %collective-permute-start.23) | collective-permute-done | bytes 524320 | tf_op jit(solution)/shard_map/ppermute | solution.py:18
  150.9 1.3 fusion.74
  152.2 2.0 %collective-permute-start.24 = (bf16[512,512]{1,0:T(8,128)(2,1)S(1)}, bf16[512,512]{1,0:T(8,128)(2,1)S(1)}, u32[]{:S(2)}, u32[]{:S(2)}) collective-permute-start(bf16[512,512]{1,0:T(8,128)(2,1)S(1)} %fusion.74), channel_id=1, source_target_pairs={{0,8},{4,12},{8,0},{12,4},{16,24},{20,28},{24,16},{28,20},{1,9},{5... | collective-permute-start | bytes 1572872 | tf_op jit(solution)/shard_map/ppermute | solution.py:21
  154.2 1.2 collective-permute-done.18
  155.4 1.1 collective-permute-done.19
  156.5 4.6 %collective-permute-done.22 = bf16[512,512]{1,0:T(8,128)(2,1)S(1)} collective-permute-done((bf16[512,512]{1,0:T(8,128)(2,1)S(1)}, bf16[512,512]{1,0:T(8,128)(2,1)S(1)}, u32[]{:S(2)}, u32[]{:S(2)}) %collective-permute-start.22) | collective-permute-done | bytes 524320 | tf_op jit(solution)/shard_map/ppermute | solution.py:18
  161.1 5.5 %collective-permute-done.24 = bf16[512,512]{1,0:T(8,128)(2,1)S(1)} collective-permute-done((bf16[512,512]{1,0:T(8,128)(2,1)S(1)}, bf16[512,512]{1,0:T(8,128)(2,1)S(1)}, u32[]{:S(2)}, u32[]{:S(2)}) %collective-permute-start.24) | collective-permute-done | bytes 524320 | tf_op jit(solution)/shard_map/ppermute | solution.py:21
  166.7 2.4 %fusion.53 = f32[512,512]{1,0:T(8,128)} fusion(bf16[512,2048]{1,0:T(8,128)(2,1)S(1)} %bitcast.67, bf16[4096,2048]{1,0:T(8,128)(2,1)S(1)} %bitcast.57, s32[]{:T(128)S(6)} %select_n.108, bf16[512,512]{1,0:T(8,128)(2,1)S(1)} %collective-permute-done.24, bf16[512,512]{1,0:T(8,128)(2,1)S(1)} %collective-permute-done.22, ...), kind=kOutput, calls=%fused_computation.43 | convolution fusion | flops 1075838976 | bytes 7340036 | tf_op jit(solution)/shard_map/dot_general | solution.py:88
  (52 shorter events, 10.6 us)
Async XLA Ops:
  0.0 15.3 %collective-permute-start.2 = (bf16[512,512]{1,0:T(8,128)(2,1)}, bf16[512,512]{1,0:T(8,128)(2,1)}, u32[]{:S(2)}, u32[]{:S(2)}) collective-permute-start(bf16[512,512]{1,0:T(8,128)(2,1)} %bitcast.68), channel_id=1, source_target_pairs={{0,16},{4,20},{8,24},{12,28},{16,0},{20,4},{24,8},{28,12},{1,17},{... | collective-permute-start | bytes 1572872 | tf_op jit(solution)/shard_map/ppermute | solution.py:18
  3.1 16.6 %collective-permute-start.3 = (bf16[512,512]{1,0:T(8,128)(2,1)}, bf16[512,512]{1,0:T(8,128)(2,1)S(1)}, u32[]{:S(2)}, u32[]{:S(2)}) collective-permute-start(bf16[512,512]{1,0:T(8,128)(2,1)} %bitcast.69), channel_id=1, source_target_pairs={{0,8},{4,12},{8,0},{12,4},{16,24},{20,28},{24,16},{28,20},{1,9},{5... | collective-permute-start | bytes 1572872 | tf_op jit(solution)/shard_map/ppermute | solution.py:21
  6.3 25.4 %collective-permute-start.1 = (bf16[512,512]{1,0:T(8,128)(2,1)}, bf16[512,512]{1,0:T(8,128)(2,1)}, u32[]{:S(2)}, u32[]{:S(2)}) collective-permute-start(bf16[512,512]{1,0:T(8,128)(2,1)} %bitcast.70), channel_id=1, source_target_pairs={{0,12},{4,0},{8,4},{12,8},{16,28},{20,16},{24,20},{28,24},{1,13},{... | collective-permute-start | bytes 1572872 | tf_op jit(solution)/shard_map/ppermute | solution.py:21
  7.4 28.7 %collective-permute-start = (bf16[512,512]{1,0:T(8,128)(2,1)}, bf16[512,512]{1,0:T(8,128)(2,1)}, u32[]{:S(2)}, u32[]{:S(2)}) collective-permute-start(bf16[512,512]{1,0:T(8,128)(2,1)} %bitcast.71), channel_id=1, source_target_pairs={{0,4},{4,8},{8,12},{12,0},{16,20},{20,24},{24,28},{28,16},{1,5},{5... | collective-permute-start | bytes 1572872 | tf_op jit(solution)/shard_map/ppermute | solution.py:21
  8.3 23.4 %copy-start = (bf16[4096,2048]{1,0:T(8,128)(2,1)S(1)}, bf16[4096,2048]{1,0:T(8,128)(2,1)}, u32[]{:S(2)}) copy-start(bf16[4096,2048]{1,0:T(8,128)(2,1)} %param.7) | copy-start | bytes 50331652
  15.3 25.4 %collective-permute-start.4 = (bf16[512,512]{1,0:T(8,128)(2,1)}, bf16[512,512]{1,0:T(8,128)(2,1)S(1)}, u32[]{:S(2)}, u32[]{:S(2)}) collective-permute-start(bf16[512,512]{1,0:T(8,128)(2,1)} %collective-permute-done.2), channel_id=1, source_target_pairs={{0,4},{4,8},{8,12},{12,0},{16,20},{20,24},{24,28},{28,16},{1,5},{5... | collective-permute-start | bytes 1572872 | tf_op jit(solution)/shard_map/ppermute | solution.py:21
  17.1 26.8 %collective-permute-start.5 = (bf16[512,512]{1,0:T(8,128)(2,1)}, bf16[512,512]{1,0:T(8,128)(2,1)S(1)}, u32[]{:S(2)}, u32[]{:S(2)}) collective-permute-start(bf16[512,512]{1,0:T(8,128)(2,1)} %collective-permute-done.2), channel_id=1, source_target_pairs={{0,12},{4,0},{8,4},{12,8},{16,28},{20,16},{24,20},{28,24},{1,13},{... | collective-permute-start | bytes 1572872 | tf_op jit(solution)/shard_map/ppermute | solution.py:21
  19.7 27.5 %collective-permute-start.6 = (bf16[512,512]{1,0:T(8,128)(2,1)S(1)}, bf16[512,512]{1,0:T(8,128)(2,1)S(1)}, u32[]{:S(2)}, u32[]{:S(2)}) collective-permute-start(bf16[512,512]{1,0:T(8,128)(2,1)S(1)} %collective-permute-done.3), channel_id=1, source_target_pairs={{0,16},{4,20},{8,24},{12,28},{16,0},{20,4},{24,8},{28,12},{1,17},{... | collective-permute-start | bytes 1572872 | tf_op jit(solution)/shard_map/ppermute | solution.py:18
  62.5 2.7 %collective-permute-start.7 = (bf16[2,2,64,2048]{3,2,1,0:T(8,128)(2,1)S(1)}, bf16[2,2,64,2048]{3,2,1,0:T(8,128)(2,1)S(1)}, u32[]{:S(2)}, u32[]{:S(2)}) collective-permute-start(bf16[2,2,64,2048]{3,2,1,0:T(8,128)(2,1)S(1)} %fusion.79), channel_id=1, source_target_pairs={{0,32},{32,0},{64,96},{96,64},{1,33},{33,1},{65,97},{97,65},{2,34}... | collective-permute-start | bytes 3145736 | tf_op jit(solution)/shard_map/ppermute | solution.py:27
  67.1 20.5 %copy-start.2 = (f32[256]{0:T(256)S(1)}, f32[256]{0:T(256)}, u32[]{:S(2)}) copy-start(f32[256]{0:T(256)} %param.10) | copy-start | bytes 3076
  67.2 20.5 %copy-start.1 = (bf16[256,256]{1,0:T(8,128)(2,1)S(1)}, bf16[256,256]{1,0:T(8,128)(2,1)}, u32[]{:S(2)}) copy-start(bf16[256,256]{1,0:T(8,128)(2,1)} %param.9) | copy-start | bytes 393220
  67.2 14.2 %collective-permute-start.8 = (bf16[2,64,2048]{2,1,0:T(8,128)(2,1)S(1)}, bf16[2,64,2048]{2,1,0:T(8,128)(2,1)S(1)}, u32[]{:S(2)}, u32[]{:S(2)}) collective-permute-start(bf16[2,64,2048]{2,1,0:T(8,128)(2,1)S(1)} %fusion.81), channel_id=1, source_target_pairs={{0,64},{32,96},{64,0},{96,32},{1,65},{33,97},{65,1},{97,33},{2,66}... | collective-permute-start | bytes 1572872 | tf_op jit(solution)/shard_map/ppermute | solution.py:30
  81.6 7.7 %collective-permute-start.10 = (bf16[2,64,512]{2,1,0:T(8,128)(2,1)S(1)}, bf16[2,64,512]{2,1,0:T(8,128)(2,1)S(1)}, u32[]{:S(2)}, u32[]{:S(2)}) collective-permute-start(bf16[2,64,512]{2,1,0:T(8,128)(2,1)S(1)} %get-tuple-element.11), channel_id=1, source_target_pairs={{0,2},{1,3},{2,0},{3,1},{4,6},{5,7},{6,4},{7,5},{8,10},{9,11},{10,... | collective-permute-start | bytes 393224 | tf_op jit(solution)/shard_map/ppermute | solution.py:24
  85.6 6.5 %collective-permute-start.11 = (bf16[2,64,512]{2,1,0:T(8,128)(2,1)S(1)}, bf16[2,64,512]{2,1,0:T(8,128)(2,1)S(1)}, u32[]{:S(2)}, u32[]{:S(2)}) collective-permute-start(bf16[2,64,512]{2,1,0:T(8,128)(2,1)S(1)} %get-tuple-element.10), channel_id=1, source_target_pairs={{0,3},{1,0},{2,1},{3,2},{4,7},{5,4},{6,5},{7,6},{8,11},{9,8},{10,9... | collective-permute-start | bytes 393224 | tf_op jit(solution)/shard_map/ppermute | solution.py:24
  86.3 6.2 %collective-permute-start.9 = (bf16[2,64,512]{2,1,0:T(8,128)(2,1)S(1)}, bf16[2,64,512]{2,1,0:T(8,128)(2,1)S(1)}, u32[]{:S(2)}, u32[]{:S(2)}) collective-permute-start(bf16[2,64,512]{2,1,0:T(8,128)(2,1)S(1)} %get-tuple-element.12), channel_id=1, source_target_pairs={{0,1},{1,2},{2,3},{3,0},{4,5},{5,6},{6,7},{7,4},{8,9},{9,10},{10,1... | collective-permute-start | bytes 393224 | tf_op jit(solution)/shard_map/ppermute | solution.py:24
  93.1 7.7 %collective-permute-start.12 = (bf16[2,64,512]{2,1,0:T(8,128)(2,1)S(1)}, bf16[2,64,512]{2,1,0:T(8,128)(2,1)S(1)}, u32[]{:S(2)}, u32[]{:S(2)}) collective-permute-start(bf16[2,64,512]{2,1,0:T(8,128)(2,1)S(1)} %get-tuple-element.7), channel_id=1, source_target_pairs={{0,3},{1,0},{2,1},{3,2},{4,7},{5,4},{6,5},{7,6},{8,11},{9,8},{10,9... | collective-permute-start | bytes 393224 | tf_op jit(solution)/shard_map/ppermute | solution.py:24
  95.5 7.7 %collective-permute-start.13 = (bf16[2,64,512]{2,1,0:T(8,128)(2,1)S(1)}, bf16[2,64,512]{2,1,0:T(8,128)(2,1)S(1)}, u32[]{:S(2)}, u32[]{:S(2)}) collective-permute-start(bf16[2,64,512]{2,1,0:T(8,128)(2,1)S(1)} %get-tuple-element.6), channel_id=1, source_target_pairs={{0,2},{1,3},{2,0},{3,1},{4,6},{5,7},{6,4},{7,5},{8,10},{9,11},{10,... | collective-permute-start | bytes 393224 | tf_op jit(solution)/shard_map/ppermute | solution.py:24
  96.0 8.3 %collective-permute-start.14 = (bf16[2,64,512]{2,1,0:T(8,128)(2,1)S(1)}, bf16[2,64,512]{2,1,0:T(8,128)(2,1)S(1)}, u32[]{:S(2)}, u32[]{:S(2)}) collective-permute-start(bf16[2,64,512]{2,1,0:T(8,128)(2,1)S(1)} %get-tuple-element.5), channel_id=1, source_target_pairs={{0,1},{1,2},{2,3},{3,0},{4,5},{5,6},{6,7},{7,4},{8,9},{9,10},{10,1... | collective-permute-start | bytes 393224 | tf_op jit(solution)/shard_map/ppermute | solution.py:24
  104.3 13.3 %collective-permute-start.16 = (bf16[2,64,2048]{2,1,0:T(8,128)(2,1)S(1)}, bf16[2,64,2048]{2,1,0:T(8,128)(2,1)S(1)}, u32[]{:S(2)}, u32[]{:S(2)}) collective-permute-start(bf16[2,64,2048]{2,1,0:T(8,128)(2,1)S(1)} %constant_dynamic-update-slice_fusion), channel_id=1, source_target_pairs={{0,64},{32,96},{64,0},{96,32},{1,65},{33,97},{65,1},{97,33},{2,66}... | collective-permute-start | bytes 1572872 | tf_op jit(solution)/shard_map/ppermute | solution.py:30
  104.9 12.6 %collective-permute-start.15 = (bf16[2,64,2048]{2,1,0:T(8,128)(2,1)S(1)}, bf16[2,64,2048]{2,1,0:T(8,128)(2,1)S(1)}, u32[]{:S(2)}, u32[]{:S(2)}) collective-permute-start(bf16[2,64,2048]{2,1,0:T(8,128)(2,1)S(1)} %constant_dynamic-update-slice_fusion), channel_id=1, source_target_pairs={{0,32},{32,0},{64,96},{96,64},{1,33},{33,1},{65,97},{97,65},{2,34}... | collective-permute-start | bytes 1572872 | tf_op jit(solution)/shard_map/ppermute | solution.py:27
  117.6 1.9 %collective-permute-start.17 = (bf16[2,64,2048]{2,1,0:T(8,128)(2,1)S(1)}, bf16[2,64,2048]{2,1,0:T(8,128)(2,1)S(1)}, u32[]{:S(2)}, u32[]{:S(2)}) collective-permute-start(bf16[2,64,2048]{2,1,0:T(8,128)(2,1)S(1)} %collective-permute-done.16), channel_id=1, source_target_pairs={{0,32},{32,0},{64,96},{96,64},{1,33},{33,1},{65,97},{97,65},{2,34}... | collective-permute-start | bytes 1572872 | tf_op jit(solution)/shard_map/ppermute | solution.py:27
  117.6 18.5 %slice-start = ((s8[16777216]{0:T(1024)(128)(4,1)}), s8[4194304]{0:T(1024)(128)(4,1)S(1)}, s32[]{:S(2)}) async-start(s8[16777216]{0:T(1024)(128)(4,1)} %bitcast.56), calls=%async_computation | async-start | bytes 8388608
  119.5 16.6 %slice-start.1 = ((s8[16777216]{0:T(1024)(128)(4,1)}), s8[4194304]{0:T(1024)(128)(4,1)S(1)}, s32[]{:S(2)}) async-start(s8[16777216]{0:T(1024)(128)(4,1)} %bitcast.56), calls=%async_computation.1 | async-start | bytes 8388608
  122.6 13.5 %slice-start.2 = ((s8[16777216]{0:T(1024)(128)(4,1)}), s8[4194304]{0:T(1024)(128)(4,1)S(1)}, s32[]{:S(2)}) async-start(s8[16777216]{0:T(1024)(128)(4,1)} %bitcast.56), calls=%async_computation.2 | async-start | bytes 8388608
  125.6 10.5 %slice-start.3 = ((s8[16777216]{0:T(1024)(128)(4,1)}), s8[4194304]{0:T(1024)(128)(4,1)S(1)}, s32[]{:S(2)}) async-start(s8[16777216]{0:T(1024)(128)(4,1)} %bitcast.56), calls=%async_computation.3 | async-start | bytes 8388608
  128.7 16.0 %collective-permute-start.20 = (bf16[512,512]{1,0:T(8,128)(2,1)S(1)}, bf16[512,512]{1,0:T(8,128)(2,1)S(1)}, u32[]{:S(2)}, u32[]{:S(2)}) collective-permute-start(bf16[512,512]{1,0:T(8,128)(2,1)S(1)} %fusion.68), channel_id=1, source_target_pairs={{0,4},{4,8},{8,12},{12,0},{16,20},{20,24},{24,28},{28,16},{1,5},{5... | collective-permute-start | bytes 1572872 | tf_op jit(solution)/shard_map/ppermute | solution.py:21
  130.5 14.8 %collective-permute-start.21 = (bf16[512,512]{1,0:T(8,128)(2,1)S(1)}, bf16[512,512]{1,0:T(8,128)(2,1)S(1)}, u32[]{:S(2)}, u32[]{:S(2)}) collective-permute-start(bf16[512,512]{1,0:T(8,128)(2,1)S(1)} %fusion.65), channel_id=1, source_target_pairs={{0,12},{4,0},{8,4},{12,8},{16,28},{20,16},{24,20},{28,24},{1,13},{... | collective-permute-start | bytes 1572872 | tf_op jit(solution)/shard_map/ppermute | solution.py:21
  134.9 16.0 %collective-permute-start.23 = (bf16[512,512]{1,0:T(8,128)(2,1)S(1)}, bf16[512,512]{1,0:T(8,128)(2,1)S(1)}, u32[]{:S(2)}, u32[]{:S(2)}) collective-permute-start(bf16[512,512]{1,0:T(8,128)(2,1)S(1)} %fusion.71), channel_id=1, source_target_pairs={{0,16},{4,20},{8,24},{12,28},{16,0},{20,4},{24,8},{28,12},{1,17},{... | collective-permute-start | bytes 1572872 | tf_op jit(solution)/shard_map/ppermute | solution.py:18
  137.4 18.0 %collective-permute-start.18 = (bf16[512,512]{1,0:T(8,128)(2,1)S(1)}, bf16[512,512]{1,0:T(8,128)(2,1)S(1)}, u32[]{:S(2)}, u32[]{:S(2)}) collective-permute-start(bf16[512,512]{1,0:T(8,128)(2,1)S(1)} %fusion.62), channel_id=1, source_target_pairs={{0,4},{4,8},{8,12},{12,0},{16,20},{20,24},{24,28},{28,16},{1,5},{5... | collective-permute-start | bytes 1572872 | tf_op jit(solution)/shard_map/ppermute | solution.py:21
  137.9 18.7 %collective-permute-start.19 = (bf16[512,512]{1,0:T(8,128)(2,1)S(1)}, bf16[512,512]{1,0:T(8,128)(2,1)S(1)}, u32[]{:S(2)}, u32[]{:S(2)}) collective-permute-start(bf16[512,512]{1,0:T(8,128)(2,1)S(1)} %fusion.59), channel_id=1, source_target_pairs={{0,12},{4,0},{8,4},{12,8},{16,28},{20,16},{24,20},{28,24},{1,13},{... | collective-permute-start | bytes 1572872 | tf_op jit(solution)/shard_map/ppermute | solution.py:21
  146.6 14.5 %collective-permute-start.22 = (bf16[512,512]{1,0:T(8,128)(2,1)S(1)}, bf16[512,512]{1,0:T(8,128)(2,1)S(1)}, u32[]{:S(2)}, u32[]{:S(2)}) collective-permute-start(bf16[512,512]{1,0:T(8,128)(2,1)S(1)} %fusion.56), channel_id=1, source_target_pairs={{0,16},{4,20},{8,24},{12,28},{16,0},{20,4},{24,8},{28,12},{1,17},{... | collective-permute-start | bytes 1572872 | tf_op jit(solution)/shard_map/ppermute | solution.py:18
  152.2 14.4 %collective-permute-start.24 = (bf16[512,512]{1,0:T(8,128)(2,1)S(1)}, bf16[512,512]{1,0:T(8,128)(2,1)S(1)}, u32[]{:S(2)}, u32[]{:S(2)}) collective-permute-start(bf16[512,512]{1,0:T(8,128)(2,1)S(1)} %fusion.74), channel_id=1, source_target_pairs={{0,8},{4,12},{8,0},{12,4},{16,24},{20,28},{24,16},{28,20},{1,9},{5... | collective-permute-start | bytes 1572872 | tf_op jit(solution)/shard_map/ppermute | solution.py:21

commit v2 on v0

v2 whole, which is shorter than its diff:
```python
import functools
import jax
import jax.numpy as jnp
from jax import lax
from jax.experimental import pallas as pl
from jax.experimental.pallas import tpu as pltpu
from jax.sharding import PartitionSpec as P

F32, BF16 = jnp.float32, jnp.bfloat16
COST = pl.CostEstimate(flops=1 << 10, transcendentals=0, bytes_accessed=1 << 10)
PARAMS = pltpu.CompilerParams(vmem_limit_bytes=4 << 20)
VMEM = pl.BlockSpec(memory_space=pltpu.VMEM)
SMEM = pl.BlockSpec(memory_space=pltpu.SMEM)


OWN, UP, DOWN, FAR, X_OWN, X_UP, X_DOWN, X_FAR = range(8)


def after(a, *others):
    return lax.optimization_barrier((a, *others))[0]


def rows_at(at_ref, i, ns):
    return pl.ds(pl.multiple_of(at_ref[i] * ns, ns), ns)


def project_kernel(which, final, has_total, at_ref, *refs):
    n = len(which)
    blocks, table, rest = refs[:n], refs[n], refs[n + 1 :]
    m, ns = blocks[0].shape
    width = table.shape[1]
    tile = width // 4
    for j in range(4):
        if final:
            from_lane = pl.multiple_of(((at_ref[8] + j) & 3) * tile, tile)
        else:
            from_lane = j * tile
        lanes = pl.ds(from_lane, tile)
        total = rest[0][:, lanes] if has_total else None
        for i, a in zip(which, blocks):
            term = jnp.dot(a[...], table[rows_at(at_ref, i, ns), lanes], preferred_element_type=F32)
            total = term if total is None else total + term
        to = slice(j * tile, (j + 1) * tile)
        if final:
            rest[-2][:, to] = total[: m // 2].astype(BF16)
            rest[-1][:, to] = total[m // 2 :]
        else:
            rest[-1][:, to] = total


def project(blocks, which, at, table, total=None, final=False):
    m, width = blocks[0].shape[0], table.shape[1]
    args = [at, *blocks, table] + ([] if total is None else [total])
    if final:
        out_shape = [
            jax.ShapeDtypeStruct((m // 2, width), BF16),
            jax.ShapeDtypeStruct((m // 2, width), F32),
        ]
    else:
        out_shape = jax.ShapeDtypeStruct((m, width), F32)
    return pl.pallas_call(
        functools.partial(project_kernel, which, final, total is not None),
        in_specs=[SMEM] + [VMEM] * (len(args) - 1),
        out_specs=[VMEM, VMEM] if final else VMEM,
        out_shape=out_shape,
        input_output_aliases={} if final or total is None else {len(args) - 1: 0},
        cost_estimate=COST,
        compiler_params=PARAMS,
        name="project",
    )(*args)


def first_kernel(at_ref, a_ref, basis_ref, table, total, sems):
    tile = table.shape[1] // 4
    copies = []
    for j in range(4):
        lanes = slice(j * tile, (j + 1) * tile)
        copies.append(pltpu.make_async_copy(basis_ref.at[:, lanes], table.at[:, lanes], sems.at[j]))
        copies[-1].start()
    for j in range(4):
        lanes = slice(j * tile, (j + 1) * tile)
        copies[j].wait()
        rows = rows_at(at_ref, OWN, a_ref.shape[1])
        total[:, lanes] = jnp.dot(a_ref[...], table[rows, lanes], preferred_element_type=F32)


def project_first(a, at, basis):
    return pl.pallas_call(
        first_kernel,
        in_specs=[SMEM, VMEM, pl.BlockSpec(memory_space=pl.ANY)],
        out_specs=[VMEM, VMEM],
        out_shape=[
            pltpu.VMEM(basis.shape, basis.dtype),
            jax.ShapeDtypeStruct((a.shape[0], basis.shape[1]), F32),
        ],
        scratch_shapes=[pltpu.SemaphoreType.DMA((4,))],
        cost_estimate=COST,
        compiler_params=PARAMS,
        name="project_first",
    )(at, a, basis)


def load_kernel(go_ref, basis_ref, table, done, sem):
    copy = pltpu.make_async_copy(basis_ref, table, sem)
    copy.start()
    done[...] = go_ref[0, :8, :128]
    copy.wait()


def load(basis, go):
    return pl.pallas_call(
        load_kernel,
        in_specs=[VMEM, pl.BlockSpec(memory_space=pl.ANY)],
        out_specs=[VMEM, VMEM],
        out_shape=[
            pltpu.VMEM(basis.shape, basis.dtype),
            jax.ShapeDtypeStruct((8, 128), go.dtype),
        ],
        scratch_shapes=[pltpu.SemaphoreType.DMA(())],
        cost_estimate=COST,
        compiler_params=PARAMS,
        name="load",
    )(go, basis)


def expand_kernel(which, ns, n, adds, at_ref, *refs):
    fields, table, refs = refs[:n], refs[n], refs[n + 1 :]
    m = fields[0].shape[0]
    for i, out in zip(which, refs[n * adds :]):
        for h, a in enumerate(fields):
            value = lax.dot_general(
                a[...],
                table[rows_at(at_ref, i, ns), :],
                (((1,), (1,)), ((), ())),
                preferred_element_type=F32,
            )
            for add in refs[h * adds : (h + 1) * adds]:
                value = value + add[...].astype(F32)
            out[h * m : (h + 1) * m, :] = value.astype(out.dtype)


def expand(fields, which, at, table, ns, adds=(), dtype=BF16):
    rows = sum(a.shape[0] for a in fields)
    flat = [a for group in adds for a in group]
    out = pl.pallas_call(
        functools.partial(expand_kernel, which, ns, len(fields), len(flat) // len(fields)),
        in_specs=[SMEM] + [VMEM] * (len(fields) + 1 + len(flat)),
        out_specs=[VMEM] * len(which),
        out_shape=[jax.ShapeDtypeStruct((rows, ns), dtype)] * len(which),
        cost_estimate=COST,
        compiler_params=PARAMS,
        name="expand",
    )(at, *fields, table, *flat)
    return out if len(which) > 1 else out[0]


def filter_kernel(at_ref, noise, space, time, turn, *refs):
    ins, outs, held = refs[:4], refs[4:8], refs[8]
    pair, nt, width = ins[0].shape
    z = at_ref[8]
    for k in range(4):
        rows = pl.ds(pl.multiple_of(((z - k) & 3) * nt, nt), nt)
        for r in range(pair):
            held[rows, r * width : (r + 1) * width] = ins[k][r]
    mixed = lax.dot_general(
        turn[...], held[...], (((0,), (0,)), ((), ())), preferred_element_type=F32
    )
    value = space[:, pl.ds(pl.multiple_of(z * width, width), width)]
    denom = value * time[...] + noise[0]
    scaled = mixed / jnp.concatenate([denom] * pair, axis=1)
    held[...] = jnp.dot(
        turn[...], scaled.astype(BF16), preferred_element_type=F32
    ).astype(BF16)
    for k in range(4):
        rows = pl.ds(pl.multiple_of(((z - k) & 3) * nt, nt), nt)
        for r in range(pair):
            outs[k][r] = held[rows, r * width : (r + 1) * width]


def time_filter(parts, at, noise, space, time, turn):
    pair, nt, width = parts[0].shape
    return pl.pallas_call(
        filter_kernel,
        in_specs=[SMEM, SMEM] + [VMEM] * 7,
        out_specs=[VMEM] * 4,
        out_shape=[jax.ShapeDtypeStruct((pair, nt, width), BF16)] * 4,
        scratch_shapes=[pltpu.VMEM((4 * nt, pair * width), BF16)],
        cost_estimate=COST,
        compiler_params=PARAMS,
        name="time_filter",
    )(at, noise, space[None, :], time[:, None], turn, *parts)


def finish_kernel(rows, at_ref, total, *refs):
    g, out = at_ref[9], refs[-1]
    value = total[...]
    for a in refs[:-1]:
        value = value + a[...].astype(F32)
    for k in range(4):
        to = pl.ds(pl.multiple_of((g ^ k) * rows, rows), rows)
        out[to, :] = value[k * rows : (k + 1) * rows]


def finish(total, at, adds):
    return pl.pallas_call(
        functools.partial(finish_kernel, total.shape[0] // 4),
        in_specs=[SMEM] + [VMEM] * (1 + len(adds)),
        out_specs=VMEM,
        out_shape=jax.ShapeDtypeStruct(total.shape, F32),
        cost_estimate=COST,
        compiler_params=PARAMS,
        name="finish",
    )(at, total, *adds)


def shards(right_sides, eigen_basis, space_values, time_basis, time_values, noise_level):
    rhs, nt, ns = right_sides.shape
    rows = rhs * nt
    basis = space_values.shape[0]
    row, col, tm = lax.axis_index("row"), lax.axis_index("col"), lax.axis_index("tm")
    core, x_hi, y = row & 1, col & 4, col & 3
    quarter = basis // 4
    pair = rhs // 4
    eigen_basis = pltpu.with_memory_space_constraint(eigen_basis, pltpu.HBM)

    def across_x(a):
        with jax.named_scope("across_x"):
            return lax.ppermute(a, "col", [(c, c ^ 4) for c in range(8)])

    def along_y(a, k):
        with jax.named_scope("along_y%d" % (k & 3)):
            return lax.ppermute(a, "col", [(c, (c & 4) | ((c + k) & 3)) for c in range(8)])

    def along_z(a, k):
        with jax.named_scope("along_z%d" % (k & 3)):
            return lax.ppermute(a, "tm", [(z, (z + k) & 3) for z in range(4)])

    def other_core(a):
        with jax.named_scope("other_core"):
            return lax.ppermute(a, "row", [(r, r ^ 1) for r in range(4)])

    def other_x(a):
        with jax.named_scope("other_x"):
            return lax.ppermute(a, "row", [(r, r ^ 2) for r in range(4)])

    steps = jnp.array([0, 1, -1, 2] * 2, jnp.int32)
    flips = jnp.array([0] * 4 + [4] * 4, jnp.int32)
    at = jnp.concatenate([(x_hi ^ flips) + ((y + steps) & 3), tm[None], row[None]])

    def group(g):
        return lax.dynamic_slice_in_dim(right_sides, g * pair, pair, 0)

    own = jnp.concatenate([group(row ^ 3), group(row ^ 1), group(row ^ 2), group(row)], 0)
    own = own.reshape(rows, ns)
    down, up = along_y(own, 1), along_y(own, -1)
    x_own = across_x(own)
    table, total = project_first(own, at, eigen_basis)
    far = jnp.concatenate(
        [along_y(down[: rows // 2], 1), along_y(up[rows // 2 :], -1)], axis=0
    )
    x_own = after(x_own, total)
    x_down, x_up = along_y(x_own, 1), along_y(x_own, -1)
    x_far = across_x(far)
    total = project([up, down], [UP, DOWN], at, table, total)
    total = project([x_own, far], [X_OWN, FAR], at, table, total)
    total = project([x_up, x_down], [X_UP, X_DOWN], at, table, total)
    give, keep = project([x_far], [X_FAR], at, table, total, final=True)

    both = keep + other_core(give).astype(F32)
    half = pair * nt

    def part(a, k):
        return a[:, k * quarter : (k + 1) * quarter]

    to_x = both[:half].astype(BF16)
    from_x = {k: other_x(part(to_x, k)) for k in (2, 1, 3, 0)}
    times = []
    spectral = to_x
    for k in (2, 1, 3, 0):
        got = after(from_x[k], spectral)
        spectral = (part(both[half:], k) + got.astype(F32)).astype(BF16)
        spectral = spectral.reshape(pair, nt, quarter)
        times.append(along_z(spectral, k) if k else spectral)
    two, one, three, zero = times

    back = time_filter(
        [zero, one, two, three], at, noise_level, space_values, time_values, time_basis
    )
    table, loaded = load(eigen_basis, back[0])
    pieces = [back[0]] + [after(along_z(back[k], -k), loaded) for k in (1, 2, 3)]

    def assembled(parts):
        whole = jnp.zeros((pair, nt, basis), BF16)
        for k in (0, 1, 3, 2):
            whole = lax.dynamic_update_slice_in_dim(whole, parts[k], ((tm + k) & 3) * quarter, 2)
        return whole.reshape(half, basis)

    from_x = {k: other_x(pieces[k]) for k in (0, 1, 3, 2)}
    mine = assembled(pieces)
    near = jnp.concatenate([mine, other_core(mine)], 0)

    def first_step(a):
        s_up, s_down = expand([a], [X_UP, X_DOWN], at, table, ns)
        s_far = expand([a], [X_FAR], at, table, ns)
        return (along_y(s_up, 1), along_y(s_down, -1), across_x(s_far)), s_up

    steps_near, sent = first_step(near)
    from_x = assembled({k: after(a, sent) for k, a in from_x.items()})
    away = jnp.concatenate([from_x, other_core(from_x)], 0)
    steps_away, _ = first_step(away)
    fields = [after(near, *steps_near[:2]), away]
    o_up, o_down = expand(fields, [UP, DOWN], at, table, ns)
    o_up, o_down = along_y(o_up, 1), along_y(o_down, -1)
    o_x = expand(fields, [X_OWN], at, table, ns, (steps_near[:2], steps_away[:2]))
    o_x = across_x(o_x)
    o_far = expand(fields, [FAR], at, table, ns, (steps_near[2:], steps_away[2:]))
    o_far = along_y(o_far, 2)
    out = expand(fields, [OWN], at, table, ns, (), F32)
    return finish(out, at, (o_up, o_down, o_x, o_far)).reshape(rhs, nt, ns)


def solution(mesh):
    placed = (P(None, "tm", ("row", "col")), P("row", "col"), P("col"), P(), P(), P())
    return jax.shard_map(
        shards, mesh=mesh, in_specs=placed, out_specs=P(None, "tm", ("row", "col")), check_vma=False
    )
```

time: 405 us -> 140 us (0.35)
  waiting for transfers between devices: 216 us -> 38.8 us
  blocking collectives: 105 us -> 0 us
  starting transfers between devices: 4.42 us -> 55.4 us
  Pallas kernels: 0 us -> 42.1 us
  matrix products: 35.1 us -> 0 us
  local copies, waits for them, and re-layouts: 29.8 us -> 1.66 us
  between operations: 14.1 us -> 1.12 us
    reduce_scatter x1 -> x0, waiting for transfers between devices: 111 us -> none  [shards(): return lax.psum_scatter(terms, 'col', scatter_dimension=2, tiled=True)]
    all_gather x1 -> x0, waiting for transfers between devices: 78.3 us -> none  [shards(): lax.all_gather(right_sides, 'col', axis=2, tiled=True)]
    psum x1 -> x0, blocking collectives: 76.4 us -> none  [shards(): spectral = lax.psum(partial_value, 'row').astype(jnp.bfloat16)]
    ppermute x0 -> x35, starting transfers between devices: none -> 55.4 us  [the longest x13 18.8 us: along_y(): return lax.ppermute(a, 'col', [(c, c & 4 | c + k & 3) for c in range(8)])]
    pallas_call x0 -> x16, Pallas kernels: none -> 42.1 us  [the longest x8 14.6 us: expand(): pl.pallas_call(functools.partial(expand_kernel, which, ns, len(fields), l...]
    ppermute x0 -> x35, waiting for transfers between devices: none -> 38.8 us  [the longest x13 23.8 us: along_y(): return lax.ppermute(a, 'col', [(c, c & 4 | c + k & 3) for c in range(8)])]
    dot_general x3 -> x0, matrix products: 35.1 us -> none  [the longest x1 15.1 us: shards(): jnp.einsum('rti,si->rts', own_part, eigen_basis, preferred_element_type=j...]
    all_to_all x1 -> x0, blocking collectives: 28.5 us -> none  [shards(): lax.all_to_all(jnp.einsum('tj,kji->kti', time_basis, scaled, preferred_el...]
  transfers between devices with their start and end apart: 3 -> 35, of which waited for: 3 -> 11; matrix products, arithmetic and copies ran while one was open for 0% -> 0% of each run, Pallas kernels for 0% -> 27%
where the time goes in v2:
time: 140 us
  starting transfers between devices  55.4 us (40%)
  Pallas kernels  42.1 us (30%)
  waiting for transfers between devices  38.8 us (28%)
  local copies, waits for them, and re-layouts  1.66 us (1%)
    ppermute x13, waiting for transfers between devices, along_y(): return lax.ppermute(a, 'col', [(c, c & 4 | c + k & 3) for c in range(8)])  23.8 us
    ppermute x13, starting transfers between devices, along_y(): return lax.ppermute(a, 'col', [(c, c & 4 | c + k & 3) for c in range(8)])  18.8 us
    ppermute x6, starting transfers between devices, along_z(): return lax.ppermute(a, 'tm', [(z, z + k & 3) for z in range(4)])  14.9 us
    pallas_call x8, Pallas kernels, expand(): pl.pallas_call(functools.partial(expand_kernel, which, ns, len(fields), l...  14.6 us
    ppermute x5, starting transfers between devices, across_x(): return lax.ppermute(a, 'col', [(c, c ^ 4) for c in range(8)])  13.1 us
    pallas_call x4, Pallas kernels, project(): pl.pallas_call(functools.partial(project_kernel, which, final, total is n...  11.3 us
    ppermute x8, waiting for transfers between devices, other_x(): return lax.ppermute(a, 'row', [(r, r ^ 2) for r in range(4)])  9.88 us
    ppermute x8, starting transfers between devices, other_x(): return lax.ppermute(a, 'row', [(r, r ^ 2) for r in range(4)])  8.34 us
  transfers between devices with their start and end apart: 35, of which 11 were waited for; matrix products, arithmetic and copies ran while one was open for 0% of the time, Pallas kernels for 27%

profile of v2, /device:TPU:0, one launch (start us, length us, event | category | flops | bytes accessed | tf_op | source)
XLA Modules:
  0.0 140.0 jit_solution(15846519759587374326)
XLA Ops:
  0.0 1.2 constant_dynamic-slice_fusion.3
  1.2 1.7 %collective-permute-start = (bf16[512,512]{1,0:T(8,128)(2,1)S(1)}, bf16[512,512]{1,0:T(8,128)(2,1)S(1)}, u32[]{:S(2)}, u32[]{:S(2)}) collective-permute-start(bf16[512,512]{1,0:T(8,128)(2,1)S(1)} %bitcast.12), channel_id=1, source_target_pairs={{0,4},{4,8},{8,12},{12,0},{16,20},{20,24},{24,28},{28,16},{1,5},{5... | collective-permute-start | bytes 1572872 | tf_op jit(solution)/shard_map/along_y1/ppermute | solution.py:232
  3.0 1.6 %collective-permute-start.2 = (bf16[512,512]{1,0:T(8,128)(2,1)S(1)}, bf16[512,512]{1,0:T(8,128)(2,1)S(1)}, u32[]{:S(2)}, u32[]{:S(2)}) collective-permute-start(bf16[512,512]{1,0:T(8,128)(2,1)S(1)} %bitcast.13), channel_id=1, source_target_pairs={{0,12},{4,0},{8,4},{12,8},{16,28},{20,16},{24,20},{28,24},{1,13},{... | collective-permute-start | bytes 1572872 | tf_op jit(solution)/shard_map/along_y3/ppermute | solution.py:232
  4.5 3.1 %collective-permute-start.5 = (bf16[512,512]{1,0:T(8,128)(2,1)S(1)}, bf16[512,512]{1,0:T(8,128)(2,1)S(1)}, u32[]{:S(2)}, u32[]{:S(2)}) collective-permute-start(bf16[512,512]{1,0:T(8,128)(2,1)S(1)} %bitcast.14), channel_id=1, source_target_pairs={{0,16},{4,20},{8,24},{12,28},{16,0},{20,4},{24,8},{28,12},{1,17},{... | collective-permute-start | bytes 1572872 | tf_op jit(solution)/shard_map/across_x/ppermute | solution.py:228
  7.7 8.7 %collective-permute-done.refs_1_ = bf16[512,512]{1,0:T(8,128)(2,1)S(1)} collective-permute-done((bf16[512,512]{1,0:T(8,128)(2,1)S(1)}, bf16[512,512]{1,0:T(8,128)(2,1)S(1)}, u32[]{:S(2)}, u32[]{:S(2)}) %collective-permute-start) | collective-permute-done | bytes 524320 | tf_op jit(solution)/shard_map/along_y1/ppermute | solution.py:232
  16.7 3.0 %collective-permute-start.3 = (bf16[256,512]{1,0:T(8,128)(2,1)S(1)}, bf16[256,512]{1,0:T(8,128)(2,1)S(1)}, u32[]{:S(2)}, u32[]{:S(2)}) collective-permute-start(bf16[256,512]{1,0:T(8,128)(2,1)S(1)} %slice.55), channel_id=1, source_target_pairs={{0,12},{4,0},{8,4},{12,8},{16,28},{20,16},{24,20},{28,24},{1,13},{... | collective-permute-start | bytes 786440 | tf_op jit(solution)/shard_map/along_y3/ppermute | solution.py:232
  19.8 6.9 %project_first.1 = (bf16[4096,2048]{1,0:T(8,128)(2,1)S(1)}, f32[512,2048]{1,0:T(8,128)S(1)}) custom-call(s32[10]{0:T(128)S(1)} %pad_add_fusion.at_ref, bf16[512,512]{1,0:T(8,128)(2,1)S(1)} %bitcast.15, bf16[4096,2048]{1,0:T(8,128)(2,1)} %basis_ref.3), custom_call_target="tpu_custom_call" | custom-call | flops 1024 | bytes 1024 | tf_op jit(solution)/shard_map/project_first/pallas_call | solution.py:88
  27.4 1.5 %collective-permute-start.7 = (bf16[512,512]{1,0:T(8,128)(2,1)S(1)}, bf16[512,512]{1,0:T(8,128)(2,1)S(1)}, u32[]{:S(2)}, u32[]{:S(2)}) collective-permute-start(bf16[512,512]{1,0:T(8,128)(2,1)S(1)} %collective-permute-done.5.refs_0_), channel_id=1, source_target_pairs={{0,4},{4,8},{8,12},{12,0},{16,20},{20,24},{24,28},{28,16},{1,5},{5... | collective-permute-start | bytes 1572872 | tf_op jit(solution)/shard_map/along_y1/ppermute | solution.py:232
  28.9 3.1 %collective-permute-start.4 = (bf16[512,512]{1,0:T(8,128)(2,1)S(1)}, bf16[512,512]{1,0:T(8,128)(2,1)S(1)}, u32[]{:S(2)}, u32[]{:S(2)}) collective-permute-start(bf16[512,512]{1,0:T(8,128)(2,1)S(1)} %constant_dynamic-update-slice_fusion.refs_1_), channel_id=1, source_target_pairs={{0,16},{4,20},{8,24},{12,28},{16,0},{20,4},{24,8},{28,12},{1,17},{... | collective-permute-start | bytes 1572872 | tf_op jit(solution)/shard_map/across_x/ppermute | solution.py:228
  32.0 3.2 %project.4.refs_3_ = f32[512,2048]{1,0:T(8,128)S(1)} custom-call(s32[10]{0:T(128)S(1)} %pad_add_fusion.at_ref, bf16[512,512]{1,0:T(8,128)(2,1)S(1)} %collective-permute-done.2.refs_0_, bf16[512,512]{1,0:T(8,128)(2,1)S(1)} %collective-permute-done.refs_1_, bf16[4096,2048]{1,0:T(8,128)(2,1)S(1)} %get-tuple-element.33.refs_2_.refs_1_, ...), custom_call_target="tpu_custom_call", output_to_operand_aliasing={{}: (4, {})} | custom-call | flops 1024 | bytes 1024 | tf_op jit(solution)/shard_map/project/pallas_call | solution.py:61
  35.2 3.2 %project.5.refs_3_ = f32[512,2048]{1,0:T(8,128)S(1)} custom-call(s32[10]{0:T(128)S(1)} %pad_add_fusion.at_ref, bf16[512,512]{1,0:T(8,128)(2,1)S(1)} %collective-permute-done.5.refs_0_, bf16[512,512]{1,0:T(8,128)(2,1)S(1)} %constant_dynamic-update-slice_fusion.refs_1_, ...), custom_call_target="tpu_custom_call", output_to_operand_aliasing={{}: (4, {})} | custom-call | flops 1024 | bytes 1024 | tf_op jit(solution)/shard_map/project/pallas_call | solution.py:61
  38.4 0.9 collective-permute-done.6.refs_0_
  39.3 1.3 collective-permute-done.7.refs_1_
  40.5 3.1 %project.6.refs_2_ = f32[512,2048]{1,0:T(8,128)S(1)} custom-call(s32[10]{0:T(128)S(1)} %pad_add_fusion.at_ref, bf16[512,512]{1,0:T(8,128)(2,1)S(1)} %collective-permute-done.6.refs_0_, bf16[512,512]{1,0:T(8,128)(2,1)S(1)} %collective-permute-done.7.refs_1_, bf16[4096,2048]{1,0:T(8,128)(2,1)S(1)} %get-tuple-element.33.refs_2_.refs_1_, ...), custom_call_target="tpu_custom_call", output_to_operand_aliasing={{}: (4, {})} | custom-call | flops 1024 | bytes 1024 | tf_op jit(solution)/shard_map/project/pallas_call | solution.py:61
  43.6 1.9 %project.7 = (bf16[256,2048]{1,0:T(8,128)(2,1)S(1)}, f32[256,2048]{1,0:T(8,128)S(1)}) custom-call(s32[10]{0:T(128)S(1)} %pad_add_fusion.at_ref, bf16[512,512]{1,0:T(8,128)(2,1)S(1)} %collective-permute-done.4.refs_0_, bf16[4096,2048]{1,0:T(8,128)(2,1)S(1)} %get-tuple-element.33.refs_2_.refs_1_, f32[512,2048]{1,0:T(8,128)S(1)} %project.6.refs_2_), custom_call_target="tpu_custom_call" | custom-call | flops 1024 | bytes 1024 | tf_op jit(solution)/shard_map/project/pallas_call | solution.py:61
  45.6 2.6 %collective-permute-done.8 = bf16[256,2048]{1,0:T(8,128)(2,1)S(1)} collective-permute-done((bf16[256,2048]{1,0:T(8,128)(2,1)S(1)}, bf16[256,2048]{1,0:T(8,128)(2,1)S(1)}, u32[]{:S(2)}, u32[]{:S(2)}) %collective-permute-start.8) | collective-permute-done | bytes 1048608 | tf_op jit(solution)/shard_map/other_core/ppermute | solution.py:240
  48.7 1.6 %collective-permute-start.12 = (bf16[128,512]{1,0:T(8,128)(2,1)S(1)}, bf16[128,512]{1,0:T(8,128)(2,1)S(1)}, u32[]{:S(2)}, u32[]{:S(2)}) collective-permute-start(bf16[128,512]{1,0:T(8,128)(2,1)S(1)} %get-tuple-element.63), channel_id=1, source_target_pairs={{0,64},{32,96},{64,0},{96,32},{1,65},{33,97},{65,1},{97,33},{2,66}... | collective-permute-start | bytes 393224 | tf_op jit(solution)/shard_map/other_x/ppermute | solution.py:244
  51.7 1.5 %collective-permute-start.10 = (bf16[128,512]{1,0:T(8,128)(2,1)S(1)}, bf16[128,512]{1,0:T(8,128)(2,1)S(1)}, u32[]{:S(2)}, u32[]{:S(2)}) collective-permute-start(bf16[128,512]{1,0:T(8,128)(2,1)S(1)} %get-tuple-element.65), channel_id=1, source_target_pairs={{0,64},{32,96},{64,0},{96,32},{1,65},{33,97},{65,1},{97,33},{2,66}... | collective-permute-start | bytes 393224 | tf_op jit(solution)/shard_map/other_x/ppermute | solution.py:244
  53.7 1.3 collective-permute-done.12
  55.0 4.0 %collective-permute-start.14 = (bf16[2,64,512]{2,1,0:T(8,128)(2,1)S(1)}, bf16[2,64,512]{2,1,0:T(8,128)(2,1)S(1)}, u32[]{:S(2)}, u32[]{:S(2)}) collective-permute-start(bf16[2,64,512]{2,1,0:T(8,128)(2,1)S(1)} %bitcast.22), channel_id=1, source_target_pairs={{0,2},{1,3},{2,0},{3,1},{4,6},{5,7},{6,4},{7,5},{8,10},{9,11},{10,... | collective-permute-start | bytes 393224 | tf_op jit(solution)/shard_map/along_z2/ppermute | solution.py:236
  59.0 1.3 collective-permute-start.13
  60.7 4.1 %collective-permute-start.15 = (bf16[2,64,512]{2,1,0:T(8,128)(2,1)S(1)}, bf16[2,64,512]{2,1,0:T(8,128)(2,1)S(1)}, u32[]{:S(2)}, u32[]{:S(2)}) collective-permute-start(bf16[2,64,512]{2,1,0:T(8,128)(2,1)S(1)} %bitcast.24), channel_id=1, source_target_pairs={{0,3},{1,0},{2,1},{3,2},{4,7},{5,4},{6,5},{7,6},{8,11},{9,8},{10,9... | collective-permute-start | bytes 393224 | tf_op jit(solution)/shard_map/along_z3/ppermute | solution.py:236
  64.8 2.5 %collective-permute-done.15.refs_3_ = bf16[2,64,512]{2,1,0:T(8,128)(2,1)S(1)} collective-permute-done((bf16[2,64,512]{2,1,0:T(8,128)(2,1)S(1)}, bf16[2,64,512]{2,1,0:T(8,128)(2,1)S(1)}, u32[]{:S(2)}, u32[]{:S(2)}) %collective-permute-start.15) | collective-permute-done | bytes 131104 | tf_op jit(solution)/shard_map/along_z3/ppermute | solution.py:236
  67.3 1.2 time_filter.1
  68.5 2.4 %collective-permute-start.18 = (bf16[2,64,512]{2,1,0:T(8,128)(2,1)S(1)}, bf16[2,64,512]{2,1,0:T(8,128)(2,1)S(1)}, u32[]{:S(2)}, u32[]{:S(2)}) collective-permute-start(bf16[2,64,512]{2,1,0:T(8,128)(2,1)S(1)} %get-tuple-element.47), channel_id=1, source_target_pairs={{0,2},{1,3},{2,0},{3,1},{4,6},{5,7},{6,4},{7,5},{8,10},{9,11},{10,... | collective-permute-start | bytes 393224 | tf_op jit(solution)/shard_map/along_z2/ppermute | solution.py:236
  70.8 2.2 %collective-permute-start.17 = (bf16[2,64,512]{2,1,0:T(8,128)(2,1)S(1)}, bf16[2,64,512]{2,1,0:T(8,128)(2,1)S(1)}, u32[]{:S(2)}, u32[]{:S(2)}) collective-permute-start(bf16[2,64,512]{2,1,0:T(8,128)(2,1)S(1)} %get-tuple-element.45), channel_id=1, source_target_pairs={{0,1},{1,2},{2,3},{3,0},{4,5},{5,6},{6,7},{7,4},{8,9},{9,10},{10,1... | collective-permute-start | bytes 393224 | tf_op jit(solution)/shard_map/along_z1/ppermute | solution.py:236
  73.1 1.0 collective-permute-start.16
  74.1 6.4 %load.1 = (bf16[4096,2048]{1,0:T(8,128)(2,1)S(1)}, bf16[8,128]{1,0:T(8,128)(2,1)}) custom-call(bf16[2,64,512]{2,1,0:T(8,128)(2,1)S(1)} %get-tuple-element.41.go_ref, bf16[4096,2048]{1,0:T(8,128)(2,1)} %basis_ref.3), custom_call_target="tpu_custom_call" | custom-call | flops 1024 | bytes 1024 | tf_op jit(solution)/shard_map/load/pallas_call | solution.py:111
  80.7 1.7 %collective-permute-start.22 = (bf16[2,64,512]{2,1,0:T(8,128)(2,1)S(1)}, bf16[2,64,512]{2,1,0:T(8,128)(2,1)S(1)}, u32[]{:S(2)}, u32[]{:S(2)}) collective-permute-start(bf16[2,64,512]{2,1,0:T(8,128)(2,1)S(1)} %get-tuple-element.41.go_ref), channel_id=1, source_target_pairs={{0,64},{32,96},{64,0},{96,32},{1,65},{33,97},{65,1},{97,33},{2,66}... | collective-permute-start | bytes 393224 | tf_op jit(solution)/shard_map/other_x/ppermute | solution.py:244
  82.8 1.6 %collective-permute-start.24 = (bf16[2,64,512]{2,1,0:T(8,128)(2,1)S(1)}, bf16[2,64,512]{2,1,0:T(8,128)(2,1)S(1)}, u32[]{:S(2)}, u32[]{:S(2)}) collective-permute-start(bf16[2,64,512]{2,1,0:T(8,128)(2,1)S(1)} %collective-permute-done.17), channel_id=1, source_target_pairs={{0,64},{32,96},{64,0},{96,32},{1,65},{33,97},{65,1},{97,33},{2,66}... | collective-permute-start | bytes 393224 | tf_op jit(solution)/shard_map/other_x/ppermute | solution.py:244
  85.0 1.8 %expand.8 = (bf16[256,512]{1,0:T(8,128)(2,1)S(1)}, bf16[256,512]{1,0:T(8,128)(2,1)S(1)}) custom-call(s32[10]{0:T(128)S(1)} %pad_add_fusion.at_ref, bf16[256,2048]{1,0:T(8,128)(2,1)S(1)} %pad_maximum_fusion.refs_0_, bf16[4096,2048]{1,0:T(8,128)(2,1)S(1)} %get-tuple-element.49.refs_1_.refs_2_), custom_call_target="tpu_custom_call" | custom-call | flops 1024 | bytes 1024 | tf_op jit(solution)/shard_map/expand/pallas_call | solution.py:145
  86.8 3.1 %collective-permute-done.25 = bf16[2,64,512]{2,1,0:T(8,128)(2,1)S(1)} collective-permute-done((bf16[2,64,512]{2,1,0:T(8,128)(2,1)S(1)}, bf16[2,64,512]{2,1,0:T(8,128)(2,1)S(1)}, u32[]{:S(2)}, u32[]{:S(2)}) %collective-permute-start.25) | collective-permute-done | bytes 131104 | tf_op jit(solution)/shard_map/other_x/ppermute | solution.py:244
  89.9 2.8 %collective-permute-done.24 = bf16[2,64,512]{2,1,0:T(8,128)(2,1)S(1)} collective-permute-done((bf16[2,64,512]{2,1,0:T(8,128)(2,1)S(1)}, bf16[2,64,512]{2,1,0:T(8,128)(2,1)S(1)}, u32[]{:S(2)}, u32[]{:S(2)}) %collective-permute-start.24) | collective-permute-done | bytes 131104 | tf_op jit(solution)/shard_map/other_x/ppermute | solution.py:244
  92.7 2.3 %collective-permute-done.23 = bf16[2,64,512]{2,1,0:T(8,128)(2,1)S(1)} collective-permute-done((bf16[2,64,512]{2,1,0:T(8,128)(2,1)S(1)}, bf16[2,64,512]{2,1,0:T(8,128)(2,1)S(1)}, u32[]{:S(2)}, u32[]{:S(2)}) %collective-permute-start.23) | collective-permute-done | bytes 131104 | tf_op jit(solution)/shard_map/other_x/ppermute | solution.py:244
  95.7 1.3 expand.13
  97.0 2.9 %collective-permute-start.21 = (bf16[256,512]{1,0:T(8,128)(2,1)S(1)}, bf16[256,512]{1,0:T(8,128)(2,1)S(1)}, u32[]{:S(2)}, u32[]{:S(2)}) collective-permute-start(bf16[256,512]{1,0:T(8,128)(2,1)S(1)} %get-tuple-element.51), channel_id=1, source_target_pairs={{0,12},{4,0},{8,4},{12,8},{16,28},{20,16},{24,20},{28,24},{1,13},{... | collective-permute-start | bytes 786440 | tf_op jit(solution)/shard_map/along_y3/ppermute | solution.py:232
  100.1 3.2 %collective-permute-start.32 = (bf16[256,512]{1,0:T(8,128)(2,1)S(1)}, bf16[256,512]{1,0:T(8,128)(2,1)S(1)}, u32[]{:S(2)}, u32[]{:S(2)}) collective-permute-start(bf16[256,512]{1,0:T(8,128)(2,1)S(1)} %expand.13), channel_id=1, source_target_pairs={{0,16},{4,20},{8,24},{12,28},{16,0},{20,4},{24,8},{28,12},{1,17},{... | collective-permute-start | bytes 786440 | tf_op jit(solution)/shard_map/across_x/ppermute | solution.py:228
  103.3 1.3 expand.14
  104.6 1.8 %expand.11 = (bf16[256,512]{1,0:T(8,128)(2,1)S(1)}, bf16[256,512]{1,0:T(8,128)(2,1)S(1)}) custom-call(s32[10]{0:T(128)S(1)} %pad_add_fusion.at_ref, bf16[256,2048]{1,0:T(8,128)(2,1)S(1)} %pad_maximum_fusion.1.refs_1_.refs_0_, bf16[4096,2048]{1,0:T(8,128)(2,1)S(1)} %get-tuple-element.49.refs_1_.refs_2_), custom_call_target="tpu_custom_call" | custom-call | flops 1024 | bytes 1024 | tf_op jit(solution)/shard_map/expand/pallas_call | solution.py:145
  106.9 3.2 %collective-permute-start.30 = (bf16[256,512]{1,0:T(8,128)(2,1)S(1)}, bf16[256,512]{1,0:T(8,128)(2,1)S(1)}, u32[]{:S(2)}, u32[]{:S(2)}) collective-permute-start(bf16[256,512]{1,0:T(8,128)(2,1)S(1)} %get-tuple-element.60), channel_id=1, source_target_pairs={{0,12},{4,0},{8,4},{12,8},{16,28},{20,16},{24,20},{28,24},{1,13},{... | collective-permute-start | bytes 786440 | tf_op jit(solution)/shard_map/along_y3/ppermute | solution.py:232
  110.1 2.9 %expand.10 = (bf16[512,512]{1,0:T(8,128)(2,1)S(1)}, bf16[512,512]{1,0:T(8,128)(2,1)S(1)}) custom-call(s32[10]{0:T(128)S(1)} %pad_add_fusion.at_ref, bf16[256,2048]{1,0:T(8,128)(2,1)S(1)} %pad_maximum_fusion.refs_0_, bf16[256,2048]{1,0:T(8,128)(2,1)S(1)} %pad_maximum_fusion.1.refs_1_.refs_0_, bf16[4096,2048]{1,0:T(8,128)(2,1)S(1)} %get-tuple-element.49.refs_1_.refs_2_), custom_call_target="tpu_custom_call" | custom-call | flops 1024 | bytes 1024 | tf_op jit(solution)/shard_map/expand/pallas_call | solution.py:145
  113.1 3.2 %collective-permute-start.28 = (bf16[512,512]{1,0:T(8,128)(2,1)S(1)}, bf16[512,512]{1,0:T(8,128)(2,1)S(1)}, u32[]{:S(2)}, u32[]{:S(2)}) collective-permute-start(bf16[512,512]{1,0:T(8,128)(2,1)S(1)} %get-tuple-element.58), channel_id=1, source_target_pairs={{0,12},{4,0},{8,4},{12,8},{16,28},{20,16},{24,20},{28,24},{1,13},{... | collective-permute-start | bytes 1572872 | tf_op jit(solution)/shard_map/along_y3/ppermute | solution.py:232
  116.4 1.8 %expand.15 = bf16[512,512]{1,0:T(8,128)(2,1)S(1)} custom-call(s32[10]{0:T(128)S(1)} %pad_add_fusion.at_ref, bf16[256,2048]{1,0:T(8,128)(2,1)S(1)} %pad_maximum_fusion.refs_0_, bf16[256,2048]{1,0:T(8,128)(2,1)S(1)} %pad_maximum_fusion.1.refs_1_.refs_0_, bf16[4096,2048]{1,0:T(8,128)(2,1)S(1)} %get-tuple-element.49.refs_1_.refs_2_, ...), custom_call_target="tpu_custom_call" | custom-call | flops 1024 | bytes 1024 | tf_op jit(solution)/shard_map/expand/pallas_call | solution.py:145
  118.3 1.9 %expand.12 = bf16[512,512]{1,0:T(8,128)(2,1)S(1)} custom-call(s32[10]{0:T(128)S(1)} %pad_add_fusion.at_ref, bf16[256,2048]{1,0:T(8,128)(2,1)S(1)} %pad_maximum_fusion.refs_0_, bf16[256,2048]{1,0:T(8,128)(2,1)S(1)} %pad_maximum_fusion.1.refs_1_.refs_0_, bf16[4096,2048]{1,0:T(8,128)(2,1)S(1)} %get-tuple-element.49.refs_1_.refs_2_, ...), custom_call_target="tpu_custom_call" | custom-call | flops 1024 | bytes 1024 | tf_op jit(solution)/shard_map/expand/pallas_call | solution.py:145
  120.2 3.2 %collective-permute-start.31 = (bf16[512,512]{1,0:T(8,128)(2,1)S(1)}, bf16[512,512]{1,0:T(8,128)(2,1)S(1)}, u32[]{:S(2)}, u32[]{:S(2)}) collective-permute-start(bf16[512,512]{1,0:T(8,128)(2,1)S(1)} %expand.12), channel_id=1, source_target_pairs={{0,16},{4,20},{8,24},{12,28},{16,0},{20,4},{24,8},{28,12},{1,17},{... | collective-permute-start | bytes 1572872 | tf_op jit(solution)/shard_map/across_x/ppermute | solution.py:228
  123.4 1.8 %expand.9.total = f32[512,512]{1,0:T(8,128)S(1)} custom-call(s32[10]{0:T(128)S(1)} %pad_add_fusion.at_ref, bf16[256,2048]{1,0:T(8,128)(2,1)S(1)} %pad_maximum_fusion.refs_0_, bf16[256,2048]{1,0:T(8,128)(2,1)S(1)} %pad_maximum_fusion.1.refs_1_.refs_0_, bf16[4096,2048]{1,0:T(8,128)(2,1)S(1)} %get-tuple-element.49.refs_1_.refs_2_), custom_call_target="tpu_custom_call" | custom-call | flops 1024 | bytes 1024 | tf_op jit(solution)/shard_map/expand/pallas_call | solution.py:145
  125.2 12.9 %collective-permute-done.27.refs_0_ = bf16[512,512]{1,0:T(8,128)(2,1)S(1)} collective-permute-done((bf16[512,512]{1,0:T(8,128)(2,1)S(1)}, bf16[512,512]{1,0:T(8,128)(2,1)S(1)}, u32[]{:S(2)}, u32[]{:S(2)}) %collective-permute-start.27) | collective-permute-done | bytes 524320 | tf_op jit(solution)/shard_map/along_y1/ppermute | solution.py:232
  138.2 1.8 %finish.1 = f32[512,512]{1,0:T(8,128)} custom-call(s32[10]{0:T(128)S(1)} %pad_add_fusion.at_ref, f32[512,512]{1,0:T(8,128)S(1)} %expand.9.total, bf16[512,512]{1,0:T(8,128)(2,1)S(1)} %collective-permute-done.27.refs_0_, bf16[512,512]{1,0:T(8,128)(2,1)S(1)} %collective-permute-done.28.refs_1_, bf16[512,512]{1,0:T(8,128)(2,1)S(1)} %collective-permute-done.31.refs_2_, ...), custom_call_target="tpu_custom_call" | custom-call | flops 1024 | bytes 1024 | tf_op jit(solution)/shard_map/finish/pallas_call | solution.py:205
  (75 shorter events, 6.0 us)
Async XLA Ops:
  0.0 19.8 %copy-start.3 = (s32[8]{0:T(128)S(1)}, s32[8]{0:T(128)}, u32[]{:S(2)}) copy-start(s32[8]{0:T(128)} %constant.36.clone) | copy-start | bytes 100
  0.0 19.8 %copy-start.4 = (s32[8]{0:T(128)S(1)}, s32[8]{0:T(128)}, u32[]{:S(2)}) copy-start(s32[8]{0:T(128)} %constant.37.clone) | copy-start | bytes 100
  1.2 15.1 %collective-permute-start = (bf16[512,512]{1,0:T(8,128)(2,1)S(1)}, bf16[512,512]{1,0:T(8,128)(2,1)S(1)}, u32[]{:S(2)}, u32[]{:S(2)}) collective-permute-start(bf16[512,512]{1,0:T(8,128)(2,1)S(1)} %bitcast.12), channel_id=1, source_target_pairs={{0,4},{4,8},{8,12},{12,0},{16,20},{20,24},{24,28},{28,16},{1,5},{5... | collective-permute-start | bytes 1572872 | tf_op jit(solution)/shard_map/along_y1/ppermute | solution.py:232
  3.0 13.8 %collective-permute-start.2 = (bf16[512,512]{1,0:T(8,128)(2,1)S(1)}, bf16[512,512]{1,0:T(8,128)(2,1)S(1)}, u32[]{:S(2)}, u32[]{:S(2)}) collective-permute-start(bf16[512,512]{1,0:T(8,128)(2,1)S(1)} %bitcast.13), channel_id=1, source_target_pairs={{0,12},{4,0},{8,4},{12,8},{16,28},{20,16},{24,20},{28,24},{1,13},{... | collective-permute-start | bytes 1572872 | tf_op jit(solution)/shard_map/along_y3/ppermute | solution.py:232
  4.5 22.2 %collective-permute-start.5 = (bf16[512,512]{1,0:T(8,128)(2,1)S(1)}, bf16[512,512]{1,0:T(8,128)(2,1)S(1)}, u32[]{:S(2)}, u32[]{:S(2)}) collective-permute-start(bf16[512,512]{1,0:T(8,128)(2,1)S(1)} %bitcast.14), channel_id=1, source_target_pairs={{0,16},{4,20},{8,24},{12,28},{16,0},{20,4},{24,8},{28,12},{1,17},{... | collective-permute-start | bytes 1572872 | tf_op jit(solution)/shard_map/across_x/ppermute | solution.py:228
  16.4 12.5 %collective-permute-start.1 = (bf16[256,512]{1,0:T(8,128)(2,1)S(1)}, bf16[256,512]{1,0:T(8,128)(2,1)S(1)}, u32[]{:S(2)}, u32[]{:S(2)}) collective-permute-start(bf16[256,512]{1,0:T(8,128)(2,1)S(1)} %slice.54), channel_id=1, source_target_pairs={{0,4},{4,8},{8,12},{12,0},{16,20},{20,24},{24,28},{28,16},{1,5},{5... | collective-permute-start | bytes 786440 | tf_op jit(solution)/shard_map/along_y1/ppermute | solution.py:232
  16.7 12.2 %collective-permute-start.3 = (bf16[256,512]{1,0:T(8,128)(2,1)S(1)}, bf16[256,512]{1,0:T(8,128)(2,1)S(1)}, u32[]{:S(2)}, u32[]{:S(2)}) collective-permute-start(bf16[256,512]{1,0:T(8,128)(2,1)S(1)} %slice.55), channel_id=1, source_target_pairs={{0,12},{4,0},{8,4},{12,8},{16,28},{20,16},{24,20},{28,24},{1,13},{... | collective-permute-start | bytes 786440 | tf_op jit(solution)/shard_map/along_y3/ppermute | solution.py:232
  26.8 12.5 %collective-permute-start.6 = (bf16[512,512]{1,0:T(8,128)(2,1)S(1)}, bf16[512,512]{1,0:T(8,128)(2,1)S(1)}, u32[]{:S(2)}, u32[]{:S(2)}) collective-permute-start(bf16[512,512]{1,0:T(8,128)(2,1)S(1)} %collective-permute-done.5.refs_0_), channel_id=1, source_target_pairs={{0,12},{4,0},{8,4},{12,8},{16,28},{20,16},{24,20},{28,24},{1,13},{... | collective-permute-start | bytes 1572872 | tf_op jit(solution)/shard_map/along_y3/ppermute | solution.py:232
  27.4 13.2 %collective-permute-start.7 = (bf16[512,512]{1,0:T(8,128)(2,1)S(1)}, bf16[512,512]{1,0:T(8,128)(2,1)S(1)}, u32[]{:S(2)}, u32[]{:S(2)}) collective-permute-start(bf16[512,512]{1,0:T(8,128)(2,1)S(1)} %collective-permute-done.5.refs_0_), channel_id=1, source_target_pairs={{0,4},{4,8},{8,12},{12,0},{16,20},{20,24},{24,28},{28,16},{1,5},{5... | collective-permute-start | bytes 1572872 | tf_op jit(solution)/shard_map/along_y1/ppermute | solution.py:232
  28.9 14.7 %collective-permute-start.4 = (bf16[512,512]{1,0:T(8,128)(2,1)S(1)}, bf16[512,512]{1,0:T(8,128)(2,1)S(1)}, u32[]{:S(2)}, u32[]{:S(2)}) collective-permute-start(bf16[512,512]{1,0:T(8,128)(2,1)S(1)} %constant_dynamic-update-slice_fusion.refs_1_), channel_id=1, source_target_pairs={{0,16},{4,20},{8,24},{12,28},{16,0},{20,4},{24,8},{28,12},{1,17},{... | collective-permute-start | bytes 1572872 | tf_op jit(solution)/shard_map/across_x/ppermute | solution.py:228
  45.5 2.7 %collective-permute-start.8 = (bf16[256,2048]{1,0:T(8,128)(2,1)S(1)}, bf16[256,2048]{1,0:T(8,128)(2,1)S(1)}, u32[]{:S(2)}, u32[]{:S(2)}) collective-permute-start(bf16[256,2048]{1,0:T(8,128)(2,1)S(1)} %get-tuple-element.37), channel_id=1, source_target_pairs={{0,32},{32,0},{64,96},{96,64},{1,33},{33,1},{65,97},{97,65},{2,34}... | collective-permute-start | bytes 3145736 | tf_op jit(solution)/shard_map/other_core/ppermute | solution.py:240
  48.2 2.0 %copy-start.2 = (f32[256]{0:T(256)S(1)}, f32[256]{0:T(256)}, u32[]{:S(2)}) copy-start(f32[256]{0:T(256)} %param.12) | copy-start | bytes 3076
  48.6 18.7 %copy-start = (bf16[256,256]{1,0:T(8,128)(2,1)S(1)}, bf16[256,256]{1,0:T(8,128)(2,1)}, u32[]{:S(2)}) copy-start(bf16[256,256]{1,0:T(8,128)(2,1)} %turn.1) | copy-start | bytes 393220
  48.6 18.6 %copy-start.1 = (f32[2048]{0:T(1024)S(1)}, f32[2048]{0:T(1024)}, u32[]{:S(2)}) copy-start(f32[2048]{0:T(1024)} %param.10) | copy-start | bytes 24580
  48.7 6.3 %collective-permute-start.12 = (bf16[128,512]{1,0:T(8,128)(2,1)S(1)}, bf16[128,512]{1,0:T(8,128)(2,1)S(1)}, u32[]{:S(2)}, u32[]{:S(2)}) collective-permute-start(bf16[128,512]{1,0:T(8,128)(2,1)S(1)} %get-tuple-element.63), channel_id=1, source_target_pairs={{0,64},{32,96},{64,0},{96,32},{1,65},{33,97},{65,1},{97,33},{2,66}... | collective-permute-start | bytes 393224 | tf_op jit(solution)/shard_map/other_x/ppermute | solution.py:244
  51.1 7.9 %collective-permute-start.11 = (bf16[128,512]{1,0:T(8,128)(2,1)S(1)}, bf16[128,512]{1,0:T(8,128)(2,1)S(1)}, u32[]{:S(2)}, u32[]{:S(2)}) collective-permute-start(bf16[128,512]{1,0:T(8,128)(2,1)S(1)} %get-tuple-element.64), channel_id=1, source_target_pairs={{0,64},{32,96},{64,0},{96,32},{1,65},{33,97},{65,1},{97,33},{2,66}... | collective-permute-start | bytes 393224 | tf_op jit(solution)/shard_map/other_x/ppermute | solution.py:244
  51.7 8.9 %collective-permute-start.10 = (bf16[128,512]{1,0:T(8,128)(2,1)S(1)}, bf16[128,512]{1,0:T(8,128)(2,1)S(1)}, u32[]{:S(2)}, u32[]{:S(2)}) collective-permute-start(bf16[128,512]{1,0:T(8,128)(2,1)S(1)} %get-tuple-element.65), channel_id=1, source_target_pairs={{0,64},{32,96},{64,0},{96,32},{1,65},{33,97},{65,1},{97,33},{2,66}... | collective-permute-start | bytes 393224 | tf_op jit(solution)/shard_map/other_x/ppermute | solution.py:244
  53.2 11.6 %collective-permute-start.9 = (bf16[128,512]{1,0:T(8,128)(2,1)S(1)}, bf16[128,512]{1,0:T(8,128)(2,1)S(1)}, u32[]{:S(2)}, u32[]{:S(2)}) collective-permute-start(bf16[128,512]{1,0:T(8,128)(2,1)S(1)} %get-tuple-element.66), channel_id=1, source_target_pairs={{0,64},{32,96},{64,0},{96,32},{1,65},{33,97},{65,1},{97,33},{2,66}... | collective-permute-start | bytes 393224 | tf_op jit(solution)/shard_map/other_x/ppermute | solution.py:244
  55.0 12.2 %collective-permute-start.14 = (bf16[2,64,512]{2,1,0:T(8,128)(2,1)S(1)}, bf16[2,64,512]{2,1,0:T(8,128)(2,1)S(1)}, u32[]{:S(2)}, u32[]{:S(2)}) collective-permute-start(bf16[2,64,512]{2,1,0:T(8,128)(2,1)S(1)} %bitcast.22), channel_id=1, source_target_pairs={{0,2},{1,3},{2,0},{3,1},{4,6},{5,7},{6,4},{7,5},{8,10},{9,11},{10,... | collective-permute-start | bytes 393224 | tf_op jit(solution)/shard_map/along_z2/ppermute | solution.py:236
  59.0 8.2 %collective-permute-start.13 = (bf16[2,64,512]{2,1,0:T(8,128)(2,1)S(1)}, bf16[2,64,512]{2,1,0:T(8,128)(2,1)S(1)}, u32[]{:S(2)}, u32[]{:S(2)}) collective-permute-start(bf16[2,64,512]{2,1,0:T(8,128)(2,1)S(1)} %bitcast.23), channel_id=1, source_target_pairs={{0,1},{1,2},{2,3},{3,0},{4,5},{5,6},{6,7},{7,4},{8,9},{9,10},{10,1... | collective-permute-start | bytes 393224 | tf_op jit(solution)/shard_map/along_z1/ppermute | solution.py:236
  60.7 6.6 %collective-permute-start.15 = (bf16[2,64,512]{2,1,0:T(8,128)(2,1)S(1)}, bf16[2,64,512]{2,1,0:T(8,128)(2,1)S(1)}, u32[]{:S(2)}, u32[]{:S(2)}) collective-permute-start(bf16[2,64,512]{2,1,0:T(8,128)(2,1)S(1)} %bitcast.24), channel_id=1, source_target_pairs={{0,3},{1,0},{2,1},{3,2},{4,7},{5,4},{6,5},{7,6},{8,11},{9,8},{10,9... | collective-permute-start | bytes 393224 | tf_op jit(solution)/shard_map/along_z3/ppermute | solution.py:236
  68.5 12.1 %collective-permute-start.18 = (bf16[2,64,512]{2,1,0:T(8,128)(2,1)S(1)}, bf16[2,64,512]{2,1,0:T(8,128)(2,1)S(1)}, u32[]{:S(2)}, u32[]{:S(2)}) collective-permute-start(bf16[2,64,512]{2,1,0:T(8,128)(2,1)S(1)} %get-tuple-element.47), channel_id=1, source_target_pairs={{0,2},{1,3},{2,0},{3,1},{4,6},{5,7},{6,4},{7,5},{8,10},{9,11},{10,... | collective-permute-start | bytes 393224 | tf_op jit(solution)/shard_map/along_z2/ppermute | solution.py:236
  70.8 9.7 %collective-permute-start.17 = (bf16[2,64,512]{2,1,0:T(8,128)(2,1)S(1)}, bf16[2,64,512]{2,1,0:T(8,128)(2,1)S(1)}, u32[]{:S(2)}, u32[]{:S(2)}) collective-permute-start(bf16[2,64,512]{2,1,0:T(8,128)(2,1)S(1)} %get-tuple-element.45), channel_id=1, source_target_pairs={{0,1},{1,2},{2,3},{3,0},{4,5},{5,6},{6,7},{7,4},{8,9},{9,10},{10,1... | collective-permute-start | bytes 393224 | tf_op jit(solution)/shard_map/along_z1/ppermute | solution.py:236
  73.1 7.5 %collective-permute-start.16 = (bf16[2,64,512]{2,1,0:T(8,128)(2,1)S(1)}, bf16[2,64,512]{2,1,0:T(8,128)(2,1)S(1)}, u32[]{:S(2)}, u32[]{:S(2)}) collective-permute-start(bf16[2,64,512]{2,1,0:T(8,128)(2,1)S(1)} %get-tuple-element.42), channel_id=1, source_target_pairs={{0,3},{1,0},{2,1},{3,2},{4,7},{5,4},{6,5},{7,6},{8,11},{9,8},{10,9... | collective-permute-start | bytes 393224 | tf_op jit(solution)/shard_map/along_z3/ppermute | solution.py:236
  80.6 4.2 %collective-permute-start.19 = (bf16[128,2048]{1,0:T(8,128)(2,1)S(1)}, bf16[128,2048]{1,0:T(8,128)(2,1)S(1)}, u32[]{:S(2)}, u32[]{:S(2)}) collective-permute-start(bf16[128,2048]{1,0:T(8,128)(2,1)S(1)} %bitcast.20), channel_id=1, source_target_pairs={{0,32},{32,0},{64,96},{96,64},{1,33},{33,1},{65,97},{97,65},{2,34}... | collective-permute-start | bytes 1572872 | tf_op jit(solution)/shard_map/other_core/ppermute | solution.py:240
  80.7 14.3 %collective-permute-start.22 = (bf16[2,64,512]{2,1,0:T(8,128)(2,1)S(1)}, bf16[2,64,512]{2,1,0:T(8,128)(2,1)S(1)}, u32[]{:S(2)}, u32[]{:S(2)}) collective-permute-start(bf16[2,64,512]{2,1,0:T(8,128)(2,1)S(1)} %get-tuple-element.41.go_ref), channel_id=1, source_target_pairs={{0,64},{32,96},{64,0},{96,32},{1,65},{33,97},{65,1},{97,33},{2,66}... | collective-permute-start | bytes 393224 | tf_op jit(solution)/shard_map/other_x/ppermute | solution.py:244
  82.4 7.5 %collective-permute-start.25 = (bf16[2,64,512]{2,1,0:T(8,128)(2,1)S(1)}, bf16[2,64,512]{2,1,0:T(8,128)(2,1)S(1)}, u32[]{:S(2)}, u32[]{:S(2)}) collective-permute-start(bf16[2,64,512]{2,1,0:T(8,128)(2,1)S(1)} %collective-permute-done.18), channel_id=1, source_target_pairs={{0,64},{32,96},{64,0},{96,32},{1,65},{33,97},{65,1},{97,33},{2,66}... | collective-permute-start | bytes 393224 | tf_op jit(solution)/shard_map/other_x/ppermute | solution.py:244
  82.8 9.9 %collective-permute-start.24 = (bf16[2,64,512]{2,1,0:T(8,128)(2,1)S(1)}, bf16[2,64,512]{2,1,0:T(8,128)(2,1)S(1)}, u32[]{:S(2)}, u32[]{:S(2)}) collective-permute-start(bf16[2,64,512]{2,1,0:T(8,128)(2,1)S(1)} %collective-permute-done.17), channel_id=1, source_target_pairs={{0,64},{32,96},{64,0},{96,32},{1,65},{33,97},{65,1},{97,33},{2,66}... | collective-permute-start | bytes 393224 | tf_op jit(solution)/shard_map/other_x/ppermute | solution.py:244
  84.4 10.6 %collective-permute-start.23 = (bf16[2,64,512]{2,1,0:T(8,128)(2,1)S(1)}, bf16[2,64,512]{2,1,0:T(8,128)(2,1)S(1)}, u32[]{:S(2)}, u32[]{:S(2)}) collective-permute-start(bf16[2,64,512]{2,1,0:T(8,128)(2,1)S(1)} %collective-permute-done.16), channel_id=1, source_target_pairs={{0,64},{32,96},{64,0},{96,32},{1,65},{33,97},{65,1},{97,33},{2,66}... | collective-permute-start | bytes 393224 | tf_op jit(solution)/shard_map/other_x/ppermute | solution.py:244
  95.2 4.8 %collective-permute-start.26 = (bf16[128,2048]{1,0:T(8,128)(2,1)S(1)}, bf16[128,2048]{1,0:T(8,128)(2,1)S(1)}, u32[]{:S(2)}, u32[]{:S(2)}) collective-permute-start(bf16[128,2048]{1,0:T(8,128)(2,1)S(1)} %bitcast.18), channel_id=1, source_target_pairs={{0,32},{32,0},{64,96},{96,64},{1,33},{33,1},{65,97},{97,65},{2,34}... | collective-permute-start | bytes 1572872 | tf_op jit(solution)/shard_map/other_core/ppermute | solution.py:240
  95.3 11.6 %collective-permute-start.20 = (bf16[256,512]{1,0:T(8,128)(2,1)S(1)}, bf16[256,512]{1,0:T(8,128)(2,1)S(1)}, u32[]{:S(2)}, u32[]{:S(2)}) collective-permute-start(bf16[256,512]{1,0:T(8,128)(2,1)S(1)} %get-tuple-element.50), channel_id=1, source_target_pairs={{0,4},{4,8},{8,12},{12,0},{16,20},{20,24},{24,28},{28,16},{1,5},{5... | collective-permute-start | bytes 786440 | tf_op jit(solution)/shard_map/along_y1/ppermute | solution.py:232
  97.0 13.1 %collective-permute-start.21 = (bf16[256,512]{1,0:T(8,128)(2,1)S(1)}, bf16[256,512]{1,0:T(8,128)(2,1)S(1)}, u32[]{:S(2)}, u32[]{:S(2)}) collective-permute-start(bf16[256,512]{1,0:T(8,128)(2,1)S(1)} %get-tuple-element.51), channel_id=1, source_target_pairs={{0,12},{4,0},{8,4},{12,8},{16,28},{20,16},{24,20},{28,24},{1,13},{... | collective-permute-start | bytes 786440 | tf_op jit(solution)/shard_map/along_y3/ppermute | solution.py:232
  100.1 13.0 %collective-permute-start.32 = (bf16[256,512]{1,0:T(8,128)(2,1)S(1)}, bf16[256,512]{1,0:T(8,128)(2,1)S(1)}, u32[]{:S(2)}, u32[]{:S(2)}) collective-permute-start(bf16[256,512]{1,0:T(8,128)(2,1)S(1)} %expand.13), channel_id=1, source_target_pairs={{0,16},{4,20},{8,24},{12,28},{16,0},{20,4},{24,8},{28,12},{1,17},{... | collective-permute-start | bytes 786440 | tf_op jit(solution)/shard_map/across_x/ppermute | solution.py:228
  106.4 9.9 %collective-permute-start.33 = (bf16[256,512]{1,0:T(8,128)(2,1)S(1)}, bf16[256,512]{1,0:T(8,128)(2,1)S(1)}, u32[]{:S(2)}, u32[]{:S(2)}) collective-permute-start(bf16[256,512]{1,0:T(8,128)(2,1)S(1)} %expand.14), channel_id=1, source_target_pairs={{0,16},{4,20},{8,24},{12,28},{16,0},{20,4},{24,8},{28,12},{1,17},{... | collective-permute-start | bytes 786440 | tf_op jit(solution)/shard_map/across_x/ppermute | solution.py:228
  106.9 11.4 %collective-permute-start.29 = (bf16[256,512]{1,0:T(8,128)(2,1)S(1)}, bf16[256,512]{1,0:T(8,128)(2,1)S(1)}, u32[]{:S(2)}, u32[]{:S(2)}) collective-permute-start(bf16[256,512]{1,0:T(8,128)(2,1)S(1)} %get-tuple-element.59), channel_id=1, source_target_pairs={{0,4},{4,8},{8,12},{12,0},{16,20},{20,24},{24,28},{28,16},{1,5},{5... | collective-permute-start | bytes 786440 | tf_op jit(solution)/shard_map/along_y1/ppermute | solution.py:232
  106.9 11.4 %collective-permute-start.30 = (bf16[256,512]{1,0:T(8,128)(2,1)S(1)}, bf16[256,512]{1,0:T(8,128)(2,1)S(1)}, u32[]{:S(2)}, u32[]{:S(2)}) collective-permute-start(bf16[256,512]{1,0:T(8,128)(2,1)S(1)} %get-tuple-element.60), channel_id=1, source_target_pairs={{0,12},{4,0},{8,4},{12,8},{16,28},{20,16},{24,20},{28,24},{1,13},{... | collective-permute-start | bytes 786440 | tf_op jit(solution)/shard_map/along_y3/ppermute | solution.py:232
  113.0 25.1 %collective-permute-start.27 = (bf16[512,512]{1,0:T(8,128)(2,1)S(1)}, bf16[512,512]{1,0:T(8,128)(2,1)S(1)}, u32[]{:S(2)}, u32[]{:S(2)}) collective-permute-start(bf16[512,512]{1,0:T(8,128)(2,1)S(1)} %get-tuple-element.57), channel_id=1, source_target_pairs={{0,4},{4,8},{8,12},{12,0},{16,20},{20,24},{24,28},{28,16},{1,5},{5... | collective-permute-start | bytes 1572872 | tf_op jit(solution)/shard_map/along_y1/ppermute | solution.py:232
  113.1 25.0 %collective-permute-start.28 = (bf16[512,512]{1,0:T(8,128)(2,1)S(1)}, bf16[512,512]{1,0:T(8,128)(2,1)S(1)}, u32[]{:S(2)}, u32[]{:S(2)}) collective-permute-start(bf16[512,512]{1,0:T(8,128)(2,1)S(1)} %get-tuple-element.58), channel_id=1, source_target_pairs={{0,12},{4,0},{8,4},{12,8},{16,28},{20,16},{24,20},{28,24},{1,13},{... | collective-permute-start | bytes 1572872 | tf_op jit(solution)/shard_map/along_y3/ppermute | solution.py:232
  118.2 20.0 %collective-permute-start.34 = (bf16[512,512]{1,0:T(8,128)(2,1)S(1)}, bf16[512,512]{1,0:T(8,128)(2,1)S(1)}, u32[]{:S(2)}, u32[]{:S(2)}) collective-permute-start(bf16[512,512]{1,0:T(8,128)(2,1)S(1)} %expand.15), channel_id=1, source_target_pairs={{0,8},{4,12},{8,0},{12,4},{16,24},{20,28},{24,16},{28,20},{1,9},{5... | collective-permute-start | bytes 1572872 | tf_op jit(solution)/shard_map/along_y2/ppermute | solution.py:232
  120.2 18.0 %collective-permute-start.31 = (bf16[512,512]{1,0:T(8,128)(2,1)S(1)}, bf16[512,512]{1,0:T(8,128)(2,1)S(1)}, u32[]{:S(2)}, u32[]{:S(2)}) collective-permute-start(bf16[512,512]{1,0:T(8,128)(2,1)S(1)} %expand.12), channel_id=1, source_target_pairs={{0,16},{4,20},{8,24},{12,28},{16,0},{20,4},{24,8},{28,12},{1,17},{... | collective-permute-start | bytes 1572872 | tf_op jit(solution)/shard_map/across_x/ppermute | solution.py:228

commit v3 on v2

--- a/solution.py
+++ b/solution.py
@@ -100,43 +100,23 @@
     )(at, a, basis)
 
 
-def load_kernel(go_ref, basis_ref, table, done, sem):
-    copy = pltpu.make_async_copy(basis_ref, table, sem)
-    copy.start()
-    done[...] = go_ref[0, :8, :128]
-    copy.wait()
-
-
-def load(basis, go):
-    return pl.pallas_call(
-        load_kernel,
-        in_specs=[VMEM, pl.BlockSpec(memory_space=pl.ANY)],
-        out_specs=[VMEM, VMEM],
-        out_shape=[
-            pltpu.VMEM(basis.shape, basis.dtype),
-            jax.ShapeDtypeStruct((8, 128), go.dtype),
-        ],
-        scratch_shapes=[pltpu.SemaphoreType.DMA(())],
-        cost_estimate=COST,
-        compiler_params=PARAMS,
-        name="load",
-    )(go, basis)
-
-
 def expand_kernel(which, ns, n, adds, at_ref, *refs):
     fields, table, refs = refs[:n], refs[n], refs[n + 1 :]
     m = fields[0].shape[0]
-    for i, out in zip(which, refs[n * adds :]):
-        for h, a in enumerate(fields):
-            value = lax.dot_general(
-                a[...],
-                table[rows_at(at_ref, i, ns), :],
-                (((1,), (1,)), ((), ())),
-                preferred_element_type=F32,
-            )
-            for add in refs[h * adds : (h + 1) * adds]:
-                value = value + add[...].astype(F32)
-            out[h * m : (h + 1) * m, :] = value.astype(out.dtype)
+    for group, out in zip(which, refs[n * adds :]):
+        row = 0
+        for i in group:
+            for h, a in enumerate(fields):
+                value = lax.dot_general(
+                    a[...],
+                    table[rows_at(at_ref, i, ns), :],
+                    (((1,), (1,)), ((), ())),
+                    preferred_element_type=F32,
+                )
+                for add in refs[h * adds : (h + 1) * adds]:
+                    value = value + add[:m, :].astype(F32)
+                out[row : row + m, :] = value.astype(out.dtype)
+                row += m
 
 
 def expand(fields, which, at, table, ns, adds=(), dtype=BF16):
@@ -146,7 +126,7 @@
         functools.partial(expand_kernel, which, ns, len(fields), len(flat) // len(fields)),
         in_specs=[SMEM] + [VMEM] * (len(fields) + 1 + len(flat)),
         out_specs=[VMEM] * len(which),
-        out_shape=[jax.ShapeDtypeStruct((rows, ns), dtype)] * len(which),
+        out_shape=[jax.ShapeDtypeStruct((rows * len(group), ns), dtype) for group in which],
         cost_estimate=COST,
         compiler_params=PARAMS,
         name="expand",
@@ -154,63 +134,99 @@
     return out if len(which) > 1 else out[0]
 
 
-def filter_kernel(at_ref, noise, space, time, turn, *refs):
+def filter_kernel(nt, at_ref, noise, space, time, turn, *refs):
     ins, outs, held = refs[:4], refs[4:8], refs[8]
-    pair, nt, width = ins[0].shape
+    rows, width = ins[0].shape
+    pair = rows // nt
     z = at_ref[8]
+
+    def times(k):
+        return pl.ds(pl.multiple_of(((z - k) & 3) * nt, nt), nt)
+
     for k in range(4):
-        rows = pl.ds(pl.multiple_of(((z - k) & 3) * nt, nt), nt)
         for r in range(pair):
-            held[rows, r * width : (r + 1) * width] = ins[k][r]
+            held[times(k), r * width : (r + 1) * width] = ins[k][r * nt : (r + 1) * nt, :]
     mixed = lax.dot_general(
         turn[...], held[...], (((0,), (0,)), ((), ())), preferred_element_type=F32
     )
-    value = space[:, pl.ds(pl.multiple_of(z * width, width), width)]
-    denom = value * time[...] + noise[0]
+    space_value = space[:, pl.ds(pl.multiple_of(z * width, width), width)]
+    time_value = jnp.broadcast_to(time[...], (8, time.shape[1])).T[:, :1]
+    denom = space_value * time_value + noise[0]
     scaled = mixed / jnp.concatenate([denom] * pair, axis=1)
-    held[...] = jnp.dot(
-        turn[...], scaled.astype(BF16), preferred_element_type=F32
-    ).astype(BF16)
+    back = jnp.dot(turn[...], scaled.astype(BF16), preferred_element_type=F32)
+    held[...] = back.astype(BF16)
     for k in range(4):
-        rows = pl.ds(pl.multiple_of(((z - k) & 3) * nt, nt), nt)
         for r in range(pair):
-            outs[k][r] = held[rows, r * width : (r + 1) * width]
-
-
-def time_filter(parts, at, noise, space, time, turn):
-    pair, nt, width = parts[0].shape
+            outs[k][r * nt : (r + 1) * nt, :] = held[times(k), r * width : (r + 1) * width]
+
+
+def time_filter(parts, nt, at, noise, space, time, turn):
+    rows, width = parts[0].shape
     return pl.pallas_call(
-        filter_kernel,
+        functools.partial(filter_kernel, nt),
         in_specs=[SMEM, SMEM] + [VMEM] * 7,
         out_specs=[VMEM] * 4,
-        out_shape=[jax.ShapeDtypeStruct((pair, nt, width), BF16)] * 4,
-        scratch_shapes=[pltpu.VMEM((4 * nt, pair * width), BF16)],
+        out_shape=[jax.ShapeDtypeStruct((rows, width), BF16)] * 4,
+        scratch_shapes=[pltpu.VMEM((4 * nt, rows // nt * width), BF16)],
         cost_estimate=COST,
         compiler_params=PARAMS,
         name="time_filter",
-    )(at, noise, space[None, :], time[:, None], turn, *parts)
+    )(at, noise, space[None, :], time[None, :], turn, *parts)
+
+
+def assemble_kernel(n, at_ref, *refs):
+    parts, whole, rest = refs[:n], refs[n], refs[n + 1 :]
+    rows, width = parts[0].shape
+    for k in range(4):
+        if n == 4:
+            part = parts[k][...]
+            if k:
+                rest[0][(k - 1) * rows : k * rows, :] = part
+        else:
+            part = parts[1][(k - 1) * rows : k * rows, :] if k else parts[0][...]
+        whole[:, pl.ds(pl.multiple_of(((at_ref[8] + k) & 3) * width, width), width)] = part
+
+
+def assemble(parts, at):
+    n = len(parts)
+    rows, width = parts[0].shape
+    out_shape = [jax.ShapeDtypeStruct((rows, 4 * width), BF16)]
+    if n == 4:
+        out_shape.append(jax.ShapeDtypeStruct((3 * rows, width), BF16))
+    out = pl.pallas_call(
+        functools.partial(assemble_kernel, n),
+        in_specs=[SMEM] + [VMEM] * n,
+        out_specs=[VMEM] * len(out_shape),
+        out_shape=out_shape,
+        cost_estimate=COST,
+        compiler_params=PARAMS,
+        name="assemble",
+    )(at, *parts)
+    return out if n == 4 else out[0]
 
 
 def finish_kernel(rows, at_ref, total, *refs):
-    g, out = at_ref[9], refs[-1]
-    value = total[...]
-    for a in refs[:-1]:
-        value = value + a[...].astype(F32)
+    g, adds, out = at_ref[9], refs[:-1], refs[-1]
+    n = len(adds) // 2
     for k in range(4):
-        to = pl.ds(pl.multiple_of((g ^ k) * rows, rows), rows)
-        out[to, :] = value[k * rows : (k + 1) * rows]
+        value = total[k * rows : (k + 1) * rows, :]
+        for a in adds[n * (k // 2) : n * (k // 2 + 1)]:
+            start = a.shape[0] - 2 * rows + (k % 2) * rows
+            value = value + a[start : start + rows, :].astype(F32)
+        out[pl.ds(pl.multiple_of((g ^ k) * rows, rows), rows), :] = value
 
 
 def finish(total, at, adds):
+    flat = [*adds[0], *adds[1]]
     return pl.pallas_call(
         functools.partial(finish_kernel, total.shape[0] // 4),
-        in_specs=[SMEM] + [VMEM] * (1 + len(adds)),
+        in_specs=[SMEM] + [VMEM] * (1 + len(flat)),
         out_specs=VMEM,
         out_shape=jax.ShapeDtypeStruct(total.shape, F32),
         cost_estimate=COST,
         compiler_params=PARAMS,
         name="finish",
-    )(at, total, *adds)
+    )(at, total, *flat)
 
 
 def shards(right_sides, eigen_basis, space_values, time_basis, time_values, noise_level):
@@ -255,6 +271,7 @@
     down, up = along_y(own, 1), along_y(own, -1)
     x_own = across_x(own)
     table, total = project_first(own, at, eigen_basis)
+    up, down = after(up, total), after(down, total)
     far = jnp.concatenate(
         [along_y(down[: rows // 2], 1), along_y(up[rows // 2 :], -1)], axis=0
     )
@@ -279,44 +296,54 @@
     for k in (2, 1, 3, 0):
         got = after(from_x[k], spectral)
         spectral = (part(both[half:], k) + got.astype(F32)).astype(BF16)
-        spectral = spectral.reshape(pair, nt, quarter)
         times.append(along_z(spectral, k) if k else spectral)
     two, one, three, zero = times
 
     back = time_filter(
-        [zero, one, two, three], at, noise_level, space_values, time_values, time_basis
-    )
-    table, loaded = load(eigen_basis, back[0])
-    pieces = [back[0]] + [after(along_z(back[k], -k), loaded) for k in (1, 2, 3)]
-
-    def assembled(parts):
-        whole = jnp.zeros((pair, nt, basis), BF16)
-        for k in (0, 1, 3, 2):
-            whole = lax.dynamic_update_slice_in_dim(whole, parts[k], ((tm + k) & 3) * quarter, 2)
-        return whole.reshape(half, basis)
-
-    from_x = {k: other_x(pieces[k]) for k in (0, 1, 3, 2)}
-    mine = assembled(pieces)
+        [zero, one, two, three], nt, at, noise_level, space_values, time_values, time_basis
+    )
+    x_first = other_x(back[0])
+    mine, rest = assemble(
+        [back[0]] + [after(along_z(back[k], -k), x_first) for k in (1, 2, 3)], at
+    )
+
+    x_rest = other_x(rest)
     near = jnp.concatenate([mine, other_core(mine)], 0)
 
-    def first_step(a):
-        s_up, s_down = expand([a], [X_UP, X_DOWN], at, table, ns)
-        s_far = expand([a], [X_FAR], at, table, ns)
-        return (along_y(s_up, 1), along_y(s_down, -1), across_x(s_far)), s_up
-
-    steps_near, sent = first_step(near)
-    from_x = assembled({k: after(a, sent) for k, a in from_x.items()})
+    def send(a, *which):
+        return expand([a], which, at, table, ns)
+
+    def both_ways(pair):
+        return along_y(pair[0], 1), along_y(pair[1], -1)
+
+    s_near = send(near, [X_UP], [X_DOWN])
+    *o_near, f_near = send(after(near, s_near[0]), [UP], [DOWN], [X_FAR])
+    sent = f_near
+    s_near, o_near, f_near = both_ways(s_near), both_ways(o_near), across_x(f_near)
+    from_x = assemble([x_first, after(x_rest, sent, *s_near)], at)
     away = jnp.concatenate([from_x, other_core(from_x)], 0)
-    steps_away, _ = first_step(away)
-    fields = [after(near, *steps_near[:2]), away]
-    o_up, o_down = expand(fields, [UP, DOWN], at, table, ns)
-    o_up, o_down = along_y(o_up, 1), along_y(o_down, -1)
-    o_x = expand(fields, [X_OWN], at, table, ns, (steps_near[:2], steps_away[:2]))
-    o_x = across_x(o_x)
-    o_far = expand(fields, [FAR], at, table, ns, (steps_near[2:], steps_away[2:]))
-    o_far = along_y(o_far, 2)
-    out = expand(fields, [OWN], at, table, ns, (), F32)
-    return finish(out, at, (o_up, o_down, o_x, o_far)).reshape(rhs, nt, ns)
+    f_away = send(away, [X_FAR])
+    s_away = send(after(away, f_away), [X_UP, UP], [X_DOWN, DOWN])
+    sent = s_away[0]
+    s_away, f_away = both_ways(s_away), across_x(f_away)
+
+    def send_sum(a, i, adds, sent, *others):
+        return expand([after(a, sent, *others)], [[i]], at, table, ns, (adds,))
+
+    sent = f_near = send_sum(near, FAR, [f_near], sent)
+    f_near = along_y(f_near, 1)
+    sent = x_near = send_sum(near, X_OWN, s_near, sent, *o_near)
+    x_near = across_x(x_near)
+    sent = f_away = send_sum(away, FAR, [f_away], sent)
+    f_away = along_y(f_away, -1)
+    sent = x_away = send_sum(away, X_OWN, s_away, sent)
+    x_away = across_x(x_away)
+    f_near = along_y(after(f_near, sent), 1)
+    f_away = along_y(after(f_away, sent), -1)
+    fields = [after(near, sent, x_near), away]
+    out = expand(fields, [[OWN]], at, table, ns, (), F32)
+    adds = (*o_near, x_near, f_near), (*s_away, x_away, f_away)
+    return finish(out, at, adds).reshape(rhs, nt, ns)
 
 
 def solution(mesh):

time: 140 us -> 132 us (0.943)
  waiting for transfers between devices: 38.8 us -> 32.6 us
  Pallas kernels: 42.1 us -> 37.7 us
  starting transfers between devices: 55.4 us -> 58.1 us
    ppermute x13 -> x16, waiting for transfers between devices: 23.8 us -> 13 us  [along_y(): return lax.ppermute(a, 'col', [(c, c & 4 | c + k & 3) for c in range(8)])]
    ppermute x8 -> x6, waiting for transfers between devices: 9.88 us -> 3.97 us  [other_x(): return lax.ppermute(a, 'row', [(r, r ^ 2) for r in range(4)])]
    pallas_call x2 -> x3, Pallas kernels: 7.51 us -> 2.39 us  [the longest x1 1.21 us: time_filter(): pl.pallas_call(functools.partial(filter_kernel, nt), in_specs=[SMEM, SMEM...]
    ppermute x6, waiting for transfers between devices: 2.5 us -> 7.45 us  [along_z(): return lax.ppermute(a, 'tm', [(z, z + k & 3) for z in range(4)])]
    ppermute x5 -> x6, waiting for transfers between devices: 0.01 us -> 4.54 us  [across_x(): return lax.ppermute(a, 'col', [(c, c ^ 4) for c in range(8)])]
    ppermute x13 -> x16, starting transfers between devices: 18.8 us -> 22.7 us  [along_y(): return lax.ppermute(a, 'col', [(c, c & 4 | c + k & 3) for c in range(8)])]
    ppermute x8 -> x6, starting transfers between devices: 8.34 us -> 6.39 us  [other_x(): return lax.ppermute(a, 'row', [(r, r ^ 2) for r in range(4)])]
    ppermute x5 -> x6, starting transfers between devices: 13.1 us -> 14.3 us  [across_x(): return lax.ppermute(a, 'col', [(c, c ^ 4) for c in range(8)])]
  transfers between devices with their start and end apart: 35 -> 37, of which waited for: 11 -> 16; matrix products, arithmetic and copies ran while one was open for 0% -> 0% of each run, Pallas kernels for 27% -> 24%
where the time goes in v3:
time: 132 us
  starting transfers between devices  58.1 us (44%)
  Pallas kernels  37.7 us (29%)
  waiting for transfers between devices  32.6 us (25%)
  local copies, waits for them, and re-layouts  1.37 us (1%)
    ppermute x16, starting transfers between devices, along_y(): return lax.ppermute(a, 'col', [(c, c & 4 | c + k & 3) for c in range(8)])  22.7 us
    pallas_call x9, Pallas kernels, expand(): pl.pallas_call(functools.partial(expand_kernel, which, ns, len(fields), l...  15.3 us
    ppermute x6, starting transfers between devices, along_z(): return lax.ppermute(a, 'tm', [(z, z + k & 3) for z in range(4)])  14.4 us
    ppermute x6, starting transfers between devices, across_x(): return lax.ppermute(a, 'col', [(c, c ^ 4) for c in range(8)])  14.3 us
    ppermute x16, waiting for transfers between devices, along_y(): return lax.ppermute(a, 'col', [(c, c & 4 | c + k & 3) for c in range(8)])  13 us
    pallas_call x4, Pallas kernels, project(): pl.pallas_call(functools.partial(project_kernel, which, final, total is n...  11.2 us
    ppermute x6, waiting for transfers between devices, along_z(): return lax.ppermute(a, 'tm', [(z, z + k & 3) for z in range(4)])  7.45 us
    pallas_call x1, Pallas kernels, project_first(): pl.pallas_call(first_kernel, in_specs=[SMEM, VMEM, pl.BlockSpec(memory_sp...  6.92 us
  transfers between devices with their start and end apart: 37, of which 16 were waited for; matrix products, arithmetic and copies ran while one was open for 0% of the time, Pallas kernels for 24%

profile of v3, /device:TPU:0, one launch (start us, length us, event | category | flops | bytes accessed | tf_op | source)
XLA Modules:
  0.0 131.5 jit_solution(16501502659179710641)
XLA Ops:
  1.2 1.7 %collective-permute-start = (bf16[512,512]{1,0:T(8,128)(2,1)S(1)}, bf16[512,512]{1,0:T(8,128)(2,1)S(1)}, u32[]{:S(2)}, u32[]{:S(2)}) collective-permute-start(bf16[512,512]{1,0:T(8,128)(2,1)S(1)} %bitcast.6), channel_id=1, source_target_pairs={{0,4},{4,8},{8,12},{12,0},{16,20},{20,24},{24,28},{28,16},{1,5},{5... | collective-permute-start | bytes 1572872 | tf_op jit(solution)/shard_map/along_y1/ppermute | solution.py:248
  3.0 1.6 %collective-permute-start.2 = (bf16[512,512]{1,0:T(8,128)(2,1)S(1)}, bf16[512,512]{1,0:T(8,128)(2,1)S(1)}, u32[]{:S(2)}, u32[]{:S(2)}) collective-permute-start(bf16[512,512]{1,0:T(8,128)(2,1)S(1)} %bitcast.7), channel_id=1, source_target_pairs={{0,12},{4,0},{8,4},{12,8},{16,28},{20,16},{24,20},{28,24},{1,13},{... | collective-permute-start | bytes 1572872 | tf_op jit(solution)/shard_map/along_y3/ppermute | solution.py:248
  4.5 3.1 %collective-permute-start.5 = (bf16[512,512]{1,0:T(8,128)(2,1)S(1)}, bf16[512,512]{1,0:T(8,128)(2,1)S(1)}, u32[]{:S(2)}, u32[]{:S(2)}) collective-permute-start(bf16[512,512]{1,0:T(8,128)(2,1)S(1)} %bitcast.8), channel_id=1, source_target_pairs={{0,16},{4,20},{8,24},{12,28},{16,0},{20,4},{24,8},{28,12},{1,17},{... | collective-permute-start | bytes 1572872 | tf_op jit(solution)/shard_map/across_x/ppermute | solution.py:244
  7.7 6.9 %project_first.1 = (bf16[4096,2048]{1,0:T(8,128)(2,1)S(1)}, f32[512,2048]{1,0:T(8,128)S(1)}) custom-call(s32[10]{0:T(128)S(1)} %pad_add_fusion.at_ref, bf16[512,512]{1,0:T(8,128)(2,1)S(1)} %bitcast.9, bf16[4096,2048]{1,0:T(8,128)(2,1)} %basis_ref.1), custom_call_target="tpu_custom_call" | custom-call | flops 1024 | bytes 1024 | tf_op jit(solution)/shard_map/project_first/pallas_call | solution.py:88
  14.7 1.7 %collective-permute-done.refs_1_ = bf16[512,512]{1,0:T(8,128)(2,1)S(1)} collective-permute-done((bf16[512,512]{1,0:T(8,128)(2,1)S(1)}, bf16[512,512]{1,0:T(8,128)(2,1)S(1)}, u32[]{:S(2)}, u32[]{:S(2)}) %collective-permute-start) | collective-permute-done | bytes 524320 | tf_op jit(solution)/shard_map/along_y1/ppermute | solution.py:248
  16.7 3.0 %collective-permute-start.3 = (bf16[256,512]{1,0:T(8,128)(2,1)S(1)}, bf16[256,512]{1,0:T(8,128)(2,1)S(1)}, u32[]{:S(2)}, u32[]{:S(2)}) collective-permute-start(bf16[256,512]{1,0:T(8,128)(2,1)S(1)} %slice.45), channel_id=1, source_target_pairs={{0,12},{4,0},{8,4},{12,8},{16,28},{20,16},{24,20},{28,24},{1,13},{... | collective-permute-start | bytes 786440 | tf_op jit(solution)/shard_map/along_y3/ppermute | solution.py:248
  19.8 1.3 collective-permute-start.6
  21.8 5.1 %collective-permute-done.1 = bf16[256,512]{1,0:T(8,128)(2,1)S(1)} collective-permute-done((bf16[256,512]{1,0:T(8,128)(2,1)S(1)}, bf16[256,512]{1,0:T(8,128)(2,1)S(1)}, u32[]{:S(2)}, u32[]{:S(2)}) %collective-permute-start.1) | collective-permute-done | bytes 262176 | tf_op jit(solution)/shard_map/along_y1/ppermute | solution.py:248
  26.9 3.0 %collective-permute-start.4 = (bf16[512,512]{1,0:T(8,128)(2,1)S(1)}, bf16[512,512]{1,0:T(8,128)(2,1)S(1)}, u32[]{:S(2)}, u32[]{:S(2)}) collective-permute-start(bf16[512,512]{1,0:T(8,128)(2,1)S(1)} %constant_dynamic-update-slice_fusion.refs_1_), channel_id=1, source_target_pairs={{0,16},{4,20},{8,24},{12,28},{16,0},{20,4},{24,8},{28,12},{1,17},{... | collective-permute-start | bytes 1572872 | tf_op jit(solution)/shard_map/across_x/ppermute | solution.py:244
  29.9 3.2 %project.4.refs_3_ = f32[512,2048]{1,0:T(8,128)S(1)} custom-call(s32[10]{0:T(128)S(1)} %pad_add_fusion.at_ref, bf16[512,512]{1,0:T(8,128)(2,1)S(1)} %collective-permute-done.2.refs_0_, bf16[512,512]{1,0:T(8,128)(2,1)S(1)} %collective-permute-done.refs_1_, bf16[4096,2048]{1,0:T(8,128)(2,1)S(1)} %get-tuple-element.44.refs_2_.refs_1_, ...), custom_call_target="tpu_custom_call", output_to_operand_aliasing={{}: (4, {})} | custom-call | flops 1024 | bytes 1024 | tf_op jit(solution)/shard_map/project/pallas_call | solution.py:61
  33.1 3.2 %project.5.refs_3_ = f32[512,2048]{1,0:T(8,128)S(1)} custom-call(s32[10]{0:T(128)S(1)} %pad_add_fusion.at_ref, bf16[512,512]{1,0:T(8,128)(2,1)S(1)} %collective-permute-done.5.refs_0_, bf16[512,512]{1,0:T(8,128)(2,1)S(1)} %constant_dynamic-update-slice_fusion.refs_1_, ...), custom_call_target="tpu_custom_call", output_to_operand_aliasing={{}: (4, {})} | custom-call | flops 1024 | bytes 1024 | tf_op jit(solution)/shard_map/project/pallas_call | solution.py:61
  36.3 3.1 %project.6.refs_2_ = f32[512,2048]{1,0:T(8,128)S(1)} custom-call(s32[10]{0:T(128)S(1)} %pad_add_fusion.at_ref, bf16[512,512]{1,0:T(8,128)(2,1)S(1)} %collective-permute-done.6.refs_0_, bf16[512,512]{1,0:T(8,128)(2,1)S(1)} %collective-permute-done.7.refs_1_, bf16[4096,2048]{1,0:T(8,128)(2,1)S(1)} %get-tuple-element.44.refs_2_.refs_1_, ...), custom_call_target="tpu_custom_call", output_to_operand_aliasing={{}: (4, {})} | custom-call | flops 1024 | bytes 1024 | tf_op jit(solution)/shard_map/project/pallas_call | solution.py:61
  39.4 1.8 %project.7 = (bf16[256,2048]{1,0:T(8,128)(2,1)S(1)}, f32[256,2048]{1,0:T(8,128)S(1)}) custom-call(s32[10]{0:T(128)S(1)} %pad_add_fusion.at_ref, bf16[512,512]{1,0:T(8,128)(2,1)S(1)} %collective-permute-done.4.refs_0_, bf16[4096,2048]{1,0:T(8,128)(2,1)S(1)} %get-tuple-element.44.refs_2_.refs_1_, f32[512,2048]{1,0:T(8,128)S(1)} %project.6.refs_2_), custom_call_target="tpu_custom_call" | custom-call | flops 1024 | bytes 1024 | tf_op jit(solution)/shard_map/project/pallas_call | solution.py:61
  41.3 2.6 %collective-permute-done.8 = bf16[256,2048]{1,0:T(8,128)(2,1)S(1)} collective-permute-done((bf16[256,2048]{1,0:T(8,128)(2,1)S(1)}, bf16[256,2048]{1,0:T(8,128)(2,1)S(1)}, u32[]{:S(2)}, u32[]{:S(2)}) %collective-permute-start.8) | collective-permute-done | bytes 1048608 | tf_op jit(solution)/shard_map/other_core/ppermute | solution.py:256
  44.4 1.4 %collective-permute-start.12 = (bf16[128,512]{1,0:T(8,128)(2,1)S(1)}, bf16[128,512]{1,0:T(8,128)(2,1)S(1)}, u32[]{:S(2)}, u32[]{:S(2)}) collective-permute-start(bf16[128,512]{1,0:T(8,128)(2,1)S(1)} %get-tuple-element.79), channel_id=1, source_target_pairs={{0,64},{32,96},{64,0},{96,32},{1,65},{33,97},{65,1},{97,33},{2,66}... | collective-permute-start | bytes 393224 | tf_op jit(solution)/shard_map/other_x/ppermute | solution.py:260
  47.2 1.3 collective-permute-start.10
  49.3 1.6 %collective-permute-done.12 = bf16[128,512]{1,0:T(8,128)(2,1)S(1)} collective-permute-done((bf16[128,512]{1,0:T(8,128)(2,1)S(1)}, bf16[128,512]{1,0:T(8,128)(2,1)S(1)}, u32[]{:S(2)}, u32[]{:S(2)}) %collective-permute-start.12) | collective-permute-done | bytes 131104 | tf_op jit(solution)/shard_map/other_x/ppermute | solution.py:260
  50.9 4.0 %collective-permute-start.14 = (bf16[128,512]{1,0:T(8,128)(2,1)S(1)}, bf16[128,512]{1,0:T(8,128)(2,1)S(1)}, u32[]{:S(2)}, u32[]{:S(2)}) collective-permute-start(bf16[128,512]{1,0:T(8,128)(2,1)S(1)} %fusion), channel_id=1, source_target_pairs={{0,2},{1,3},{2,0},{3,1},{4,6},{5,7},{6,4},{7,5},{8,10},{9,11},{10,... | collective-permute-start | bytes 393224 | tf_op jit(solution)/shard_map/along_z2/ppermute | solution.py:252
  54.9 1.2 collective-permute-start.13
  56.5 4.1 %collective-permute-start.15 = (bf16[128,512]{1,0:T(8,128)(2,1)S(1)}, bf16[128,512]{1,0:T(8,128)(2,1)S(1)}, u32[]{:S(2)}, u32[]{:S(2)}) collective-permute-start(bf16[128,512]{1,0:T(8,128)(2,1)S(1)} %fusion.2), channel_id=1, source_target_pairs={{0,3},{1,0},{2,1},{3,2},{4,7},{5,4},{6,5},{7,6},{8,11},{9,8},{10,9... | collective-permute-start | bytes 393224 | tf_op jit(solution)/shard_map/along_z3/ppermute | solution.py:252
  60.6 2.5 %collective-permute-done.15.refs_3_ = bf16[128,512]{1,0:T(8,128)(2,1)S(1)} collective-permute-done((bf16[128,512]{1,0:T(8,128)(2,1)S(1)}, bf16[128,512]{1,0:T(8,128)(2,1)S(1)}, u32[]{:S(2)}, u32[]{:S(2)}) %collective-permute-start.15) | collective-permute-done | bytes 131104 | tf_op jit(solution)/shard_map/along_z3/ppermute | solution.py:252
  64.3 1.4 %collective-permute-start.17 = (bf16[128,512]{1,0:T(8,128)(2,1)S(1)}, bf16[128,512]{1,0:T(8,128)(2,1)S(1)}, u32[]{:S(2)}, u32[]{:S(2)}) collective-permute-start(bf16[128,512]{1,0:T(8,128)(2,1)S(1)} %get-tuple-element.51.refs_0_), channel_id=1, source_target_pairs={{0,64},{32,96},{64,0},{96,32},{1,65},{33,97},{65,1},{97,33},{2,66}... | collective-permute-start | bytes 393224 | tf_op jit(solution)/shard_map/other_x/ppermute | solution.py:260
  66.0 4.8 %collective-permute-start.18 = (bf16[128,512]{1,0:T(8,128)(2,1)S(1)}, bf16[128,512]{1,0:T(8,128)(2,1)S(1)}, u32[]{:S(2)}, u32[]{:S(2)}) collective-permute-start(bf16[128,512]{1,0:T(8,128)(2,1)S(1)} %get-tuple-element.54), channel_id=1, source_target_pairs={{0,2},{1,3},{2,0},{3,1},{4,6},{5,7},{6,4},{7,5},{8,10},{9,11},{10,... | collective-permute-start | bytes 393224 | tf_op jit(solution)/shard_map/along_z2/ppermute | solution.py:252
  70.9 1.9 %collective-permute-done.19.refs_3_ = bf16[128,512]{1,0:T(8,128)(2,1)S(1)} collective-permute-done((bf16[128,512]{1,0:T(8,128)(2,1)S(1)}, bf16[128,512]{1,0:T(8,128)(2,1)S(1)}, u32[]{:S(2)}, u32[]{:S(2)}) %collective-permute-start.19) | collective-permute-done | bytes 131104 | tf_op jit(solution)/shard_map/along_z1/ppermute | solution.py:252
  72.7 2.5 %collective-permute-done.18.refs_2_ = bf16[128,512]{1,0:T(8,128)(2,1)S(1)} collective-permute-done((bf16[128,512]{1,0:T(8,128)(2,1)S(1)}, bf16[128,512]{1,0:T(8,128)(2,1)S(1)}, u32[]{:S(2)}, u32[]{:S(2)}) %collective-permute-start.18) | collective-permute-done | bytes 131104 | tf_op jit(solution)/shard_map/along_z2/ppermute | solution.py:252
  78.5 1.8 %expand.9 = (bf16[256,512]{1,0:T(8,128)(2,1)S(1)}, bf16[256,512]{1,0:T(8,128)(2,1)S(1)}) custom-call(s32[10]{0:T(128)S(1)} %pad_add_fusion.at_ref, bf16[256,2048]{1,0:T(8,128)(2,1)S(1)} %constant_dynamic-update-slice_fusion.2.refs_0_, bf16[4096,2048]{1,0:T(8,128)(2,1)S(1)} %get-tuple-element.44.refs_2_.refs_1_), custom_call_target="tpu_custom_call" | custom-call | flops 1024 | bytes 1024 | tf_op jit(solution)/shard_map/expand/pallas_call | solution.py:125
  80.8 2.8 %collective-permute-start.23 = (bf16[256,512]{1,0:T(8,128)(2,1)S(1)}, bf16[256,512]{1,0:T(8,128)(2,1)S(1)}, u32[]{:S(2)}, u32[]{:S(2)}) collective-permute-start(bf16[256,512]{1,0:T(8,128)(2,1)S(1)} %get-tuple-element.63), channel_id=1, source_target_pairs={{0,12},{4,0},{8,4},{12,8},{16,28},{20,16},{24,20},{28,24},{1,13},{... | collective-permute-start | bytes 786440 | tf_op jit(solution)/shard_map/along_y3/ppermute | solution.py:248
  83.6 2.4 %expand.10 = (bf16[256,512]{1,0:T(8,128)(2,1)S(1)}, bf16[256,512]{1,0:T(8,128)(2,1)S(1)}, bf16[256,512]{1,0:T(8,128)(2,1)S(1)}) custom-call(s32[10]{0:T(128)S(1)} %pad_add_fusion.at_ref, bf16[256,2048]{1,0:T(8,128)(2,1)S(1)} %constant_dynamic-update-slice_fusion.2.refs_0_, bf16[4096,2048]{1,0:T(8,128)(2,1)S(1)} %get-tuple-element.44.refs_2_.refs_1_), custom_call_target="tpu_custom_call" | custom-call | flops 1024 | bytes 1024 | tf_op jit(solution)/shard_map/expand/pallas_call | solution.py:125
  86.0 2.1 %collective-permute-done.21.refs_1_ = bf16[384,512]{1,0:T(8,128)(2,1)S(1)} collective-permute-done((bf16[384,512]{1,0:T(8,128)(2,1)S(1)}, bf16[384,512]{1,0:T(8,128)(2,1)S(1)}, u32[]{:S(2)}, u32[]{:S(2)}) %collective-permute-start.21) | collective-permute-done | bytes 393248 | tf_op jit(solution)/shard_map/other_x/ppermute | solution.py:260
  88.1 2.0 %collective-permute-done.22.refs_2_ = bf16[256,512]{1,0:T(8,128)(2,1)S(1)} collective-permute-done((bf16[256,512]{1,0:T(8,128)(2,1)S(1)}, bf16[256,512]{1,0:T(8,128)(2,1)S(1)}, u32[]{:S(2)}, u32[]{:S(2)}) %collective-permute-start.22) | collective-permute-done | bytes 262176 | tf_op jit(solution)/shard_map/along_y1/ppermute | solution.py:248
  90.7 2.8 %collective-permute-start.25 = (bf16[256,512]{1,0:T(8,128)(2,1)S(1)}, bf16[256,512]{1,0:T(8,128)(2,1)S(1)}, u32[]{:S(2)}, u32[]{:S(2)}) collective-permute-start(bf16[256,512]{1,0:T(8,128)(2,1)S(1)} %get-tuple-element.62), channel_id=1, source_target_pairs={{0,16},{4,20},{8,24},{12,28},{16,0},{20,4},{24,8},{28,12},{1,17},{... | collective-permute-start | bytes 786440 | tf_op jit(solution)/shard_map/across_x/ppermute | solution.py:244
  94.8 2.2 %collective-permute-start.27 = (bf16[256,512]{1,0:T(8,128)(2,1)S(1)}, bf16[256,512]{1,0:T(8,128)(2,1)S(1)}, u32[]{:S(2)}, u32[]{:S(2)}) collective-permute-start(bf16[256,512]{1,0:T(8,128)(2,1)S(1)} %get-tuple-element.69), channel_id=1, source_target_pairs={{0,12},{4,0},{8,4},{12,8},{16,28},{20,16},{24,20},{28,24},{1,13},{... | collective-permute-start | bytes 786440 | tf_op jit(solution)/shard_map/along_y3/ppermute | solution.py:248
  96.9 1.3 expand.11
  98.2 2.9 %expand.12 = (bf16[512,512]{1,0:T(8,128)(2,1)S(1)}, bf16[512,512]{1,0:T(8,128)(2,1)S(1)}) custom-call(s32[10]{0:T(128)S(1)} %pad_add_fusion.at_ref, bf16[256,2048]{1,0:T(8,128)(2,1)S(1)} %pad_maximum_fusion.refs_0_.refs_1_, bf16[4096,2048]{1,0:T(8,128)(2,1)S(1)} %get-tuple-element.44.refs_2_.refs_1_), custom_call_target="tpu_custom_call" | custom-call | flops 1024 | bytes 1024 | tf_op jit(solution)/shard_map/expand/pallas_call | solution.py:125
  101.2 3.2 %collective-permute-start.30 = (bf16[512,512]{1,0:T(8,128)(2,1)S(1)}, bf16[512,512]{1,0:T(8,128)(2,1)S(1)}, u32[]{:S(2)}, u32[]{:S(2)}) collective-permute-start(bf16[512,512]{1,0:T(8,128)(2,1)S(1)} %get-tuple-element.73), channel_id=1, source_target_pairs={{0,12},{4,0},{8,4},{12,8},{16,28},{20,16},{24,20},{28,24},{1,13},{... | collective-permute-start | bytes 1572872 | tf_op jit(solution)/shard_map/along_y3/ppermute | solution.py:248
  104.4 1.6 %collective-permute-start.28 = (bf16[256,512]{1,0:T(8,128)(2,1)S(1)}, bf16[256,512]{1,0:T(8,128)(2,1)S(1)}, u32[]{:S(2)}, u32[]{:S(2)}) collective-permute-start(bf16[256,512]{1,0:T(8,128)(2,1)S(1)} %expand.11), channel_id=1, source_target_pairs={{0,16},{4,20},{8,24},{12,28},{16,0},{20,4},{24,8},{28,12},{1,17},{... | collective-permute-start | bytes 786440 | tf_op jit(solution)/shard_map/across_x/ppermute | solution.py:244
  106.0 1.3 expand.13
  107.7 1.3 expand.14
  109.0 4.3 %collective-permute-done.28.refs_2_ = bf16[256,512]{1,0:T(8,128)(2,1)S(1)} collective-permute-done((bf16[256,512]{1,0:T(8,128)(2,1)S(1)}, bf16[256,512]{1,0:T(8,128)(2,1)S(1)}, u32[]{:S(2)}, u32[]{:S(2)}) %collective-permute-start.28) | collective-permute-done | bytes 262176 | tf_op jit(solution)/shard_map/across_x/ppermute | solution.py:244
  113.3 1.3 expand.15
  115.2 2.3 %collective-permute-start.31 = (bf16[256,512]{1,0:T(8,128)(2,1)S(1)}, bf16[256,512]{1,0:T(8,128)(2,1)S(1)}, u32[]{:S(2)}, u32[]{:S(2)}) collective-permute-start(bf16[256,512]{1,0:T(8,128)(2,1)S(1)} %expand.14), channel_id=1, source_target_pairs={{0,16},{4,20},{8,24},{12,28},{16,0},{20,4},{24,8},{28,12},{1,17},{... | collective-permute-start | bytes 786440 | tf_op jit(solution)/shard_map/across_x/ppermute | solution.py:244
  117.4 1.3 expand.16
  118.7 1.5 %collective-permute-start.34 = (bf16[256,512]{1,0:T(8,128)(2,1)S(1)}, bf16[256,512]{1,0:T(8,128)(2,1)S(1)}, u32[]{:S(2)}, u32[]{:S(2)}) collective-permute-start(bf16[256,512]{1,0:T(8,128)(2,1)S(1)} %expand.16), channel_id=1, source_target_pairs={{0,16},{4,20},{8,24},{12,28},{16,0},{20,4},{24,8},{28,12},{1,17},{... | collective-permute-start | bytes 786440 | tf_op jit(solution)/shard_map/across_x/ppermute | solution.py:244
  120.2 1.3 collective-permute-done.32
  121.6 3.2 %collective-permute-start.36 = (bf16[256,512]{1,0:T(8,128)(2,1)S(1)}, bf16[256,512]{1,0:T(8,128)(2,1)S(1)}, u32[]{:S(2)}, u32[]{:S(2)}) collective-permute-start(bf16[256,512]{1,0:T(8,128)(2,1)S(1)} %collective-permute-done.35), channel_id=1, source_target_pairs={{0,12},{4,0},{8,4},{12,8},{16,28},{20,16},{24,20},{28,24},{1,13},{... | collective-permute-start | bytes 786440 | tf_op jit(solution)/shard_map/along_y3/ppermute | solution.py:248
  125.0 1.8 %expand.17.total = f32[512,512]{1,0:T(8,128)S(1)} custom-call(s32[10]{0:T(128)S(1)} %pad_add_fusion.at_ref, bf16[256,2048]{1,0:T(8,128)(2,1)S(1)} %constant_dynamic-update-slice_fusion.2.refs_0_, bf16[256,2048]{1,0:T(8,128)(2,1)S(1)} %pad_maximum_fusion.refs_0_.refs_1_, bf16[4096,2048]{1,0:T(8,128)(2,1)S(1)} %get-tuple-element.44.refs_2_.refs_1_), custom_call_target="tpu_custom_call" | custom-call | flops 1024 | bytes 1024 | tf_op jit(solution)/shard_map/expand/pallas_call | solution.py:125
  126.8 2.9 %collective-permute-done.33.refs_3_ = bf16[256,512]{1,0:T(8,128)(2,1)S(1)} collective-permute-done((bf16[256,512]{1,0:T(8,128)(2,1)S(1)}, bf16[256,512]{1,0:T(8,128)(2,1)S(1)}, u32[]{:S(2)}, u32[]{:S(2)}) %collective-permute-start.33) | collective-permute-done | bytes 262176 | tf_op jit(solution)/shard_map/along_y1/ppermute | solution.py:248
  129.7 1.8 %finish.1 = f32[512,512]{1,0:T(8,128)} custom-call(s32[10]{0:T(128)S(1)} %pad_add_fusion.at_ref, f32[512,512]{1,0:T(8,128)S(1)} %expand.17.total, bf16[256,512]{1,0:T(8,128)(2,1)S(1)} %collective-permute-done.26.refs_0_, bf16[256,512]{1,0:T(8,128)(2,1)S(1)} %collective-permute-done.27.refs_1_, bf16[256,512]{1,0:T(8,128)(2,1)S(1)} %collective-permute-done.31.refs_2_, ...), custom_call_target="tpu_custom_call" | custom-call | flops 1024 | bytes 1024 | tf_op jit(solution)/shard_map/finish/pallas_call | solution.py:221
  (71 shorter events, 13.5 us)
Async XLA Ops:
  0.0 7.7 %copy-start.3 = (s32[8]{0:T(128)S(1)}, s32[8]{0:T(128)}, u32[]{:S(2)}) copy-start(s32[8]{0:T(128)} %constant.30.clone) | copy-start | bytes 100
  0.0 7.7 %copy-start.4 = (s32[8]{0:T(128)S(1)}, s32[8]{0:T(128)}, u32[]{:S(2)}) copy-start(s32[8]{0:T(128)} %constant.31.clone) | copy-start | bytes 100
  1.2 15.1 %collective-permute-start = (bf16[512,512]{1,0:T(8,128)(2,1)S(1)}, bf16[512,512]{1,0:T(8,128)(2,1)S(1)}, u32[]{:S(2)}, u32[]{:S(2)}) collective-permute-start(bf16[512,512]{1,0:T(8,128)(2,1)S(1)} %bitcast.6), channel_id=1, source_target_pairs={{0,4},{4,8},{8,12},{12,0},{16,20},{20,24},{24,28},{28,16},{1,5},{5... | collective-permute-start | bytes 1572872 | tf_op jit(solution)/shard_map/along_y1/ppermute | solution.py:248
  3.0 13.8 %collective-permute-start.2 = (bf16[512,512]{1,0:T(8,128)(2,1)S(1)}, bf16[512,512]{1,0:T(8,128)(2,1)S(1)}, u32[]{:S(2)}, u32[]{:S(2)}) collective-permute-start(bf16[512,512]{1,0:T(8,128)(2,1)S(1)} %bitcast.7), channel_id=1, source_target_pairs={{0,12},{4,0},{8,4},{12,8},{16,28},{20,16},{24,20},{28,24},{1,13},{... | collective-permute-start | bytes 1572872 | tf_op jit(solution)/shard_map/along_y3/ppermute | solution.py:248
  4.5 15.2 %collective-permute-start.5 = (bf16[512,512]{1,0:T(8,128)(2,1)S(1)}, bf16[512,512]{1,0:T(8,128)(2,1)S(1)}, u32[]{:S(2)}, u32[]{:S(2)}) collective-permute-start(bf16[512,512]{1,0:T(8,128)(2,1)S(1)} %bitcast.8), channel_id=1, source_target_pairs={{0,16},{4,20},{8,24},{12,28},{16,0},{20,4},{24,8},{28,12},{1,17},{... | collective-permute-start | bytes 1572872 | tf_op jit(solution)/shard_map/across_x/ppermute | solution.py:244
  16.4 10.5 %collective-permute-start.1 = (bf16[256,512]{1,0:T(8,128)(2,1)S(1)}, bf16[256,512]{1,0:T(8,128)(2,1)S(1)}, u32[]{:S(2)}, u32[]{:S(2)}) collective-permute-start(bf16[256,512]{1,0:T(8,128)(2,1)S(1)} %slice.44), channel_id=1, source_target_pairs={{0,4},{4,8},{8,12},{12,0},{16,20},{20,24},{24,28},{28,16},{1,5},{5... | collective-permute-start | bytes 786440 | tf_op jit(solution)/shard_map/along_y1/ppermute | solution.py:248
  16.7 10.2 %collective-permute-start.3 = (bf16[256,512]{1,0:T(8,128)(2,1)S(1)}, bf16[256,512]{1,0:T(8,128)(2,1)S(1)}, u32[]{:S(2)}, u32[]{:S(2)}) collective-permute-start(bf16[256,512]{1,0:T(8,128)(2,1)S(1)} %slice.45), channel_id=1, source_target_pairs={{0,12},{4,0},{8,4},{12,8},{16,28},{20,16},{24,20},{28,24},{1,13},{... | collective-permute-start | bytes 786440 | tf_op jit(solution)/shard_map/along_y3/ppermute | solution.py:248
  19.8 16.5 %collective-permute-start.6 = (bf16[512,512]{1,0:T(8,128)(2,1)S(1)}, bf16[512,512]{1,0:T(8,128)(2,1)S(1)}, u32[]{:S(2)}, u32[]{:S(2)}) collective-permute-start(bf16[512,512]{1,0:T(8,128)(2,1)S(1)} %collective-permute-done.5.refs_0_), channel_id=1, source_target_pairs={{0,12},{4,0},{8,4},{12,8},{16,28},{20,16},{24,20},{28,24},{1,13},{... | collective-permute-start | bytes 1572872 | tf_op jit(solution)/shard_map/along_y3/ppermute | solution.py:248
  21.0 15.3 %collective-permute-start.7 = (bf16[512,512]{1,0:T(8,128)(2,1)S(1)}, bf16[512,512]{1,0:T(8,128)(2,1)S(1)}, u32[]{:S(2)}, u32[]{:S(2)}) collective-permute-start(bf16[512,512]{1,0:T(8,128)(2,1)S(1)} %collective-permute-done.5.refs_0_), channel_id=1, source_target_pairs={{0,4},{4,8},{8,12},{12,0},{16,20},{20,24},{24,28},{28,16},{1,5},{5... | collective-permute-start | bytes 1572872 | tf_op jit(solution)/shard_map/along_y1/ppermute | solution.py:248
  26.9 12.5 %collective-permute-start.4 = (bf16[512,512]{1,0:T(8,128)(2,1)S(1)}, bf16[512,512]{1,0:T(8,128)(2,1)S(1)}, u32[]{:S(2)}, u32[]{:S(2)}) collective-permute-start(bf16[512,512]{1,0:T(8,128)(2,1)S(1)} %constant_dynamic-update-slice_fusion.refs_1_), channel_id=1, source_target_pairs={{0,16},{4,20},{8,24},{12,28},{16,0},{20,4},{24,8},{28,12},{1,17},{... | collective-permute-start | bytes 1572872 | tf_op jit(solution)/shard_map/across_x/ppermute | solution.py:244
  41.2 2.7 %collective-permute-start.8 = (bf16[256,2048]{1,0:T(8,128)(2,1)S(1)}, bf16[256,2048]{1,0:T(8,128)(2,1)S(1)}, u32[]{:S(2)}, u32[]{:S(2)}) collective-permute-start(bf16[256,2048]{1,0:T(8,128)(2,1)S(1)} %get-tuple-element.47), channel_id=1, source_target_pairs={{0,32},{32,0},{64,96},{96,64},{1,33},{33,1},{65,97},{97,65},{2,34}... | collective-permute-start | bytes 3145736 | tf_op jit(solution)/shard_map/other_core/ppermute | solution.py:256
  44.3 18.8 %copy-start = (bf16[256,256]{1,0:T(8,128)(2,1)S(1)}, bf16[256,256]{1,0:T(8,128)(2,1)}, u32[]{:S(2)}) copy-start(bf16[256,256]{1,0:T(8,128)(2,1)} %turn.1) | copy-start | bytes 393220
  44.3 18.8 %copy-start.1 = (f32[2048]{0:T(1024)S(1)}, f32[2048]{0:T(1024)}, u32[]{:S(2)}) copy-start(f32[2048]{0:T(1024)} %param.10) | copy-start | bytes 24580
  44.4 18.8 %copy-start.2 = (f32[256]{0:T(256)S(1)}, f32[256]{0:T(256)}, u32[]{:S(2)}) copy-start(f32[256]{0:T(256)} %param.12) | copy-start | bytes 3076
  44.4 6.4 %collective-permute-start.12 = (bf16[128,512]{1,0:T(8,128)(2,1)S(1)}, bf16[128,512]{1,0:T(8,128)(2,1)S(1)}, u32[]{:S(2)}, u32[]{:S(2)}) collective-permute-start(bf16[128,512]{1,0:T(8,128)(2,1)S(1)} %get-tuple-element.79), channel_id=1, source_target_pairs={{0,64},{32,96},{64,0},{96,32},{1,65},{33,97},{65,1},{97,33},{2,66}... | collective-permute-start | bytes 393224 | tf_op jit(solution)/shard_map/other_x/ppermute | solution.py:260
  46.4 8.4 %collective-permute-start.11 = (bf16[128,512]{1,0:T(8,128)(2,1)S(1)}, bf16[128,512]{1,0:T(8,128)(2,1)S(1)}, u32[]{:S(2)}, u32[]{:S(2)}) collective-permute-start(bf16[128,512]{1,0:T(8,128)(2,1)S(1)} %get-tuple-element.80), channel_id=1, source_target_pairs={{0,64},{32,96},{64,0},{96,32},{1,65},{33,97},{65,1},{97,33},{2,66}... | collective-permute-start | bytes 393224 | tf_op jit(solution)/shard_map/other_x/ppermute | solution.py:260
  47.2 9.2 %collective-permute-start.10 = (bf16[128,512]{1,0:T(8,128)(2,1)S(1)}, bf16[128,512]{1,0:T(8,128)(2,1)S(1)}, u32[]{:S(2)}, u32[]{:S(2)}) collective-permute-start(bf16[128,512]{1,0:T(8,128)(2,1)S(1)} %get-tuple-element.81), channel_id=1, source_target_pairs={{0,64},{32,96},{64,0},{96,32},{1,65},{33,97},{65,1},{97,33},{2,66}... | collective-permute-start | bytes 393224 | tf_op jit(solution)/shard_map/other_x/ppermute | solution.py:260
  48.5 12.0 %collective-permute-start.9 = (bf16[128,512]{1,0:T(8,128)(2,1)S(1)}, bf16[128,512]{1,0:T(8,128)(2,1)S(1)}, u32[]{:S(2)}, u32[]{:S(2)}) collective-permute-start(bf16[128,512]{1,0:T(8,128)(2,1)S(1)} %get-tuple-element.82), channel_id=1, source_target_pairs={{0,64},{32,96},{64,0},{96,32},{1,65},{33,97},{65,1},{97,33},{2,66}... | collective-permute-start | bytes 393224 | tf_op jit(solution)/shard_map/other_x/ppermute | solution.py:260
  50.9 12.2 %collective-permute-start.14 = (bf16[128,512]{1,0:T(8,128)(2,1)S(1)}, bf16[128,512]{1,0:T(8,128)(2,1)S(1)}, u32[]{:S(2)}, u32[]{:S(2)}) collective-permute-start(bf16[128,512]{1,0:T(8,128)(2,1)S(1)} %fusion), channel_id=1, source_target_pairs={{0,2},{1,3},{2,0},{3,1},{4,6},{5,7},{6,4},{7,5},{8,10},{9,11},{10,... | collective-permute-start | bytes 393224 | tf_op jit(solution)/shard_map/along_z2/ppermute | solution.py:252
  54.9 8.2 %collective-permute-start.13 = (bf16[128,512]{1,0:T(8,128)(2,1)S(1)}, bf16[128,512]{1,0:T(8,128)(2,1)S(1)}, u32[]{:S(2)}, u32[]{:S(2)}) collective-permute-start(bf16[128,512]{1,0:T(8,128)(2,1)S(1)} %fusion.1), channel_id=1, source_target_pairs={{0,1},{1,2},{2,3},{3,0},{4,5},{5,6},{6,7},{7,4},{8,9},{9,10},{10,1... | collective-permute-start | bytes 393224 | tf_op jit(solution)/shard_map/along_z1/ppermute | solution.py:252
  56.5 6.6 %collective-permute-start.15 = (bf16[128,512]{1,0:T(8,128)(2,1)S(1)}, bf16[128,512]{1,0:T(8,128)(2,1)S(1)}, u32[]{:S(2)}, u32[]{:S(2)}) collective-permute-start(bf16[128,512]{1,0:T(8,128)(2,1)S(1)} %fusion.2), channel_id=1, source_target_pairs={{0,3},{1,0},{2,1},{3,2},{4,7},{5,4},{6,5},{7,6},{8,11},{9,8},{10,9... | collective-permute-start | bytes 393224 | tf_op jit(solution)/shard_map/along_z3/ppermute | solution.py:252
  64.3 6.5 %collective-permute-start.17 = (bf16[128,512]{1,0:T(8,128)(2,1)S(1)}, bf16[128,512]{1,0:T(8,128)(2,1)S(1)}, u32[]{:S(2)}, u32[]{:S(2)}) collective-permute-start(bf16[128,512]{1,0:T(8,128)(2,1)S(1)} %get-tuple-element.51.refs_0_), channel_id=1, source_target_pairs={{0,64},{32,96},{64,0},{96,32},{1,65},{33,97},{65,1},{97,33},{2,66}... | collective-permute-start | bytes 393224 | tf_op jit(solution)/shard_map/other_x/ppermute | solution.py:260
  65.7 7.0 %collective-permute-start.19 = (bf16[128,512]{1,0:T(8,128)(2,1)S(1)}, bf16[128,512]{1,0:T(8,128)(2,1)S(1)}, u32[]{:S(2)}, u32[]{:S(2)}) collective-permute-start(bf16[128,512]{1,0:T(8,128)(2,1)S(1)} %get-tuple-element.56), channel_id=1, source_target_pairs={{0,1},{1,2},{2,3},{3,0},{4,5},{5,6},{6,7},{7,4},{8,9},{9,10},{10,1... | collective-permute-start | bytes 393224 | tf_op jit(solution)/shard_map/along_z1/ppermute | solution.py:252
  66.0 9.1 %collective-permute-start.18 = (bf16[128,512]{1,0:T(8,128)(2,1)S(1)}, bf16[128,512]{1,0:T(8,128)(2,1)S(1)}, u32[]{:S(2)}, u32[]{:S(2)}) collective-permute-start(bf16[128,512]{1,0:T(8,128)(2,1)S(1)} %get-tuple-element.54), channel_id=1, source_target_pairs={{0,2},{1,3},{2,0},{3,1},{4,6},{5,7},{6,4},{7,5},{8,10},{9,11},{10,... | collective-permute-start | bytes 393224 | tf_op jit(solution)/shard_map/along_z2/ppermute | solution.py:252
  70.9 5.0 %collective-permute-start.16 = (bf16[128,512]{1,0:T(8,128)(2,1)S(1)}, bf16[128,512]{1,0:T(8,128)(2,1)S(1)}, u32[]{:S(2)}, u32[]{:S(2)}) collective-permute-start(bf16[128,512]{1,0:T(8,128)(2,1)S(1)} %get-tuple-element.52), channel_id=1, source_target_pairs={{0,3},{1,0},{2,1},{3,2},{4,7},{5,4},{6,5},{7,6},{8,11},{9,8},{10,9... | collective-permute-start | bytes 393224 | tf_op jit(solution)/shard_map/along_z3/ppermute | solution.py:252
  76.4 2.0 %collective-permute-start.20 = (bf16[128,2048]{1,0:T(8,128)(2,1)S(1)}, bf16[128,2048]{1,0:T(8,128)(2,1)S(1)}, u32[]{:S(2)}, u32[]{:S(2)}) collective-permute-start(bf16[128,2048]{1,0:T(8,128)(2,1)S(1)} %get-tuple-element.58), channel_id=1, source_target_pairs={{0,32},{32,0},{64,96},{96,64},{1,33},{33,1},{65,97},{97,65},{2,34}... | collective-permute-start | bytes 1572872 | tf_op jit(solution)/shard_map/other_core/ppermute | solution.py:256
  76.5 11.5 %collective-permute-start.21 = (bf16[384,512]{1,0:T(8,128)(2,1)S(1)}, bf16[384,512]{1,0:T(8,128)(2,1)S(1)}, u32[]{:S(2)}, u32[]{:S(2)}) collective-permute-start(bf16[384,512]{1,0:T(8,128)(2,1)S(1)} %get-tuple-element.59), channel_id=1, source_target_pairs={{0,64},{32,96},{64,0},{96,32},{1,65},{33,97},{65,1},{97,33},{2,66}... | collective-permute-start | bytes 1179656 | tf_op jit(solution)/shard_map/other_x/ppermute | solution.py:260
  80.3 9.7 %collective-permute-start.22 = (bf16[256,512]{1,0:T(8,128)(2,1)S(1)}, bf16[256,512]{1,0:T(8,128)(2,1)S(1)}, u32[]{:S(2)}, u32[]{:S(2)}) collective-permute-start(bf16[256,512]{1,0:T(8,128)(2,1)S(1)} %get-tuple-element.60), channel_id=1, source_target_pairs={{0,4},{4,8},{8,12},{12,0},{16,20},{20,24},{24,28},{28,16},{1,5},{5... | collective-permute-start | bytes 786440 | tf_op jit(solution)/shard_map/along_y1/ppermute | solution.py:248
  80.8 9.3 %collective-permute-start.23 = (bf16[256,512]{1,0:T(8,128)(2,1)S(1)}, bf16[256,512]{1,0:T(8,128)(2,1)S(1)}, u32[]{:S(2)}, u32[]{:S(2)}) collective-permute-start(bf16[256,512]{1,0:T(8,128)(2,1)S(1)} %get-tuple-element.63), channel_id=1, source_target_pairs={{0,12},{4,0},{8,4},{12,8},{16,28},{20,16},{24,20},{28,24},{1,13},{... | collective-permute-start | bytes 786440 | tf_op jit(solution)/shard_map/along_y3/ppermute | solution.py:248
  90.6 4.0 %collective-permute-start.24 = (bf16[128,2048]{1,0:T(8,128)(2,1)S(1)}, bf16[128,2048]{1,0:T(8,128)(2,1)S(1)}, u32[]{:S(2)}, u32[]{:S(2)}) collective-permute-start(bf16[128,2048]{1,0:T(8,128)(2,1)S(1)} %assemble.3), channel_id=1, source_target_pairs={{0,32},{32,0},{64,96},{96,64},{1,33},{33,1},{65,97},{97,65},{2,34}... | collective-permute-start | bytes 1572872 | tf_op jit(solution)/shard_map/other_core/ppermute | solution.py:256
  90.7 13.7 %collective-permute-start.25 = (bf16[256,512]{1,0:T(8,128)(2,1)S(1)}, bf16[256,512]{1,0:T(8,128)(2,1)S(1)}, u32[]{:S(2)}, u32[]{:S(2)}) collective-permute-start(bf16[256,512]{1,0:T(8,128)(2,1)S(1)} %get-tuple-element.62), channel_id=1, source_target_pairs={{0,16},{4,20},{8,24},{12,28},{16,0},{20,4},{24,8},{28,12},{1,17},{... | collective-permute-start | bytes 786440 | tf_op jit(solution)/shard_map/across_x/ppermute | solution.py:244
  93.5 13.8 %collective-permute-start.26 = (bf16[256,512]{1,0:T(8,128)(2,1)S(1)}, bf16[256,512]{1,0:T(8,128)(2,1)S(1)}, u32[]{:S(2)}, u32[]{:S(2)}) collective-permute-start(bf16[256,512]{1,0:T(8,128)(2,1)S(1)} %get-tuple-element.68), channel_id=1, source_target_pairs={{0,4},{4,8},{8,12},{12,0},{16,20},{20,24},{24,28},{28,16},{1,5},{5... | collective-permute-start | bytes 786440 | tf_op jit(solution)/shard_map/along_y1/ppermute | solution.py:248
  94.8 12.9 %collective-permute-start.27 = (bf16[256,512]{1,0:T(8,128)(2,1)S(1)}, bf16[256,512]{1,0:T(8,128)(2,1)S(1)}, u32[]{:S(2)}, u32[]{:S(2)}) collective-permute-start(bf16[256,512]{1,0:T(8,128)(2,1)S(1)} %get-tuple-element.69), channel_id=1, source_target_pairs={{0,12},{4,0},{8,4},{12,8},{16,28},{20,16},{24,20},{28,24},{1,13},{... | collective-permute-start | bytes 786440 | tf_op jit(solution)/shard_map/along_y3/ppermute | solution.py:248
  101.1 16.3 %collective-permute-start.29 = (bf16[512,512]{1,0:T(8,128)(2,1)S(1)}, bf16[512,512]{1,0:T(8,128)(2,1)S(1)}, u32[]{:S(2)}, u32[]{:S(2)}) collective-permute-start(bf16[512,512]{1,0:T(8,128)(2,1)S(1)} %get-tuple-element.66), channel_id=1, source_target_pairs={{0,4},{4,8},{8,12},{12,0},{16,20},{20,24},{24,28},{28,16},{1,5},{5... | collective-permute-start | bytes 1572872 | tf_op jit(solution)/shard_map/along_y1/ppermute | solution.py:248
  101.2 16.2 %collective-permute-start.30 = (bf16[512,512]{1,0:T(8,128)(2,1)S(1)}, bf16[512,512]{1,0:T(8,128)(2,1)S(1)}, u32[]{:S(2)}, u32[]{:S(2)}) collective-permute-start(bf16[512,512]{1,0:T(8,128)(2,1)S(1)} %get-tuple-element.73), channel_id=1, source_target_pairs={{0,12},{4,0},{8,4},{12,8},{16,28},{20,16},{24,20},{28,24},{1,13},{... | collective-permute-start | bytes 1572872 | tf_op jit(solution)/shard_map/along_y3/ppermute | solution.py:248
  104.4 8.8 %collective-permute-start.28 = (bf16[256,512]{1,0:T(8,128)(2,1)S(1)}, bf16[256,512]{1,0:T(8,128)(2,1)S(1)}, u32[]{:S(2)}, u32[]{:S(2)}) collective-permute-start(bf16[256,512]{1,0:T(8,128)(2,1)S(1)} %expand.11), channel_id=1, source_target_pairs={{0,16},{4,20},{8,24},{12,28},{16,0},{20,4},{24,8},{28,12},{1,17},{... | collective-permute-start | bytes 786440 | tf_op jit(solution)/shard_map/across_x/ppermute | solution.py:244
  107.3 14.2 %collective-permute-start.32 = (bf16[256,512]{1,0:T(8,128)(2,1)S(1)}, bf16[256,512]{1,0:T(8,128)(2,1)S(1)}, u32[]{:S(2)}, u32[]{:S(2)}) collective-permute-start(bf16[256,512]{1,0:T(8,128)(2,1)S(1)} %expand.13), channel_id=1, source_target_pairs={{0,4},{4,8},{8,12},{12,0},{16,20},{20,24},{24,28},{28,16},{1,5},{5... | collective-permute-start | bytes 786440 | tf_op jit(solution)/shard_map/along_y1/ppermute | solution.py:248
  114.6 7.0 %collective-permute-start.35 = (bf16[256,512]{1,0:T(8,128)(2,1)S(1)}, bf16[256,512]{1,0:T(8,128)(2,1)S(1)}, u32[]{:S(2)}, u32[]{:S(2)}) collective-permute-start(bf16[256,512]{1,0:T(8,128)(2,1)S(1)} %expand.15), channel_id=1, source_target_pairs={{0,12},{4,0},{8,4},{12,8},{16,28},{20,16},{24,20},{28,24},{1,13},{... | collective-permute-start | bytes 786440 | tf_op jit(solution)/shard_map/along_y3/ppermute | solution.py:248
  115.2 9.8 %collective-permute-start.31 = (bf16[256,512]{1,0:T(8,128)(2,1)S(1)}, bf16[256,512]{1,0:T(8,128)(2,1)S(1)}, u32[]{:S(2)}, u32[]{:S(2)}) collective-permute-start(bf16[256,512]{1,0:T(8,128)(2,1)S(1)} %expand.14), channel_id=1, source_target_pairs={{0,16},{4,20},{8,24},{12,28},{16,0},{20,4},{24,8},{28,12},{1,17},{... | collective-permute-start | bytes 786440 | tf_op jit(solution)/shard_map/across_x/ppermute | solution.py:244
  118.7 11.0 %collective-permute-start.34 = (bf16[256,512]{1,0:T(8,128)(2,1)S(1)}, bf16[256,512]{1,0:T(8,128)(2,1)S(1)}, u32[]{:S(2)}, u32[]{:S(2)}) collective-permute-start(bf16[256,512]{1,0:T(8,128)(2,1)S(1)} %expand.16), channel_id=1, source_target_pairs={{0,16},{4,20},{8,24},{12,28},{16,0},{20,4},{24,8},{28,12},{1,17},{... | collective-permute-start | bytes 786440 | tf_op jit(solution)/shard_map/across_x/ppermute | solution.py:244
  121.5 8.2 %collective-permute-start.33 = (bf16[256,512]{1,0:T(8,128)(2,1)S(1)}, bf16[256,512]{1,0:T(8,128)(2,1)S(1)}, u32[]{:S(2)}, u32[]{:S(2)}) collective-permute-start(bf16[256,512]{1,0:T(8,128)(2,1)S(1)} %collective-permute-done.32), channel_id=1, source_target_pairs={{0,4},{4,8},{8,12},{12,0},{16,20},{20,24},{24,28},{28,16},{1,5},{5... | collective-permute-start | bytes 786440 | tf_op jit(solution)/shard_map/along_y1/ppermute | solution.py:248
  121.6 8.1 %collective-permute-start.36 = (bf16[256,512]{1,0:T(8,128)(2,1)S(1)}, bf16[256,512]{1,0:T(8,128)(2,1)S(1)}, u32[]{:S(2)}, u32[]{:S(2)}) collective-permute-start(bf16[256,512]{1,0:T(8,128)(2,1)S(1)} %collective-permute-done.35), channel_id=1, source_target_pairs={{0,12},{4,0},{8,4},{12,8},{16,28},{20,16},{24,20},{28,24},{1,13},{... | collective-permute-start | bytes 786440 | tf_op jit(solution)/shard_map/along_y3/ppermute | solution.py:248

commit v4 on v3

--- a/solution.py
+++ b/solution.py
@@ -8,6 +8,7 @@
 
 F32, BF16 = jnp.float32, jnp.bfloat16
 COST = pl.CostEstimate(flops=1 << 10, transcendentals=0, bytes_accessed=1 << 10)
+WORK = pl.CostEstimate(flops=1 << 30, transcendentals=0, bytes_accessed=1 << 10)
 PARAMS = pltpu.CompilerParams(vmem_limit_bytes=4 << 20)
 VMEM = pl.BlockSpec(memory_space=pltpu.VMEM)
 SMEM = pl.BlockSpec(memory_space=pltpu.SMEM)
@@ -24,50 +25,58 @@
     return pl.ds(pl.multiple_of(at_ref[i] * ns, ns), ns)
 
 
-def project_kernel(which, final, has_total, at_ref, *refs):
+def project_kernel(which, at_ref, *refs):
     n = len(which)
-    blocks, table, rest = refs[:n], refs[n], refs[n + 1 :]
-    m, ns = blocks[0].shape
-    width = table.shape[1]
-    tile = width // 4
+    blocks, table, total, out = refs[:n], refs[n], refs[n + 1], refs[n + 2]
+    ns = blocks[0].shape[1]
+    tile = table.shape[1] // 4
     for j in range(4):
-        if final:
-            from_lane = pl.multiple_of(((at_ref[8] + j) & 3) * tile, tile)
-        else:
-            from_lane = j * tile
-        lanes = pl.ds(from_lane, tile)
-        total = rest[0][:, lanes] if has_total else None
+        lanes = slice(j * tile, (j + 1) * tile)
+        value = total[:, lanes]
         for i, a in zip(which, blocks):
-            term = jnp.dot(a[...], table[rows_at(at_ref, i, ns), lanes], preferred_element_type=F32)
-            total = term if total is None else total + term
-        to = slice(j * tile, (j + 1) * tile)
-        if final:
-            rest[-2][:, to] = total[: m // 2].astype(BF16)
-            rest[-1][:, to] = total[m // 2 :]
-        else:
-            rest[-1][:, to] = total
-
-
-def project(blocks, which, at, table, total=None, final=False):
-    m, width = blocks[0].shape[0], table.shape[1]
-    args = [at, *blocks, table] + ([] if total is None else [total])
-    if final:
-        out_shape = [
-            jax.ShapeDtypeStruct((m // 2, width), BF16),
-            jax.ShapeDtypeStruct((m // 2, width), F32),
-        ]
-    else:
-        out_shape = jax.ShapeDtypeStruct((m, width), F32)
-    return pl.pallas_call(
-        functools.partial(project_kernel, which, final, total is not None),
+            value = value + jnp.dot(
+                a[...], table[rows_at(at_ref, i, ns), lanes], preferred_element_type=F32
+            )
+        out[:, lanes] = value
+
+
+def project(blocks, which, at, table, total):
+    args = [at, *blocks, table, total]
+    return pl.pallas_call(
+        functools.partial(project_kernel, which),
         in_specs=[SMEM] + [VMEM] * (len(args) - 1),
-        out_specs=[VMEM, VMEM] if final else VMEM,
-        out_shape=out_shape,
-        input_output_aliases={} if final or total is None else {len(args) - 1: 0},
+        out_specs=VMEM,
+        out_shape=jax.ShapeDtypeStruct(total.shape, F32),
+        input_output_aliases={len(args) - 1: 0},
         cost_estimate=COST,
         compiler_params=PARAMS,
         name="project",
     )(*args)
+
+
+def last_kernel(i, start, at_ref, a_ref, table, total, out):
+    m, ns = out.shape[0], a_ref.shape[1]
+    rows = slice(start, start + m)
+    tile = table.shape[1] // 4
+    for j in range(4):
+        lanes = pl.ds(pl.multiple_of(((at_ref[8] + j) & 3) * tile, tile), tile)
+        value = total[rows, lanes] + jnp.dot(
+            a_ref[rows, :], table[rows_at(at_ref, i, ns), lanes], preferred_element_type=F32
+        )
+        out[:, j * tile : (j + 1) * tile] = value.astype(out.dtype)
+
+
+def project_last(a, i, at, table, total, start, dtype):
+    m, width = total.shape
+    return pl.pallas_call(
+        functools.partial(last_kernel, i, start),
+        in_specs=[SMEM] + [VMEM] * 3,
+        out_specs=VMEM,
+        out_shape=jax.ShapeDtypeStruct((m // 2, width), dtype),
+        cost_estimate=COST,
+        compiler_params=PARAMS,
+        name="project_last",
+    )(at, a, table, total)
 
 
 def first_kernel(at_ref, a_ref, basis_ref, table, total, sems):
@@ -103,7 +112,9 @@
 def expand_kernel(which, ns, n, adds, at_ref, *refs):
     fields, table, refs = refs[:n], refs[n], refs[n + 1 :]
     m = fields[0].shape[0]
-    for group, out in zip(which, refs[n * adds :]):
+    adds = adds or (0,) * n
+    lower = which == [[OWN]]
+    for group, out in zip(which, refs[sum(adds) :]):
         row = 0
         for i in group:
             for h, a in enumerate(fields):
@@ -113,21 +124,22 @@
                     (((1,), (1,)), ((), ())),
                     preferred_element_type=F32,
                 )
-                for add in refs[h * adds : (h + 1) * adds]:
-                    value = value + add[:m, :].astype(F32)
+                for add in refs[sum(adds[:h]) : sum(adds[: h + 1])]:
+                    part = add[-m:, :] if lower else add[:m, :]
+                    value = value + part.astype(F32)
                 out[row : row + m, :] = value.astype(out.dtype)
                 row += m
 
 
-def expand(fields, which, at, table, ns, adds=(), dtype=BF16):
+def expand(fields, which, at, table, ns, adds=(), dtype=BF16, cost=COST):
     rows = sum(a.shape[0] for a in fields)
     flat = [a for group in adds for a in group]
     out = pl.pallas_call(
-        functools.partial(expand_kernel, which, ns, len(fields), len(flat) // len(fields)),
+        functools.partial(expand_kernel, which, ns, len(fields), tuple(len(group) for group in adds)),
         in_specs=[SMEM] + [VMEM] * (len(fields) + 1 + len(flat)),
         out_specs=[VMEM] * len(which),
         out_shape=[jax.ShapeDtypeStruct((rows * len(group), ns), dtype) for group in which],
-        cost_estimate=COST,
+        cost_estimate=cost,
         compiler_params=PARAMS,
         name="expand",
     )(at, *fields, table, *flat)
@@ -205,21 +217,20 @@
     return out if n == 4 else out[0]
 
 
-def finish_kernel(rows, at_ref, total, *refs):
-    g, adds, out = at_ref[9], refs[:-1], refs[-1]
-    n = len(adds) // 2
+def finish_kernel(rows, n, at_ref, total, *refs):
+    g, out = at_ref[9], refs[-1]
+    adds = refs[:n], refs[n:-1]
     for k in range(4):
         value = total[k * rows : (k + 1) * rows, :]
-        for a in adds[n * (k // 2) : n * (k // 2 + 1)]:
-            start = a.shape[0] - 2 * rows + (k % 2) * rows
-            value = value + a[start : start + rows, :].astype(F32)
+        for a in adds[k // 2]:
+            value = value + a[k % 2 * rows : (k % 2 + 1) * rows, :].astype(F32)
         out[pl.ds(pl.multiple_of((g ^ k) * rows, rows), rows), :] = value
 
 
 def finish(total, at, adds):
     flat = [*adds[0], *adds[1]]
     return pl.pallas_call(
-        functools.partial(finish_kernel, total.shape[0] // 4),
+        functools.partial(finish_kernel, total.shape[0] // 4, len(adds[0])),
         in_specs=[SMEM] + [VMEM] * (1 + len(flat)),
         out_specs=VMEM,
         out_shape=jax.ShapeDtypeStruct(total.shape, F32),
@@ -281,7 +292,8 @@
     total = project([up, down], [UP, DOWN], at, table, total)
     total = project([x_own, far], [X_OWN, FAR], at, table, total)
     total = project([x_up, x_down], [X_UP, X_DOWN], at, table, total)
-    give, keep = project([x_far], [X_FAR], at, table, total, final=True)
+    give = project_last(x_far, X_FAR, at, table, total, 0, BF16)
+    keep = project_last(after(x_far, give), X_FAR, at, table, total, rows // 2, F32)
 
     both = keep + other_core(give).astype(F32)
     half = pair * nt
@@ -310,14 +322,14 @@
     x_rest = other_x(rest)
     near = jnp.concatenate([mine, other_core(mine)], 0)
 
-    def send(a, *which):
-        return expand([a], which, at, table, ns)
+    def send(a, *which, cost=COST):
+        return expand([a], which, at, table, ns, cost=cost)
 
     def both_ways(pair):
         return along_y(pair[0], 1), along_y(pair[1], -1)
 
-    s_near = send(near, [X_UP], [X_DOWN])
-    *o_near, f_near = send(after(near, s_near[0]), [UP], [DOWN], [X_FAR])
+    s_near = send(near, [X_UP], [X_DOWN], cost=WORK)
+    *o_near, f_near = send(after(near, s_near[0]), [UP], [DOWN], [X_FAR], cost=WORK)
     sent = f_near
     s_near, o_near, f_near = both_ways(s_near), both_ways(o_near), across_x(f_near)
     from_x = assemble([x_first, after(x_rest, sent, *s_near)], at)
@@ -340,9 +352,10 @@
     x_away = across_x(x_away)
     f_near = along_y(after(f_near, sent), 1)
     f_away = along_y(after(f_away, sent), -1)
-    fields = [after(near, sent, x_near), away]
-    out = expand(fields, [[OWN]], at, table, ns, (), F32)
-    adds = (*o_near, x_near, f_near), (*s_away, x_away, f_away)
+    fields = [after(near, sent), away]
+    early = (*o_near, x_near), s_away
+    out = expand(fields, [[OWN]], at, table, ns, early, F32)
+    adds = (f_near,), (x_away, f_away)
     return finish(out, at, adds).reshape(rhs, nt, ns)
 
 

time: 132 us -> 131 us (level)
    pallas_call x14 -> x15, Pallas kernels: 28.4 us -> 29 us  [the longest x9 15.4 us: expand(): pl.pallas_call(functools.partial(expand_kernel, which, ns, len(fields), t...]
  transfers between devices with their start and end apart: 37 -> 37, of which waited for: 16 -> 16; matrix products, arithmetic and copies ran while one was open for 0% -> 0% of each run, Pallas kernels for 24% -> 25%
where the time goes in v4:
time: 131 us
  starting transfers between devices  57.9 us (44%)
  Pallas kernels  38.3 us (29%)
  waiting for transfers between devices  31.5 us (24%)
  local copies, waits for them, and re-layouts  1.36 us (1%)
    ppermute x16, starting transfers between devices, along_y(): return lax.ppermute(a, 'col', [(c, c & 4 | c + k & 3) for c in range(8)])  22.5 us
    pallas_call x9, Pallas kernels, expand(): pl.pallas_call(functools.partial(expand_kernel, which, ns, len(fields), t...  15.4 us
    ppermute x6, starting transfers between devices, along_z(): return lax.ppermute(a, 'tm', [(z, z + k & 3) for z in range(4)])  14.4 us
    ppermute x6, starting transfers between devices, across_x(): return lax.ppermute(a, 'col', [(c, c ^ 4) for c in range(8)])  14.3 us
    ppermute x16, waiting for transfers between devices, along_y(): return lax.ppermute(a, 'col', [(c, c & 4 | c + k & 3) for c in range(8)])  12.8 us
    pallas_call x3, Pallas kernels, project(): pl.pallas_call(functools.partial(project_kernel, which), in_specs=[SMEM]...  9.41 us
    ppermute x6, waiting for transfers between devices, along_z(): return lax.ppermute(a, 'tm', [(z, z + k & 3) for z in range(4)])  7.45 us
    pallas_call x1, Pallas kernels, project_first(): pl.pallas_call(first_kernel, in_specs=[SMEM, VMEM, pl.BlockSpec(memory_sp...  6.92 us
  transfers between devices with their start and end apart: 37, of which 16 were waited for; matrix products, arithmetic and copies ran while one was open for 0% of the time, Pallas kernels for 25%

profile of v4, /device:TPU:0, one launch (start us, length us, event | category | flops | bytes accessed | tf_op | source)
XLA Modules:
  0.0 130.8 jit_solution(4908042989271267680)
XLA Ops:
  1.2 1.7 %collective-permute-start = (bf16[512,512]{1,0:T(8,128)(2,1)S(1)}, bf16[512,512]{1,0:T(8,128)(2,1)S(1)}, u32[]{:S(2)}, u32[]{:S(2)}) collective-permute-start(bf16[512,512]{1,0:T(8,128)(2,1)S(1)} %bitcast.6), channel_id=1, source_target_pairs={{0,4},{4,8},{8,12},{12,0},{16,20},{20,24},{24,28},{28,16},{1,5},{5... | collective-permute-start | bytes 1572872 | tf_op jit(solution)/shard_map/along_y1/ppermute | solution.py:259
  3.0 1.6 %collective-permute-start.2 = (bf16[512,512]{1,0:T(8,128)(2,1)S(1)}, bf16[512,512]{1,0:T(8,128)(2,1)S(1)}, u32[]{:S(2)}, u32[]{:S(2)}) collective-permute-start(bf16[512,512]{1,0:T(8,128)(2,1)S(1)} %bitcast.7), channel_id=1, source_target_pairs={{0,12},{4,0},{8,4},{12,8},{16,28},{20,16},{24,20},{28,24},{1,13},{... | collective-permute-start | bytes 1572872 | tf_op jit(solution)/shard_map/along_y3/ppermute | solution.py:259
  4.5 3.1 %collective-permute-start.5 = (bf16[512,512]{1,0:T(8,128)(2,1)S(1)}, bf16[512,512]{1,0:T(8,128)(2,1)S(1)}, u32[]{:S(2)}, u32[]{:S(2)}) collective-permute-start(bf16[512,512]{1,0:T(8,128)(2,1)S(1)} %bitcast.8), channel_id=1, source_target_pairs={{0,16},{4,20},{8,24},{12,28},{16,0},{20,4},{24,8},{28,12},{1,17},{... | collective-permute-start | bytes 1572872 | tf_op jit(solution)/shard_map/across_x/ppermute | solution.py:255
  7.7 6.9 %project_first.1 = (bf16[4096,2048]{1,0:T(8,128)(2,1)S(1)}, f32[512,2048]{1,0:T(8,128)S(1)}) custom-call(s32[10]{0:T(128)S(1)} %pad_add_fusion.at_ref, bf16[512,512]{1,0:T(8,128)(2,1)S(1)} %bitcast.9, bf16[4096,2048]{1,0:T(8,128)(2,1)} %basis_ref.1), custom_call_target="tpu_custom_call" | custom-call | flops 1024 | bytes 1024 | tf_op jit(solution)/shard_map/project_first/pallas_call | solution.py:97
  14.7 1.7 %collective-permute-done.refs_1_ = bf16[512,512]{1,0:T(8,128)(2,1)S(1)} collective-permute-done((bf16[512,512]{1,0:T(8,128)(2,1)S(1)}, bf16[512,512]{1,0:T(8,128)(2,1)S(1)}, u32[]{:S(2)}, u32[]{:S(2)}) %collective-permute-start) | collective-permute-done | bytes 524320 | tf_op jit(solution)/shard_map/along_y1/ppermute | solution.py:259
  16.7 3.0 %collective-permute-start.3 = (bf16[256,512]{1,0:T(8,128)(2,1)S(1)}, bf16[256,512]{1,0:T(8,128)(2,1)S(1)}, u32[]{:S(2)}, u32[]{:S(2)}) collective-permute-start(bf16[256,512]{1,0:T(8,128)(2,1)S(1)} %slice.45), channel_id=1, source_target_pairs={{0,12},{4,0},{8,4},{12,8},{16,28},{20,16},{24,20},{28,24},{1,13},{... | collective-permute-start | bytes 786440 | tf_op jit(solution)/shard_map/along_y3/ppermute | solution.py:259
  19.8 1.3 collective-permute-start.6
  21.8 5.1 %collective-permute-done.1 = bf16[256,512]{1,0:T(8,128)(2,1)S(1)} collective-permute-done((bf16[256,512]{1,0:T(8,128)(2,1)S(1)}, bf16[256,512]{1,0:T(8,128)(2,1)S(1)}, u32[]{:S(2)}, u32[]{:S(2)}) %collective-permute-start.1) | collective-permute-done | bytes 262176 | tf_op jit(solution)/shard_map/along_y1/ppermute | solution.py:259
  26.9 3.0 %collective-permute-start.4 = (bf16[512,512]{1,0:T(8,128)(2,1)S(1)}, bf16[512,512]{1,0:T(8,128)(2,1)S(1)}, u32[]{:S(2)}, u32[]{:S(2)}) collective-permute-start(bf16[512,512]{1,0:T(8,128)(2,1)S(1)} %constant_dynamic-update-slice_fusion.refs_1_), channel_id=1, source_target_pairs={{0,16},{4,20},{8,24},{12,28},{16,0},{20,4},{24,8},{28,12},{1,17},{... | collective-permute-start | bytes 1572872 | tf_op jit(solution)/shard_map/across_x/ppermute | solution.py:255
  29.9 3.2 %project.3.refs_3_ = f32[512,2048]{1,0:T(8,128)S(1)} custom-call(s32[10]{0:T(128)S(1)} %pad_add_fusion.at_ref, bf16[512,512]{1,0:T(8,128)(2,1)S(1)} %collective-permute-done.2.refs_0_, bf16[512,512]{1,0:T(8,128)(2,1)S(1)} %collective-permute-done.refs_1_, ...), custom_call_target="tpu_custom_call", output_to_operand_aliasing={{}: (4, {})} | custom-call | flops 1024 | bytes 1024 | tf_op jit(solution)/shard_map/project/pallas_call | solution.py:45
  33.1 3.2 %project.4.refs_3_ = f32[512,2048]{1,0:T(8,128)S(1)} custom-call(s32[10]{0:T(128)S(1)} %pad_add_fusion.at_ref, bf16[512,512]{1,0:T(8,128)(2,1)S(1)} %collective-permute-done.5.refs_0_, bf16[512,512]{1,0:T(8,128)(2,1)S(1)} %constant_dynamic-update-slice_fusion.refs_1_, ...), custom_call_target="tpu_custom_call", output_to_operand_aliasing={{}: (4, {})} | custom-call | flops 1024 | bytes 1024 | tf_op jit(solution)/shard_map/project/pallas_call | solution.py:45
  36.3 3.1 %project.5.total = f32[512,2048]{1,0:T(8,128)S(1)} custom-call(s32[10]{0:T(128)S(1)} %pad_add_fusion.at_ref, bf16[512,512]{1,0:T(8,128)(2,1)S(1)} %collective-permute-done.6.refs_0_, bf16[512,512]{1,0:T(8,128)(2,1)S(1)} %collective-permute-done.7.refs_1_, ...), custom_call_target="tpu_custom_call", output_to_operand_aliasing={{}: (4, {})} | custom-call | flops 1024 | bytes 1024 | tf_op jit(solution)/shard_map/project/pallas_call | solution.py:45
  39.4 1.3 project_last.2
  40.8 1.3 project_last.3
  42.0 1.4 %collective-permute-done.8 = bf16[256,2048]{1,0:T(8,128)(2,1)S(1)} collective-permute-done((bf16[256,2048]{1,0:T(8,128)(2,1)S(1)}, bf16[256,2048]{1,0:T(8,128)(2,1)S(1)}, u32[]{:S(2)}, u32[]{:S(2)}) %collective-permute-start.8) | collective-permute-done | bytes 1048608 | tf_op jit(solution)/shard_map/other_core/ppermute | solution.py:267
  43.9 1.4 %collective-permute-start.12 = (bf16[128,512]{1,0:T(8,128)(2,1)S(1)}, bf16[128,512]{1,0:T(8,128)(2,1)S(1)}, u32[]{:S(2)}, u32[]{:S(2)}) collective-permute-start(bf16[128,512]{1,0:T(8,128)(2,1)S(1)} %get-tuple-element.77), channel_id=1, source_target_pairs={{0,64},{32,96},{64,0},{96,32},{1,65},{33,97},{65,1},{97,33},{2,66}... | collective-permute-start | bytes 393224 | tf_op jit(solution)/shard_map/other_x/ppermute | solution.py:271
  46.7 1.3 collective-permute-start.10
  48.8 1.6 %collective-permute-done.12 = bf16[128,512]{1,0:T(8,128)(2,1)S(1)} collective-permute-done((bf16[128,512]{1,0:T(8,128)(2,1)S(1)}, bf16[128,512]{1,0:T(8,128)(2,1)S(1)}, u32[]{:S(2)}, u32[]{:S(2)}) %collective-permute-start.12) | collective-permute-done | bytes 131104 | tf_op jit(solution)/shard_map/other_x/ppermute | solution.py:271
  50.4 4.1 %collective-permute-start.14 = (bf16[128,512]{1,0:T(8,128)(2,1)S(1)}, bf16[128,512]{1,0:T(8,128)(2,1)S(1)}, u32[]{:S(2)}, u32[]{:S(2)}) collective-permute-start(bf16[128,512]{1,0:T(8,128)(2,1)S(1)} %fusion), channel_id=1, source_target_pairs={{0,2},{1,3},{2,0},{3,1},{4,6},{5,7},{6,4},{7,5},{8,10},{9,11},{10,... | collective-permute-start | bytes 393224 | tf_op jit(solution)/shard_map/along_z2/ppermute | solution.py:263
  56.0 4.1 %collective-permute-start.15 = (bf16[128,512]{1,0:T(8,128)(2,1)S(1)}, bf16[128,512]{1,0:T(8,128)(2,1)S(1)}, u32[]{:S(2)}, u32[]{:S(2)}) collective-permute-start(bf16[128,512]{1,0:T(8,128)(2,1)S(1)} %fusion.2), channel_id=1, source_target_pairs={{0,3},{1,0},{2,1},{3,2},{4,7},{5,4},{6,5},{7,6},{8,11},{9,8},{10,9... | collective-permute-start | bytes 393224 | tf_op jit(solution)/shard_map/along_z3/ppermute | solution.py:263
  60.1 2.5 %collective-permute-done.15.refs_3_ = bf16[128,512]{1,0:T(8,128)(2,1)S(1)} collective-permute-done((bf16[128,512]{1,0:T(8,128)(2,1)S(1)}, bf16[128,512]{1,0:T(8,128)(2,1)S(1)}, u32[]{:S(2)}, u32[]{:S(2)}) %collective-permute-start.15) | collective-permute-done | bytes 131104 | tf_op jit(solution)/shard_map/along_z3/ppermute | solution.py:263
  63.8 1.4 %collective-permute-start.17 = (bf16[128,512]{1,0:T(8,128)(2,1)S(1)}, bf16[128,512]{1,0:T(8,128)(2,1)S(1)}, u32[]{:S(2)}, u32[]{:S(2)}) collective-permute-start(bf16[128,512]{1,0:T(8,128)(2,1)S(1)} %get-tuple-element.49.refs_0_), channel_id=1, source_target_pairs={{0,64},{32,96},{64,0},{96,32},{1,65},{33,97},{65,1},{97,33},{2,66}... | collective-permute-start | bytes 393224 | tf_op jit(solution)/shard_map/other_x/ppermute | solution.py:271
  65.5 4.8 %collective-permute-start.18 = (bf16[128,512]{1,0:T(8,128)(2,1)S(1)}, bf16[128,512]{1,0:T(8,128)(2,1)S(1)}, u32[]{:S(2)}, u32[]{:S(2)}) collective-permute-start(bf16[128,512]{1,0:T(8,128)(2,1)S(1)} %get-tuple-element.52), channel_id=1, source_target_pairs={{0,2},{1,3},{2,0},{3,1},{4,6},{5,7},{6,4},{7,5},{8,10},{9,11},{10,... | collective-permute-start | bytes 393224 | tf_op jit(solution)/shard_map/along_z2/ppermute | solution.py:263
  70.4 1.8 %collective-permute-done.19.refs_3_ = bf16[128,512]{1,0:T(8,128)(2,1)S(1)} collective-permute-done((bf16[128,512]{1,0:T(8,128)(2,1)S(1)}, bf16[128,512]{1,0:T(8,128)(2,1)S(1)}, u32[]{:S(2)}, u32[]{:S(2)}) %collective-permute-start.19) | collective-permute-done | bytes 131104 | tf_op jit(solution)/shard_map/along_z1/ppermute | solution.py:263
  72.2 2.5 %collective-permute-done.18.refs_2_ = bf16[128,512]{1,0:T(8,128)(2,1)S(1)} collective-permute-done((bf16[128,512]{1,0:T(8,128)(2,1)S(1)}, bf16[128,512]{1,0:T(8,128)(2,1)S(1)}, u32[]{:S(2)}, u32[]{:S(2)}) %collective-permute-start.18) | collective-permute-done | bytes 131104 | tf_op jit(solution)/shard_map/along_z2/ppermute | solution.py:263
  78.0 1.8 %expand.9 = (bf16[256,512]{1,0:T(8,128)(2,1)S(1)}, bf16[256,512]{1,0:T(8,128)(2,1)S(1)}) custom-call(s32[10]{0:T(128)S(1)} %pad_add_fusion.at_ref, bf16[256,2048]{1,0:T(8,128)(2,1)S(1)} %constant_dynamic-update-slice_fusion.2.refs_0_, bf16[4096,2048]{1,0:T(8,128)(2,1)S(1)} %get-tuple-element.43.refs_2_.table.refs_1_), custom_call_target="tpu_custom_call" | custom-call | flops 1073741824 | bytes 1024 | tf_op jit(solution)/shard_map/expand/pallas_call | solution.py:137
  80.3 2.8 %collective-permute-start.23 = (bf16[256,512]{1,0:T(8,128)(2,1)S(1)}, bf16[256,512]{1,0:T(8,128)(2,1)S(1)}, u32[]{:S(2)}, u32[]{:S(2)}) collective-permute-start(bf16[256,512]{1,0:T(8,128)(2,1)S(1)} %get-tuple-element.61), channel_id=1, source_target_pairs={{0,12},{4,0},{8,4},{12,8},{16,28},{20,16},{24,20},{28,24},{1,13},{... | collective-permute-start | bytes 786440 | tf_op jit(solution)/shard_map/along_y3/ppermute | solution.py:259
  83.1 2.4 %expand.10 = (bf16[256,512]{1,0:T(8,128)(2,1)S(1)}, bf16[256,512]{1,0:T(8,128)(2,1)S(1)}, bf16[256,512]{1,0:T(8,128)(2,1)S(1)}) custom-call(s32[10]{0:T(128)S(1)} %pad_add_fusion.at_ref, bf16[256,2048]{1,0:T(8,128)(2,1)S(1)} %constant_dynamic-update-slice_fusion.2.refs_0_, bf16[4096,2048]{1,0:T(8,128)(2,1)S(1)} %get-tuple-element.43.refs_2_.table.refs_1_), custom_call_target="tpu_custom_call" | custom-call | flops 1073741824 | bytes 1024 | tf_op jit(solution)/shard_map/expand/pallas_call | solution.py:137
  85.5 2.1 %collective-permute-done.21.refs_1_ = bf16[384,512]{1,0:T(8,128)(2,1)S(1)} collective-permute-done((bf16[384,512]{1,0:T(8,128)(2,1)S(1)}, bf16[384,512]{1,0:T(8,128)(2,1)S(1)}, u32[]{:S(2)}, u32[]{:S(2)}) %collective-permute-start.21) | collective-permute-done | bytes 393248 | tf_op jit(solution)/shard_map/other_x/ppermute | solution.py:271
  87.6 2.0 %collective-permute-done.22.refs_2_ = bf16[256,512]{1,0:T(8,128)(2,1)S(1)} collective-permute-done((bf16[256,512]{1,0:T(8,128)(2,1)S(1)}, bf16[256,512]{1,0:T(8,128)(2,1)S(1)}, u32[]{:S(2)}, u32[]{:S(2)}) %collective-permute-start.22) | collective-permute-done | bytes 262176 | tf_op jit(solution)/shard_map/along_y1/ppermute | solution.py:259
  90.2 2.8 %collective-permute-start.25 = (bf16[256,512]{1,0:T(8,128)(2,1)S(1)}, bf16[256,512]{1,0:T(8,128)(2,1)S(1)}, u32[]{:S(2)}, u32[]{:S(2)}) collective-permute-start(bf16[256,512]{1,0:T(8,128)(2,1)S(1)} %get-tuple-element.60), channel_id=1, source_target_pairs={{0,16},{4,20},{8,24},{12,28},{16,0},{20,4},{24,8},{28,12},{1,17},{... | collective-permute-start | bytes 786440 | tf_op jit(solution)/shard_map/across_x/ppermute | solution.py:255
  94.3 2.2 %collective-permute-start.27 = (bf16[256,512]{1,0:T(8,128)(2,1)S(1)}, bf16[256,512]{1,0:T(8,128)(2,1)S(1)}, u32[]{:S(2)}, u32[]{:S(2)}) collective-permute-start(bf16[256,512]{1,0:T(8,128)(2,1)S(1)} %get-tuple-element.67), channel_id=1, source_target_pairs={{0,12},{4,0},{8,4},{12,8},{16,28},{20,16},{24,20},{28,24},{1,13},{... | collective-permute-start | bytes 786440 | tf_op jit(solution)/shard_map/along_y3/ppermute | solution.py:259
  96.4 1.3 expand.11
  97.7 2.9 %expand.12 = (bf16[512,512]{1,0:T(8,128)(2,1)S(1)}, bf16[512,512]{1,0:T(8,128)(2,1)S(1)}) custom-call(s32[10]{0:T(128)S(1)} %pad_add_fusion.at_ref, bf16[256,2048]{1,0:T(8,128)(2,1)S(1)} %pad_maximum_fusion.refs_0_.refs_1_, bf16[4096,2048]{1,0:T(8,128)(2,1)S(1)} %get-tuple-element.43.refs_2_.table.refs_1_), custom_call_target="tpu_custom_call" | custom-call | flops 1024 | bytes 1024 | tf_op jit(solution)/shard_map/expand/pallas_call | solution.py:137
  100.7 3.2 %collective-permute-start.30 = (bf16[512,512]{1,0:T(8,128)(2,1)S(1)}, bf16[512,512]{1,0:T(8,128)(2,1)S(1)}, u32[]{:S(2)}, u32[]{:S(2)}) collective-permute-start(bf16[512,512]{1,0:T(8,128)(2,1)S(1)} %get-tuple-element.71), channel_id=1, source_target_pairs={{0,12},{4,0},{8,4},{12,8},{16,28},{20,16},{24,20},{28,24},{1,13},{... | collective-permute-start | bytes 1572872 | tf_op jit(solution)/shard_map/along_y3/ppermute | solution.py:259
  103.9 1.6 %collective-permute-start.28 = (bf16[256,512]{1,0:T(8,128)(2,1)S(1)}, bf16[256,512]{1,0:T(8,128)(2,1)S(1)}, u32[]{:S(2)}, u32[]{:S(2)}) collective-permute-start(bf16[256,512]{1,0:T(8,128)(2,1)S(1)} %expand.11), channel_id=1, source_target_pairs={{0,16},{4,20},{8,24},{12,28},{16,0},{20,4},{24,8},{28,12},{1,17},{... | collective-permute-start | bytes 786440 | tf_op jit(solution)/shard_map/across_x/ppermute | solution.py:255
  105.5 1.3 expand.13
  106.9 1.3 expand.14
  108.2 4.5 %collective-permute-done.28.refs_2_ = bf16[256,512]{1,0:T(8,128)(2,1)S(1)} collective-permute-done((bf16[256,512]{1,0:T(8,128)(2,1)S(1)}, bf16[256,512]{1,0:T(8,128)(2,1)S(1)}, u32[]{:S(2)}, u32[]{:S(2)}) %collective-permute-start.28) | collective-permute-done | bytes 262176 | tf_op jit(solution)/shard_map/across_x/ppermute | solution.py:255
  112.8 1.3 expand.15
  114.7 2.3 %collective-permute-start.31 = (bf16[256,512]{1,0:T(8,128)(2,1)S(1)}, bf16[256,512]{1,0:T(8,128)(2,1)S(1)}, u32[]{:S(2)}, u32[]{:S(2)}) collective-permute-start(bf16[256,512]{1,0:T(8,128)(2,1)S(1)} %expand.14), channel_id=1, source_target_pairs={{0,16},{4,20},{8,24},{12,28},{16,0},{20,4},{24,8},{28,12},{1,17},{... | collective-permute-start | bytes 786440 | tf_op jit(solution)/shard_map/across_x/ppermute | solution.py:255
  116.9 1.3 expand.16
  118.2 1.5 %collective-permute-start.34 = (bf16[256,512]{1,0:T(8,128)(2,1)S(1)}, bf16[256,512]{1,0:T(8,128)(2,1)S(1)}, u32[]{:S(2)}, u32[]{:S(2)}) collective-permute-start(bf16[256,512]{1,0:T(8,128)(2,1)S(1)} %expand.16), channel_id=1, source_target_pairs={{0,16},{4,20},{8,24},{12,28},{16,0},{20,4},{24,8},{28,12},{1,17},{... | collective-permute-start | bytes 786440 | tf_op jit(solution)/shard_map/across_x/ppermute | solution.py:255
  119.7 1.3 %collective-permute-done.32 = bf16[256,512]{1,0:T(8,128)(2,1)S(1)} collective-permute-done((bf16[256,512]{1,0:T(8,128)(2,1)S(1)}, bf16[256,512]{1,0:T(8,128)(2,1)S(1)}, u32[]{:S(2)}, u32[]{:S(2)}) %collective-permute-start.32) | collective-permute-done | bytes 262176 | tf_op jit(solution)/shard_map/along_y1/ppermute | solution.py:259
  121.1 3.2 %collective-permute-start.36 = (bf16[256,512]{1,0:T(8,128)(2,1)S(1)}, bf16[256,512]{1,0:T(8,128)(2,1)S(1)}, u32[]{:S(2)}, u32[]{:S(2)}) collective-permute-start(bf16[256,512]{1,0:T(8,128)(2,1)S(1)} %collective-permute-done.35), channel_id=1, source_target_pairs={{0,12},{4,0},{8,4},{12,8},{16,28},{20,16},{24,20},{28,24},{1,13},{... | collective-permute-start | bytes 786440 | tf_op jit(solution)/shard_map/along_y3/ppermute | solution.py:259
  124.5 1.9 %expand.17.total = f32[512,512]{1,0:T(8,128)S(1)} custom-call(s32[10]{0:T(128)S(1)} %pad_add_fusion.at_ref, bf16[256,2048]{1,0:T(8,128)(2,1)S(1)} %constant_dynamic-update-slice_fusion.2.refs_0_, bf16[256,2048]{1,0:T(8,128)(2,1)S(1)} %pad_maximum_fusion.refs_0_.refs_1_, bf16[4096,2048]{1,0:T(8,128)(2,1)S(1)} %get-tuple-element.43.refs_2_.table.refs_1_, ...), custom_call_target="tpu_custom_call" | custom-call | flops 1024 | bytes 1024 | tf_op jit(solution)/shard_map/expand/pallas_call | solution.py:137
  126.4 2.8 %collective-permute-done.33.refs_0_ = bf16[256,512]{1,0:T(8,128)(2,1)S(1)} collective-permute-done((bf16[256,512]{1,0:T(8,128)(2,1)S(1)}, bf16[256,512]{1,0:T(8,128)(2,1)S(1)}, u32[]{:S(2)}, u32[]{:S(2)}) %collective-permute-start.33) | collective-permute-done | bytes 262176 | tf_op jit(solution)/shard_map/along_y1/ppermute | solution.py:259
  129.2 1.6 %finish.1 = f32[512,512]{1,0:T(8,128)} custom-call(s32[10]{0:T(128)S(1)} %pad_add_fusion.at_ref, f32[512,512]{1,0:T(8,128)S(1)} %expand.17.total, bf16[256,512]{1,0:T(8,128)(2,1)S(1)} %collective-permute-done.33.refs_0_, bf16[256,512]{1,0:T(8,128)(2,1)S(1)} %collective-permute-done.34.refs_1_, bf16[256,512]{1,0:T(8,128)(2,1)S(1)} %collective-permute-done.36.refs_2_), custom_call_target="tpu_custom_call" | custom-call | flops 1024 | bytes 1024 | tf_op jit(solution)/shard_map/finish/pallas_call | solution.py:232
  (72 shorter events, 14.4 us)
Async XLA Ops:
  0.0 7.7 %copy-start.3 = (s32[8]{0:T(128)S(1)}, s32[8]{0:T(128)}, u32[]{:S(2)}) copy-start(s32[8]{0:T(128)} %constant.30.clone) | copy-start | bytes 100
  0.0 7.7 %copy-start.4 = (s32[8]{0:T(128)S(1)}, s32[8]{0:T(128)}, u32[]{:S(2)}) copy-start(s32[8]{0:T(128)} %constant.31.clone) | copy-start | bytes 100
  1.2 15.1 %collective-permute-start = (bf16[512,512]{1,0:T(8,128)(2,1)S(1)}, bf16[512,512]{1,0:T(8,128)(2,1)S(1)}, u32[]{:S(2)}, u32[]{:S(2)}) collective-permute-start(bf16[512,512]{1,0:T(8,128)(2,1)S(1)} %bitcast.6), channel_id=1, source_target_pairs={{0,4},{4,8},{8,12},{12,0},{16,20},{20,24},{24,28},{28,16},{1,5},{5... | collective-permute-start | bytes 1572872 | tf_op jit(solution)/shard_map/along_y1/ppermute | solution.py:259
  3.0 13.8 %collective-permute-start.2 = (bf16[512,512]{1,0:T(8,128)(2,1)S(1)}, bf16[512,512]{1,0:T(8,128)(2,1)S(1)}, u32[]{:S(2)}, u32[]{:S(2)}) collective-permute-start(bf16[512,512]{1,0:T(8,128)(2,1)S(1)} %bitcast.7), channel_id=1, source_target_pairs={{0,12},{4,0},{8,4},{12,8},{16,28},{20,16},{24,20},{28,24},{1,13},{... | collective-permute-start | bytes 1572872 | tf_op jit(solution)/shard_map/along_y3/ppermute | solution.py:259
  4.5 15.2 %collective-permute-start.5 = (bf16[512,512]{1,0:T(8,128)(2,1)S(1)}, bf16[512,512]{1,0:T(8,128)(2,1)S(1)}, u32[]{:S(2)}, u32[]{:S(2)}) collective-permute-start(bf16[512,512]{1,0:T(8,128)(2,1)S(1)} %bitcast.8), channel_id=1, source_target_pairs={{0,16},{4,20},{8,24},{12,28},{16,0},{20,4},{24,8},{28,12},{1,17},{... | collective-permute-start | bytes 1572872 | tf_op jit(solution)/shard_map/across_x/ppermute | solution.py:255
  16.4 10.5 %collective-permute-start.1 = (bf16[256,512]{1,0:T(8,128)(2,1)S(1)}, bf16[256,512]{1,0:T(8,128)(2,1)S(1)}, u32[]{:S(2)}, u32[]{:S(2)}) collective-permute-start(bf16[256,512]{1,0:T(8,128)(2,1)S(1)} %slice.44), channel_id=1, source_target_pairs={{0,4},{4,8},{8,12},{12,0},{16,20},{20,24},{24,28},{28,16},{1,5},{5... | collective-permute-start | bytes 786440 | tf_op jit(solution)/shard_map/along_y1/ppermute | solution.py:259
  16.7 10.2 %collective-permute-start.3 = (bf16[256,512]{1,0:T(8,128)(2,1)S(1)}, bf16[256,512]{1,0:T(8,128)(2,1)S(1)}, u32[]{:S(2)}, u32[]{:S(2)}) collective-permute-start(bf16[256,512]{1,0:T(8,128)(2,1)S(1)} %slice.45), channel_id=1, source_target_pairs={{0,12},{4,0},{8,4},{12,8},{16,28},{20,16},{24,20},{28,24},{1,13},{... | collective-permute-start | bytes 786440 | tf_op jit(solution)/shard_map/along_y3/ppermute | solution.py:259
  19.8 16.5 %collective-permute-start.6 = (bf16[512,512]{1,0:T(8,128)(2,1)S(1)}, bf16[512,512]{1,0:T(8,128)(2,1)S(1)}, u32[]{:S(2)}, u32[]{:S(2)}) collective-permute-start(bf16[512,512]{1,0:T(8,128)(2,1)S(1)} %collective-permute-done.5.refs_0_), channel_id=1, source_target_pairs={{0,12},{4,0},{8,4},{12,8},{16,28},{20,16},{24,20},{28,24},{1,13},{... | collective-permute-start | bytes 1572872 | tf_op jit(solution)/shard_map/along_y3/ppermute | solution.py:259
  21.0 15.3 %collective-permute-start.7 = (bf16[512,512]{1,0:T(8,128)(2,1)S(1)}, bf16[512,512]{1,0:T(8,128)(2,1)S(1)}, u32[]{:S(2)}, u32[]{:S(2)}) collective-permute-start(bf16[512,512]{1,0:T(8,128)(2,1)S(1)} %collective-permute-done.5.refs_0_), channel_id=1, source_target_pairs={{0,4},{4,8},{8,12},{12,0},{16,20},{20,24},{24,28},{28,16},{1,5},{5... | collective-permute-start | bytes 1572872 | tf_op jit(solution)/shard_map/along_y1/ppermute | solution.py:259
  26.9 12.5 %collective-permute-start.4 = (bf16[512,512]{1,0:T(8,128)(2,1)S(1)}, bf16[512,512]{1,0:T(8,128)(2,1)S(1)}, u32[]{:S(2)}, u32[]{:S(2)}) collective-permute-start(bf16[512,512]{1,0:T(8,128)(2,1)S(1)} %constant_dynamic-update-slice_fusion.refs_1_), channel_id=1, source_target_pairs={{0,16},{4,20},{8,24},{12,28},{16,0},{20,4},{24,8},{28,12},{1,17},{... | collective-permute-start | bytes 1572872 | tf_op jit(solution)/shard_map/across_x/ppermute | solution.py:255
  40.7 2.7 %collective-permute-start.8 = (bf16[256,2048]{1,0:T(8,128)(2,1)S(1)}, bf16[256,2048]{1,0:T(8,128)(2,1)S(1)}, u32[]{:S(2)}, u32[]{:S(2)}) collective-permute-start(bf16[256,2048]{1,0:T(8,128)(2,1)S(1)} %project_last.2), channel_id=1, source_target_pairs={{0,32},{32,0},{64,96},{96,64},{1,33},{33,1},{65,97},{97,65},{2,34}... | collective-permute-start | bytes 3145736 | tf_op jit(solution)/shard_map/other_core/ppermute | solution.py:267
  43.8 18.8 %copy-start = (bf16[256,256]{1,0:T(8,128)(2,1)S(1)}, bf16[256,256]{1,0:T(8,128)(2,1)}, u32[]{:S(2)}) copy-start(bf16[256,256]{1,0:T(8,128)(2,1)} %turn.1) | copy-start | bytes 393220
  43.8 18.8 %copy-start.1 = (f32[2048]{0:T(1024)S(1)}, f32[2048]{0:T(1024)}, u32[]{:S(2)}) copy-start(f32[2048]{0:T(1024)} %param.10) | copy-start | bytes 24580
  43.9 18.8 %copy-start.2 = (f32[256]{0:T(256)S(1)}, f32[256]{0:T(256)}, u32[]{:S(2)}) copy-start(f32[256]{0:T(256)} %param.12) | copy-start | bytes 3076
  43.9 6.4 %collective-permute-start.12 = (bf16[128,512]{1,0:T(8,128)(2,1)S(1)}, bf16[128,512]{1,0:T(8,128)(2,1)S(1)}, u32[]{:S(2)}, u32[]{:S(2)}) collective-permute-start(bf16[128,512]{1,0:T(8,128)(2,1)S(1)} %get-tuple-element.77), channel_id=1, source_target_pairs={{0,64},{32,96},{64,0},{96,32},{1,65},{33,97},{65,1},{97,33},{2,66}... | collective-permute-start | bytes 393224 | tf_op jit(solution)/shard_map/other_x/ppermute | solution.py:271
  45.9 8.6 %collective-permute-start.11 = (bf16[128,512]{1,0:T(8,128)(2,1)S(1)}, bf16[128,512]{1,0:T(8,128)(2,1)S(1)}, u32[]{:S(2)}, u32[]{:S(2)}) collective-permute-start(bf16[128,512]{1,0:T(8,128)(2,1)S(1)} %get-tuple-element.78), channel_id=1, source_target_pairs={{0,64},{32,96},{64,0},{96,32},{1,65},{33,97},{65,1},{97,33},{2,66}... | collective-permute-start | bytes 393224 | tf_op jit(solution)/shard_map/other_x/ppermute | solution.py:271
  46.7 9.2 %collective-permute-start.10 = (bf16[128,512]{1,0:T(8,128)(2,1)S(1)}, bf16[128,512]{1,0:T(8,128)(2,1)S(1)}, u32[]{:S(2)}, u32[]{:S(2)}) collective-permute-start(bf16[128,512]{1,0:T(8,128)(2,1)S(1)} %get-tuple-element.79), channel_id=1, source_target_pairs={{0,64},{32,96},{64,0},{96,32},{1,65},{33,97},{65,1},{97,33},{2,66}... | collective-permute-start | bytes 393224 | tf_op jit(solution)/shard_map/other_x/ppermute | solution.py:271
  48.0 12.0 %collective-permute-start.9 = (bf16[128,512]{1,0:T(8,128)(2,1)S(1)}, bf16[128,512]{1,0:T(8,128)(2,1)S(1)}, u32[]{:S(2)}, u32[]{:S(2)}) collective-permute-start(bf16[128,512]{1,0:T(8,128)(2,1)S(1)} %get-tuple-element.80), channel_id=1, source_target_pairs={{0,64},{32,96},{64,0},{96,32},{1,65},{33,97},{65,1},{97,33},{2,66}... | collective-permute-start | bytes 393224 | tf_op jit(solution)/shard_map/other_x/ppermute | solution.py:271
  50.4 12.2 %collective-permute-start.14 = (bf16[128,512]{1,0:T(8,128)(2,1)S(1)}, bf16[128,512]{1,0:T(8,128)(2,1)S(1)}, u32[]{:S(2)}, u32[]{:S(2)}) collective-permute-start(bf16[128,512]{1,0:T(8,128)(2,1)S(1)} %fusion), channel_id=1, source_target_pairs={{0,2},{1,3},{2,0},{3,1},{4,6},{5,7},{6,4},{7,5},{8,10},{9,11},{10,... | collective-permute-start | bytes 393224 | tf_op jit(solution)/shard_map/along_z2/ppermute | solution.py:263
  54.5 8.1 %collective-permute-start.13 = (bf16[128,512]{1,0:T(8,128)(2,1)S(1)}, bf16[128,512]{1,0:T(8,128)(2,1)S(1)}, u32[]{:S(2)}, u32[]{:S(2)}) collective-permute-start(bf16[128,512]{1,0:T(8,128)(2,1)S(1)} %fusion.1), channel_id=1, source_target_pairs={{0,1},{1,2},{2,3},{3,0},{4,5},{5,6},{6,7},{7,4},{8,9},{9,10},{10,1... | collective-permute-start | bytes 393224 | tf_op jit(solution)/shard_map/along_z1/ppermute | solution.py:263
  56.0 6.6 %collective-permute-start.15 = (bf16[128,512]{1,0:T(8,128)(2,1)S(1)}, bf16[128,512]{1,0:T(8,128)(2,1)S(1)}, u32[]{:S(2)}, u32[]{:S(2)}) collective-permute-start(bf16[128,512]{1,0:T(8,128)(2,1)S(1)} %fusion.2), channel_id=1, source_target_pairs={{0,3},{1,0},{2,1},{3,2},{4,7},{5,4},{6,5},{7,6},{8,11},{9,8},{10,9... | collective-permute-start | bytes 393224 | tf_op jit(solution)/shard_map/along_z3/ppermute | solution.py:263
  63.8 6.5 %collective-permute-start.17 = (bf16[128,512]{1,0:T(8,128)(2,1)S(1)}, bf16[128,512]{1,0:T(8,128)(2,1)S(1)}, u32[]{:S(2)}, u32[]{:S(2)}) collective-permute-start(bf16[128,512]{1,0:T(8,128)(2,1)S(1)} %get-tuple-element.49.refs_0_), channel_id=1, source_target_pairs={{0,64},{32,96},{64,0},{96,32},{1,65},{33,97},{65,1},{97,33},{2,66}... | collective-permute-start | bytes 393224 | tf_op jit(solution)/shard_map/other_x/ppermute | solution.py:271
  65.2 7.0 %collective-permute-start.19 = (bf16[128,512]{1,0:T(8,128)(2,1)S(1)}, bf16[128,512]{1,0:T(8,128)(2,1)S(1)}, u32[]{:S(2)}, u32[]{:S(2)}) collective-permute-start(bf16[128,512]{1,0:T(8,128)(2,1)S(1)} %get-tuple-element.54), channel_id=1, source_target_pairs={{0,1},{1,2},{2,3},{3,0},{4,5},{5,6},{6,7},{7,4},{8,9},{9,10},{10,1... | collective-permute-start | bytes 393224 | tf_op jit(solution)/shard_map/along_z1/ppermute | solution.py:263
  65.5 9.2 %collective-permute-start.18 = (bf16[128,512]{1,0:T(8,128)(2,1)S(1)}, bf16[128,512]{1,0:T(8,128)(2,1)S(1)}, u32[]{:S(2)}, u32[]{:S(2)}) collective-permute-start(bf16[128,512]{1,0:T(8,128)(2,1)S(1)} %get-tuple-element.52), channel_id=1, source_target_pairs={{0,2},{1,3},{2,0},{3,1},{4,6},{5,7},{6,4},{7,5},{8,10},{9,11},{10,... | collective-permute-start | bytes 393224 | tf_op jit(solution)/shard_map/along_z2/ppermute | solution.py:263
  70.3 5.0 %collective-permute-start.16 = (bf16[128,512]{1,0:T(8,128)(2,1)S(1)}, bf16[128,512]{1,0:T(8,128)(2,1)S(1)}, u32[]{:S(2)}, u32[]{:S(2)}) collective-permute-start(bf16[128,512]{1,0:T(8,128)(2,1)S(1)} %get-tuple-element.50), channel_id=1, source_target_pairs={{0,3},{1,0},{2,1},{3,2},{4,7},{5,4},{6,5},{7,6},{8,11},{9,8},{10,9... | collective-permute-start | bytes 393224 | tf_op jit(solution)/shard_map/along_z3/ppermute | solution.py:263
  75.9 2.0 %collective-permute-start.20 = (bf16[128,2048]{1,0:T(8,128)(2,1)S(1)}, bf16[128,2048]{1,0:T(8,128)(2,1)S(1)}, u32[]{:S(2)}, u32[]{:S(2)}) collective-permute-start(bf16[128,2048]{1,0:T(8,128)(2,1)S(1)} %get-tuple-element.56), channel_id=1, source_target_pairs={{0,32},{32,0},{64,96},{96,64},{1,33},{33,1},{65,97},{97,65},{2,34}... | collective-permute-start | bytes 1572872 | tf_op jit(solution)/shard_map/other_core/ppermute | solution.py:267
  76.0 11.5 %collective-permute-start.21 = (bf16[384,512]{1,0:T(8,128)(2,1)S(1)}, bf16[384,512]{1,0:T(8,128)(2,1)S(1)}, u32[]{:S(2)}, u32[]{:S(2)}) collective-permute-start(bf16[384,512]{1,0:T(8,128)(2,1)S(1)} %get-tuple-element.57), channel_id=1, source_target_pairs={{0,64},{32,96},{64,0},{96,32},{1,65},{33,97},{65,1},{97,33},{2,66}... | collective-permute-start | bytes 1179656 | tf_op jit(solution)/shard_map/other_x/ppermute | solution.py:271
  79.8 9.7 %collective-permute-start.22 = (bf16[256,512]{1,0:T(8,128)(2,1)S(1)}, bf16[256,512]{1,0:T(8,128)(2,1)S(1)}, u32[]{:S(2)}, u32[]{:S(2)}) collective-permute-start(bf16[256,512]{1,0:T(8,128)(2,1)S(1)} %get-tuple-element.58), channel_id=1, source_target_pairs={{0,4},{4,8},{8,12},{12,0},{16,20},{20,24},{24,28},{28,16},{1,5},{5... | collective-permute-start | bytes 786440 | tf_op jit(solution)/shard_map/along_y1/ppermute | solution.py:259
  80.3 9.2 %collective-permute-start.23 = (bf16[256,512]{1,0:T(8,128)(2,1)S(1)}, bf16[256,512]{1,0:T(8,128)(2,1)S(1)}, u32[]{:S(2)}, u32[]{:S(2)}) collective-permute-start(bf16[256,512]{1,0:T(8,128)(2,1)S(1)} %get-tuple-element.61), channel_id=1, source_target_pairs={{0,12},{4,0},{8,4},{12,8},{16,28},{20,16},{24,20},{28,24},{1,13},{... | collective-permute-start | bytes 786440 | tf_op jit(solution)/shard_map/along_y3/ppermute | solution.py:259
  90.1 4.0 %collective-permute-start.24 = (bf16[128,2048]{1,0:T(8,128)(2,1)S(1)}, bf16[128,2048]{1,0:T(8,128)(2,1)S(1)}, u32[]{:S(2)}, u32[]{:S(2)}) collective-permute-start(bf16[128,2048]{1,0:T(8,128)(2,1)S(1)} %assemble.3), channel_id=1, source_target_pairs={{0,32},{32,0},{64,96},{96,64},{1,33},{33,1},{65,97},{97,65},{2,34}... | collective-permute-start | bytes 1572872 | tf_op jit(solution)/shard_map/other_core/ppermute | solution.py:267
  90.2 13.7 %collective-permute-start.25 = (bf16[256,512]{1,0:T(8,128)(2,1)S(1)}, bf16[256,512]{1,0:T(8,128)(2,1)S(1)}, u32[]{:S(2)}, u32[]{:S(2)}) collective-permute-start(bf16[256,512]{1,0:T(8,128)(2,1)S(1)} %get-tuple-element.60), channel_id=1, source_target_pairs={{0,16},{4,20},{8,24},{12,28},{16,0},{20,4},{24,8},{28,12},{1,17},{... | collective-permute-start | bytes 786440 | tf_op jit(solution)/shard_map/across_x/ppermute | solution.py:255
  93.0 13.8 %collective-permute-start.26 = (bf16[256,512]{1,0:T(8,128)(2,1)S(1)}, bf16[256,512]{1,0:T(8,128)(2,1)S(1)}, u32[]{:S(2)}, u32[]{:S(2)}) collective-permute-start(bf16[256,512]{1,0:T(8,128)(2,1)S(1)} %get-tuple-element.66), channel_id=1, source_target_pairs={{0,4},{4,8},{8,12},{12,0},{16,20},{20,24},{24,28},{28,16},{1,5},{5... | collective-permute-start | bytes 786440 | tf_op jit(solution)/shard_map/along_y1/ppermute | solution.py:259
  94.3 12.7 %collective-permute-start.27 = (bf16[256,512]{1,0:T(8,128)(2,1)S(1)}, bf16[256,512]{1,0:T(8,128)(2,1)S(1)}, u32[]{:S(2)}, u32[]{:S(2)}) collective-permute-start(bf16[256,512]{1,0:T(8,128)(2,1)S(1)} %get-tuple-element.67), channel_id=1, source_target_pairs={{0,12},{4,0},{8,4},{12,8},{16,28},{20,16},{24,20},{28,24},{1,13},{... | collective-permute-start | bytes 786440 | tf_op jit(solution)/shard_map/along_y3/ppermute | solution.py:259
  100.6 16.3 %collective-permute-start.29 = (bf16[512,512]{1,0:T(8,128)(2,1)S(1)}, bf16[512,512]{1,0:T(8,128)(2,1)S(1)}, u32[]{:S(2)}, u32[]{:S(2)}) collective-permute-start(bf16[512,512]{1,0:T(8,128)(2,1)S(1)} %get-tuple-element.64), channel_id=1, source_target_pairs={{0,4},{4,8},{8,12},{12,0},{16,20},{20,24},{24,28},{28,16},{1,5},{5... | collective-permute-start | bytes 1572872 | tf_op jit(solution)/shard_map/along_y1/ppermute | solution.py:259
  100.7 16.2 %collective-permute-start.30 = (bf16[512,512]{1,0:T(8,128)(2,1)S(1)}, bf16[512,512]{1,0:T(8,128)(2,1)S(1)}, u32[]{:S(2)}, u32[]{:S(2)}) collective-permute-start(bf16[512,512]{1,0:T(8,128)(2,1)S(1)} %get-tuple-element.71), channel_id=1, source_target_pairs={{0,12},{4,0},{8,4},{12,8},{16,28},{20,16},{24,20},{28,24},{1,13},{... | collective-permute-start | bytes 1572872 | tf_op jit(solution)/shard_map/along_y3/ppermute | solution.py:259
  103.9 8.8 %collective-permute-start.28 = (bf16[256,512]{1,0:T(8,128)(2,1)S(1)}, bf16[256,512]{1,0:T(8,128)(2,1)S(1)}, u32[]{:S(2)}, u32[]{:S(2)}) collective-permute-start(bf16[256,512]{1,0:T(8,128)(2,1)S(1)} %expand.11), channel_id=1, source_target_pairs={{0,16},{4,20},{8,24},{12,28},{16,0},{20,4},{24,8},{28,12},{1,17},{... | collective-permute-start | bytes 786440 | tf_op jit(solution)/shard_map/across_x/ppermute | solution.py:255
  106.8 14.2 %collective-permute-start.32 = (bf16[256,512]{1,0:T(8,128)(2,1)S(1)}, bf16[256,512]{1,0:T(8,128)(2,1)S(1)}, u32[]{:S(2)}, u32[]{:S(2)}) collective-permute-start(bf16[256,512]{1,0:T(8,128)(2,1)S(1)} %expand.13), channel_id=1, source_target_pairs={{0,4},{4,8},{8,12},{12,0},{16,20},{20,24},{24,28},{28,16},{1,5},{5... | collective-permute-start | bytes 786440 | tf_op jit(solution)/shard_map/along_y1/ppermute | solution.py:259
  114.1 7.0 %collective-permute-start.35 = (bf16[256,512]{1,0:T(8,128)(2,1)S(1)}, bf16[256,512]{1,0:T(8,128)(2,1)S(1)}, u32[]{:S(2)}, u32[]{:S(2)}) collective-permute-start(bf16[256,512]{1,0:T(8,128)(2,1)S(1)} %expand.15), channel_id=1, source_target_pairs={{0,12},{4,0},{8,4},{12,8},{16,28},{20,16},{24,20},{28,24},{1,13},{... | collective-permute-start | bytes 786440 | tf_op jit(solution)/shard_map/along_y3/ppermute | solution.py:259
  114.7 9.9 %collective-permute-start.31 = (bf16[256,512]{1,0:T(8,128)(2,1)S(1)}, bf16[256,512]{1,0:T(8,128)(2,1)S(1)}, u32[]{:S(2)}, u32[]{:S(2)}) collective-permute-start(bf16[256,512]{1,0:T(8,128)(2,1)S(1)} %expand.14), channel_id=1, source_target_pairs={{0,16},{4,20},{8,24},{12,28},{16,0},{20,4},{24,8},{28,12},{1,17},{... | collective-permute-start | bytes 786440 | tf_op jit(solution)/shard_map/across_x/ppermute | solution.py:255
  118.2 11.0 %collective-permute-start.34 = (bf16[256,512]{1,0:T(8,128)(2,1)S(1)}, bf16[256,512]{1,0:T(8,128)(2,1)S(1)}, u32[]{:S(2)}, u32[]{:S(2)}) collective-permute-start(bf16[256,512]{1,0:T(8,128)(2,1)S(1)} %expand.16), channel_id=1, source_target_pairs={{0,16},{4,20},{8,24},{12,28},{16,0},{20,4},{24,8},{28,12},{1,17},{... | collective-permute-start | bytes 786440 | tf_op jit(solution)/shard_map/across_x/ppermute | solution.py:255
  121.0 8.2 %collective-permute-start.33 = (bf16[256,512]{1,0:T(8,128)(2,1)S(1)}, bf16[256,512]{1,0:T(8,128)(2,1)S(1)}, u32[]{:S(2)}, u32[]{:S(2)}) collective-permute-start(bf16[256,512]{1,0:T(8,128)(2,1)S(1)} %collective-permute-done.32), channel_id=1, source_target_pairs={{0,4},{4,8},{8,12},{12,0},{16,20},{20,24},{24,28},{28,16},{1,5},{5... | collective-permute-start | bytes 786440 | tf_op jit(solution)/shard_map/along_y1/ppermute | solution.py:259
  121.1 8.1 %collective-permute-start.36 = (bf16[256,512]{1,0:T(8,128)(2,1)S(1)}, bf16[256,512]{1,0:T(8,128)(2,1)S(1)}, u32[]{:S(2)}, u32[]{:S(2)}) collective-permute-start(bf16[256,512]{1,0:T(8,128)(2,1)S(1)} %collective-permute-done.35), channel_id=1, source_target_pairs={{0,12},{4,0},{8,4},{12,8},{16,28},{20,16},{24,20},{28,24},{1,13},{... | collective-permute-start | bytes 786440 | tf_op jit(solution)/shard_map/along_y3/ppermute | solution.py:259

commit v5 on v4

--- a/solution.py
+++ b/solution.py
@@ -54,25 +54,25 @@
     )(*args)
 
 
-def last_kernel(i, start, at_ref, a_ref, table, total, out):
-    m, ns = out.shape[0], a_ref.shape[1]
-    rows = slice(start, start + m)
+def last_kernel(i, places, at_ref, a_ref, table, total, out):
+    m, ns = out.shape[0] // len(places), a_ref.shape[1]
     tile = table.shape[1] // 4
+    groups = [pl.ds(pl.multiple_of((at_ref[9] ^ p) * m, m), m) for p in places]
+    a = jnp.concatenate([a_ref[rows, :] for rows in groups], axis=0)
     for j in range(4):
         lanes = pl.ds(pl.multiple_of(((at_ref[8] + j) & 3) * tile, tile), tile)
-        value = total[rows, lanes] + jnp.dot(
-            a_ref[rows, :], table[rows_at(at_ref, i, ns), lanes], preferred_element_type=F32
-        )
+        value = jnp.dot(a, table[rows_at(at_ref, i, ns), lanes], preferred_element_type=F32)
+        value = value + jnp.concatenate([total[rows, lanes] for rows in groups], axis=0)
         out[:, j * tile : (j + 1) * tile] = value.astype(out.dtype)
 
 
-def project_last(a, i, at, table, total, start, dtype):
+def project_last(a, i, at, table, total, places, dtype):
     m, width = total.shape
     return pl.pallas_call(
-        functools.partial(last_kernel, i, start),
+        functools.partial(last_kernel, i, places),
         in_specs=[SMEM] + [VMEM] * 3,
         out_specs=VMEM,
-        out_shape=jax.ShapeDtypeStruct((m // 2, width), dtype),
+        out_shape=jax.ShapeDtypeStruct((m // 4 * len(places), width), dtype),
         cost_estimate=COST,
         compiler_params=PARAMS,
         name="project_last",
@@ -274,11 +274,7 @@
     flips = jnp.array([0] * 4 + [4] * 4, jnp.int32)
     at = jnp.concatenate([(x_hi ^ flips) + ((y + steps) & 3), tm[None], row[None]])
 
-    def group(g):
-        return lax.dynamic_slice_in_dim(right_sides, g * pair, pair, 0)
-
-    own = jnp.concatenate([group(row ^ 3), group(row ^ 1), group(row ^ 2), group(row)], 0)
-    own = own.reshape(rows, ns)
+    own = right_sides.reshape(rows, ns)
     down, up = along_y(own, 1), along_y(own, -1)
     x_own = across_x(own)
     table, total = project_first(own, at, eigen_basis)
@@ -292,8 +288,8 @@
     total = project([up, down], [UP, DOWN], at, table, total)
     total = project([x_own, far], [X_OWN, FAR], at, table, total)
     total = project([x_up, x_down], [X_UP, X_DOWN], at, table, total)
-    give = project_last(x_far, X_FAR, at, table, total, 0, BF16)
-    keep = project_last(after(x_far, give), X_FAR, at, table, total, rows // 2, F32)
+    give = project_last(x_far, X_FAR, at, table, total, (3, 1), BF16)
+    keep = project_last(after(x_far, give), X_FAR, at, table, total, (2, 0), F32)
 
     both = keep + other_core(give).astype(F32)
     half = pair * nt

time: 131 us -> 130 us (level)
  waiting for transfers between devices: 31.5 us -> 29.8 us
    ppermute x16, waiting for transfers between devices: 12.8 us -> 11.4 us  [along_y(): return lax.ppermute(a, 'col', [(c, c & 4 | c + k & 3) for c in range(8)])]
  transfers between devices with their start and end apart: 37 -> 37, of which waited for: 16 -> 16; matrix products, arithmetic and copies ran while one was open for 0% -> 1% of each run, Pallas kernels for 25% -> 25%
where the time goes in v5:
time: 130 us
  starting transfers between devices  58.1 us (45%)
  Pallas kernels  38.3 us (29%)
  waiting for transfers between devices  29.8 us (23%)
  other arithmetic  1.36 us (1%)
    ppermute x16, starting transfers between devices, along_y(): return lax.ppermute(a, 'col', [(c, c & 4 | c + k & 3) for c in range(8)])  22.7 us
    pallas_call x9, Pallas kernels, expand(): pl.pallas_call(functools.partial(expand_kernel, which, ns, len(fields), t...  15.4 us
    ppermute x6, starting transfers between devices, along_z(): return lax.ppermute(a, 'tm', [(z, z + k & 3) for z in range(4)])  14.5 us
    ppermute x6, starting transfers between devices, across_x(): return lax.ppermute(a, 'col', [(c, c ^ 4) for c in range(8)])  14.3 us
    ppermute x16, waiting for transfers between devices, along_y(): return lax.ppermute(a, 'col', [(c, c & 4 | c + k & 3) for c in range(8)])  11.4 us
    pallas_call x3, Pallas kernels, project(): pl.pallas_call(functools.partial(project_kernel, which), in_specs=[SMEM]...  9.4 us
    ppermute x6, waiting for transfers between devices, along_z(): return lax.ppermute(a, 'tm', [(z, z + k & 3) for z in range(4)])  7.45 us
    pallas_call x1, Pallas kernels, project_first(): pl.pallas_call(first_kernel, in_specs=[SMEM, VMEM, pl.BlockSpec(memory_sp...  6.91 us
  transfers between devices with their start and end apart: 37, of which 16 were waited for; matrix products, arithmetic and copies ran while one was open for 1% of the time, Pallas kernels for 25%

profile of v5, /device:TPU:0, one launch (start us, length us, event | category | flops | bytes accessed | tf_op | source)
XLA Modules:
  0.0 129.7 jit_solution(6632166519559177357)
XLA Ops:
  0.0 1.7 %collective-permute-start = (bf16[512,512]{1,0:T(8,128)(2,1)}, bf16[512,512]{1,0:T(8,128)(2,1)S(1)}, u32[]{:S(2)}, u32[]{:S(2)}) collective-permute-start(bf16[512,512]{1,0:T(8,128)(2,1)} %bitcast.6), channel_id=1, source_target_pairs={{0,4},{4,8},{8,12},{12,0},{16,20},{20,24},{24,28},{28,16},{1,5},{5... | collective-permute-start | bytes 1572872 | tf_op jit(solution)/shard_map/along_y1/ppermute | solution.py:259
  1.7 1.6 %collective-permute-start.2 = (bf16[512,512]{1,0:T(8,128)(2,1)}, bf16[512,512]{1,0:T(8,128)(2,1)S(1)}, u32[]{:S(2)}, u32[]{:S(2)}) collective-permute-start(bf16[512,512]{1,0:T(8,128)(2,1)} %bitcast.7), channel_id=1, source_target_pairs={{0,12},{4,0},{8,4},{12,8},{16,28},{20,16},{24,20},{28,24},{1,13},{... | collective-permute-start | bytes 1572872 | tf_op jit(solution)/shard_map/along_y3/ppermute | solution.py:259
  3.2 3.1 %collective-permute-start.5 = (bf16[512,512]{1,0:T(8,128)(2,1)}, bf16[512,512]{1,0:T(8,128)(2,1)S(1)}, u32[]{:S(2)}, u32[]{:S(2)}) collective-permute-start(bf16[512,512]{1,0:T(8,128)(2,1)} %bitcast.8), channel_id=1, source_target_pairs={{0,16},{4,20},{8,24},{12,28},{16,0},{20,4},{24,8},{28,12},{1,17},{... | collective-permute-start | bytes 1572872 | tf_op jit(solution)/shard_map/across_x/ppermute | solution.py:255
  8.1 6.9 %project_first.1 = (bf16[4096,2048]{1,0:T(8,128)(2,1)S(1)}, f32[512,2048]{1,0:T(8,128)S(1)}) custom-call(s32[10]{0:T(128)S(1)} %pad_add_fusion.at_ref, bf16[512,512]{1,0:T(8,128)(2,1)S(1)} %bitcast.9, bf16[4096,2048]{1,0:T(8,128)(2,1)} %basis_ref.1), custom_call_target="tpu_custom_call" | custom-call | flops 1024 | bytes 1024 | tf_op jit(solution)/shard_map/project_first/pallas_call | solution.py:97
  15.7 3.0 %collective-permute-start.3 = (bf16[256,512]{1,0:T(8,128)(2,1)S(1)}, bf16[256,512]{1,0:T(8,128)(2,1)S(1)}, u32[]{:S(2)}, u32[]{:S(2)}) collective-permute-start(bf16[256,512]{1,0:T(8,128)(2,1)S(1)} %slice.45), channel_id=1, source_target_pairs={{0,12},{4,0},{8,4},{12,8},{16,28},{20,16},{24,20},{28,24},{1,13},{... | collective-permute-start | bytes 786440 | tf_op jit(solution)/shard_map/along_y3/ppermute | solution.py:259
  18.7 1.3 collective-permute-start.6
  20.7 5.1 %collective-permute-done.1 = bf16[256,512]{1,0:T(8,128)(2,1)S(1)} collective-permute-done((bf16[256,512]{1,0:T(8,128)(2,1)S(1)}, bf16[256,512]{1,0:T(8,128)(2,1)S(1)}, u32[]{:S(2)}, u32[]{:S(2)}) %collective-permute-start.1) | collective-permute-done | bytes 262176 | tf_op jit(solution)/shard_map/along_y1/ppermute | solution.py:259
  25.8 3.0 %collective-permute-start.4 = (bf16[512,512]{1,0:T(8,128)(2,1)S(1)}, bf16[512,512]{1,0:T(8,128)(2,1)S(1)}, u32[]{:S(2)}, u32[]{:S(2)}) collective-permute-start(bf16[512,512]{1,0:T(8,128)(2,1)S(1)} %constant_dynamic-update-slice_fusion.refs_1_), channel_id=1, source_target_pairs={{0,16},{4,20},{8,24},{12,28},{16,0},{20,4},{24,8},{28,12},{1,17},{... | collective-permute-start | bytes 1572872 | tf_op jit(solution)/shard_map/across_x/ppermute | solution.py:255
  28.8 3.2 %project.3.refs_3_ = f32[512,2048]{1,0:T(8,128)S(1)} custom-call(s32[10]{0:T(128)S(1)} %pad_add_fusion.at_ref, bf16[512,512]{1,0:T(8,128)(2,1)S(1)} %collective-permute-done.2.refs_0_, bf16[512,512]{1,0:T(8,128)(2,1)S(1)} %collective-permute-done.refs_1_, ...), custom_call_target="tpu_custom_call", output_to_operand_aliasing={{}: (4, {})} | custom-call | flops 1024 | bytes 1024 | tf_op jit(solution)/shard_map/project/pallas_call | solution.py:45
  32.0 3.2 %project.4.refs_3_ = f32[512,2048]{1,0:T(8,128)S(1)} custom-call(s32[10]{0:T(128)S(1)} %pad_add_fusion.at_ref, bf16[512,512]{1,0:T(8,128)(2,1)S(1)} %collective-permute-done.5.refs_0_, bf16[512,512]{1,0:T(8,128)(2,1)S(1)} %constant_dynamic-update-slice_fusion.refs_1_, ...), custom_call_target="tpu_custom_call", output_to_operand_aliasing={{}: (4, {})} | custom-call | flops 1024 | bytes 1024 | tf_op jit(solution)/shard_map/project/pallas_call | solution.py:45
  35.2 3.1 %project.5.total = f32[512,2048]{1,0:T(8,128)S(1)} custom-call(s32[10]{0:T(128)S(1)} %pad_add_fusion.at_ref, bf16[512,512]{1,0:T(8,128)(2,1)S(1)} %collective-permute-done.6.refs_0_, bf16[512,512]{1,0:T(8,128)(2,1)S(1)} %collective-permute-done.7.refs_1_, ...), custom_call_target="tpu_custom_call", output_to_operand_aliasing={{}: (4, {})} | custom-call | flops 1024 | bytes 1024 | tf_op jit(solution)/shard_map/project/pallas_call | solution.py:45
  38.3 1.3 project_last.2
  39.7 1.3 project_last.3
  40.9 1.4 %collective-permute-done.8 = bf16[256,2048]{1,0:T(8,128)(2,1)S(1)} collective-permute-done((bf16[256,2048]{1,0:T(8,128)(2,1)S(1)}, bf16[256,2048]{1,0:T(8,128)(2,1)S(1)}, u32[]{:S(2)}, u32[]{:S(2)}) %collective-permute-start.8) | collective-permute-done | bytes 1048608 | tf_op jit(solution)/shard_map/other_core/ppermute | solution.py:267
  42.8 1.4 %collective-permute-start.12 = (bf16[128,512]{1,0:T(8,128)(2,1)S(1)}, bf16[128,512]{1,0:T(8,128)(2,1)S(1)}, u32[]{:S(2)}, u32[]{:S(2)}) collective-permute-start(bf16[128,512]{1,0:T(8,128)(2,1)S(1)} %get-tuple-element.77), channel_id=1, source_target_pairs={{0,64},{32,96},{64,0},{96,32},{1,65},{33,97},{65,1},{97,33},{2,66}... | collective-permute-start | bytes 393224 | tf_op jit(solution)/shard_map/other_x/ppermute | solution.py:271
  45.6 1.3 collective-permute-start.10
  47.7 1.6 %collective-permute-done.12 = bf16[128,512]{1,0:T(8,128)(2,1)S(1)} collective-permute-done((bf16[128,512]{1,0:T(8,128)(2,1)S(1)}, bf16[128,512]{1,0:T(8,128)(2,1)S(1)}, u32[]{:S(2)}, u32[]{:S(2)}) %collective-permute-start.12) | collective-permute-done | bytes 131104 | tf_op jit(solution)/shard_map/other_x/ppermute | solution.py:271
  49.2 4.0 %collective-permute-start.14 = (bf16[128,512]{1,0:T(8,128)(2,1)S(1)}, bf16[128,512]{1,0:T(8,128)(2,1)S(1)}, u32[]{:S(2)}, u32[]{:S(2)}) collective-permute-start(bf16[128,512]{1,0:T(8,128)(2,1)S(1)} %fusion), channel_id=1, source_target_pairs={{0,2},{1,3},{2,0},{3,1},{4,6},{5,7},{6,4},{7,5},{8,10},{9,11},{10,... | collective-permute-start | bytes 393224 | tf_op jit(solution)/shard_map/along_z2/ppermute | solution.py:263
  53.2 1.3 collective-permute-start.13
  54.9 4.1 %collective-permute-start.15 = (bf16[128,512]{1,0:T(8,128)(2,1)S(1)}, bf16[128,512]{1,0:T(8,128)(2,1)S(1)}, u32[]{:S(2)}, u32[]{:S(2)}) collective-permute-start(bf16[128,512]{1,0:T(8,128)(2,1)S(1)} %fusion.2), channel_id=1, source_target_pairs={{0,3},{1,0},{2,1},{3,2},{4,7},{5,4},{6,5},{7,6},{8,11},{9,8},{10,9... | collective-permute-start | bytes 393224 | tf_op jit(solution)/shard_map/along_z3/ppermute | solution.py:263
  59.0 2.5 %collective-permute-done.15.refs_3_ = bf16[128,512]{1,0:T(8,128)(2,1)S(1)} collective-permute-done((bf16[128,512]{1,0:T(8,128)(2,1)S(1)}, bf16[128,512]{1,0:T(8,128)(2,1)S(1)}, u32[]{:S(2)}, u32[]{:S(2)}) %collective-permute-start.15) | collective-permute-done | bytes 131104 | tf_op jit(solution)/shard_map/along_z3/ppermute | solution.py:263
  62.7 1.4 %collective-permute-start.17 = (bf16[128,512]{1,0:T(8,128)(2,1)S(1)}, bf16[128,512]{1,0:T(8,128)(2,1)S(1)}, u32[]{:S(2)}, u32[]{:S(2)}) collective-permute-start(bf16[128,512]{1,0:T(8,128)(2,1)S(1)} %get-tuple-element.49.refs_0_), channel_id=1, source_target_pairs={{0,64},{32,96},{64,0},{96,32},{1,65},{33,97},{65,1},{97,33},{2,66}... | collective-permute-start | bytes 393224 | tf_op jit(solution)/shard_map/other_x/ppermute | solution.py:271
  64.4 4.8 %collective-permute-start.18 = (bf16[128,512]{1,0:T(8,128)(2,1)S(1)}, bf16[128,512]{1,0:T(8,128)(2,1)S(1)}, u32[]{:S(2)}, u32[]{:S(2)}) collective-permute-start(bf16[128,512]{1,0:T(8,128)(2,1)S(1)} %get-tuple-element.52), channel_id=1, source_target_pairs={{0,2},{1,3},{2,0},{3,1},{4,6},{5,7},{6,4},{7,5},{8,10},{9,11},{10,... | collective-permute-start | bytes 393224 | tf_op jit(solution)/shard_map/along_z2/ppermute | solution.py:263
  69.2 1.9 %collective-permute-done.19.refs_3_ = bf16[128,512]{1,0:T(8,128)(2,1)S(1)} collective-permute-done((bf16[128,512]{1,0:T(8,128)(2,1)S(1)}, bf16[128,512]{1,0:T(8,128)(2,1)S(1)}, u32[]{:S(2)}, u32[]{:S(2)}) %collective-permute-start.19) | collective-permute-done | bytes 131104 | tf_op jit(solution)/shard_map/along_z1/ppermute | solution.py:263
  71.1 2.5 %collective-permute-done.18.refs_2_ = bf16[128,512]{1,0:T(8,128)(2,1)S(1)} collective-permute-done((bf16[128,512]{1,0:T(8,128)(2,1)S(1)}, bf16[128,512]{1,0:T(8,128)(2,1)S(1)}, u32[]{:S(2)}, u32[]{:S(2)}) %collective-permute-start.18) | collective-permute-done | bytes 131104 | tf_op jit(solution)/shard_map/along_z2/ppermute | solution.py:263
  76.9 1.8 %expand.9 = (bf16[256,512]{1,0:T(8,128)(2,1)S(1)}, bf16[256,512]{1,0:T(8,128)(2,1)S(1)}) custom-call(s32[10]{0:T(128)S(1)} %pad_add_fusion.at_ref, bf16[256,2048]{1,0:T(8,128)(2,1)S(1)} %constant_dynamic-update-slice_fusion.2.refs_0_, bf16[4096,2048]{1,0:T(8,128)(2,1)S(1)} %get-tuple-element.43.refs_2_.table.refs_1_), custom_call_target="tpu_custom_call" | custom-call | flops 1073741824 | bytes 1024 | tf_op jit(solution)/shard_map/expand/pallas_call | solution.py:137
  79.2 2.8 %collective-permute-start.23 = (bf16[256,512]{1,0:T(8,128)(2,1)S(1)}, bf16[256,512]{1,0:T(8,128)(2,1)S(1)}, u32[]{:S(2)}, u32[]{:S(2)}) collective-permute-start(bf16[256,512]{1,0:T(8,128)(2,1)S(1)} %get-tuple-element.61), channel_id=1, source_target_pairs={{0,12},{4,0},{8,4},{12,8},{16,28},{20,16},{24,20},{28,24},{1,13},{... | collective-permute-start | bytes 786440 | tf_op jit(solution)/shard_map/along_y3/ppermute | solution.py:259
  82.0 2.4 %expand.10 = (bf16[256,512]{1,0:T(8,128)(2,1)S(1)}, bf16[256,512]{1,0:T(8,128)(2,1)S(1)}, bf16[256,512]{1,0:T(8,128)(2,1)S(1)}) custom-call(s32[10]{0:T(128)S(1)} %pad_add_fusion.at_ref, bf16[256,2048]{1,0:T(8,128)(2,1)S(1)} %constant_dynamic-update-slice_fusion.2.refs_0_, bf16[4096,2048]{1,0:T(8,128)(2,1)S(1)} %get-tuple-element.43.refs_2_.table.refs_1_), custom_call_target="tpu_custom_call" | custom-call | flops 1073741824 | bytes 1024 | tf_op jit(solution)/shard_map/expand/pallas_call | solution.py:137
  84.4 2.1 %collective-permute-done.21.refs_1_ = bf16[384,512]{1,0:T(8,128)(2,1)S(1)} collective-permute-done((bf16[384,512]{1,0:T(8,128)(2,1)S(1)}, bf16[384,512]{1,0:T(8,128)(2,1)S(1)}, u32[]{:S(2)}, u32[]{:S(2)}) %collective-permute-start.21) | collective-permute-done | bytes 393248 | tf_op jit(solution)/shard_map/other_x/ppermute | solution.py:271
  86.4 2.0 %collective-permute-done.22.refs_2_ = bf16[256,512]{1,0:T(8,128)(2,1)S(1)} collective-permute-done((bf16[256,512]{1,0:T(8,128)(2,1)S(1)}, bf16[256,512]{1,0:T(8,128)(2,1)S(1)}, u32[]{:S(2)}, u32[]{:S(2)}) %collective-permute-start.22) | collective-permute-done | bytes 262176 | tf_op jit(solution)/shard_map/along_y1/ppermute | solution.py:259
  89.1 2.8 %collective-permute-start.25 = (bf16[256,512]{1,0:T(8,128)(2,1)S(1)}, bf16[256,512]{1,0:T(8,128)(2,1)S(1)}, u32[]{:S(2)}, u32[]{:S(2)}) collective-permute-start(bf16[256,512]{1,0:T(8,128)(2,1)S(1)} %get-tuple-element.60), channel_id=1, source_target_pairs={{0,16},{4,20},{8,24},{12,28},{16,0},{20,4},{24,8},{28,12},{1,17},{... | collective-permute-start | bytes 786440 | tf_op jit(solution)/shard_map/across_x/ppermute | solution.py:255
  93.2 2.2 %collective-permute-start.27 = (bf16[256,512]{1,0:T(8,128)(2,1)S(1)}, bf16[256,512]{1,0:T(8,128)(2,1)S(1)}, u32[]{:S(2)}, u32[]{:S(2)}) collective-permute-start(bf16[256,512]{1,0:T(8,128)(2,1)S(1)} %get-tuple-element.67), channel_id=1, source_target_pairs={{0,12},{4,0},{8,4},{12,8},{16,28},{20,16},{24,20},{28,24},{1,13},{... | collective-permute-start | bytes 786440 | tf_op jit(solution)/shard_map/along_y3/ppermute | solution.py:259
  95.3 1.3 expand.11
  96.6 2.9 %expand.12 = (bf16[512,512]{1,0:T(8,128)(2,1)S(1)}, bf16[512,512]{1,0:T(8,128)(2,1)S(1)}) custom-call(s32[10]{0:T(128)S(1)} %pad_add_fusion.at_ref, bf16[256,2048]{1,0:T(8,128)(2,1)S(1)} %pad_maximum_fusion.refs_0_.refs_1_, bf16[4096,2048]{1,0:T(8,128)(2,1)S(1)} %get-tuple-element.43.refs_2_.table.refs_1_), custom_call_target="tpu_custom_call" | custom-call | flops 1024 | bytes 1024 | tf_op jit(solution)/shard_map/expand/pallas_call | solution.py:137
  99.6 3.2 %collective-permute-start.30 = (bf16[512,512]{1,0:T(8,128)(2,1)S(1)}, bf16[512,512]{1,0:T(8,128)(2,1)S(1)}, u32[]{:S(2)}, u32[]{:S(2)}) collective-permute-start(bf16[512,512]{1,0:T(8,128)(2,1)S(1)} %get-tuple-element.71), channel_id=1, source_target_pairs={{0,12},{4,0},{8,4},{12,8},{16,28},{20,16},{24,20},{28,24},{1,13},{... | collective-permute-start | bytes 1572872 | tf_op jit(solution)/shard_map/along_y3/ppermute | solution.py:259
  102.8 1.6 %collective-permute-start.28 = (bf16[256,512]{1,0:T(8,128)(2,1)S(1)}, bf16[256,512]{1,0:T(8,128)(2,1)S(1)}, u32[]{:S(2)}, u32[]{:S(2)}) collective-permute-start(bf16[256,512]{1,0:T(8,128)(2,1)S(1)} %expand.11), channel_id=1, source_target_pairs={{0,16},{4,20},{8,24},{12,28},{16,0},{20,4},{24,8},{28,12},{1,17},{... | collective-permute-start | bytes 786440 | tf_op jit(solution)/shard_map/across_x/ppermute | solution.py:255
  104.4 1.3 expand.13
  106.1 1.3 expand.14
  107.4 4.3 %collective-permute-done.28.refs_2_ = bf16[256,512]{1,0:T(8,128)(2,1)S(1)} collective-permute-done((bf16[256,512]{1,0:T(8,128)(2,1)S(1)}, bf16[256,512]{1,0:T(8,128)(2,1)S(1)}, u32[]{:S(2)}, u32[]{:S(2)}) %collective-permute-start.28) | collective-permute-done | bytes 262176 | tf_op jit(solution)/shard_map/across_x/ppermute | solution.py:255
  111.7 1.3 expand.15
  113.5 2.3 %collective-permute-start.31 = (bf16[256,512]{1,0:T(8,128)(2,1)S(1)}, bf16[256,512]{1,0:T(8,128)(2,1)S(1)}, u32[]{:S(2)}, u32[]{:S(2)}) collective-permute-start(bf16[256,512]{1,0:T(8,128)(2,1)S(1)} %expand.14), channel_id=1, source_target_pairs={{0,16},{4,20},{8,24},{12,28},{16,0},{20,4},{24,8},{28,12},{1,17},{... | collective-permute-start | bytes 786440 | tf_op jit(solution)/shard_map/across_x/ppermute | solution.py:255
  115.8 1.3 expand.16
  117.1 1.5 %collective-permute-start.34 = (bf16[256,512]{1,0:T(8,128)(2,1)S(1)}, bf16[256,512]{1,0:T(8,128)(2,1)S(1)}, u32[]{:S(2)}, u32[]{:S(2)}) collective-permute-start(bf16[256,512]{1,0:T(8,128)(2,1)S(1)} %expand.16), channel_id=1, source_target_pairs={{0,16},{4,20},{8,24},{12,28},{16,0},{20,4},{24,8},{28,12},{1,17},{... | collective-permute-start | bytes 786440 | tf_op jit(solution)/shard_map/across_x/ppermute | solution.py:255
  118.6 1.3 %collective-permute-done.32 = bf16[256,512]{1,0:T(8,128)(2,1)S(1)} collective-permute-done((bf16[256,512]{1,0:T(8,128)(2,1)S(1)}, bf16[256,512]{1,0:T(8,128)(2,1)S(1)}, u32[]{:S(2)}, u32[]{:S(2)}) %collective-permute-start.32) | collective-permute-done | bytes 262176 | tf_op jit(solution)/shard_map/along_y1/ppermute | solution.py:259
  120.0 3.2 %collective-permute-start.36 = (bf16[256,512]{1,0:T(8,128)(2,1)S(1)}, bf16[256,512]{1,0:T(8,128)(2,1)S(1)}, u32[]{:S(2)}, u32[]{:S(2)}) collective-permute-start(bf16[256,512]{1,0:T(8,128)(2,1)S(1)} %collective-permute-done.35), channel_id=1, source_target_pairs={{0,12},{4,0},{8,4},{12,8},{16,28},{20,16},{24,20},{28,24},{1,13},{... | collective-permute-start | bytes 786440 | tf_op jit(solution)/shard_map/along_y3/ppermute | solution.py:259
  123.4 1.9 %expand.17.total = f32[512,512]{1,0:T(8,128)S(1)} custom-call(s32[10]{0:T(128)S(1)} %pad_add_fusion.at_ref, bf16[256,2048]{1,0:T(8,128)(2,1)S(1)} %constant_dynamic-update-slice_fusion.2.refs_0_, bf16[256,2048]{1,0:T(8,128)(2,1)S(1)} %pad_maximum_fusion.refs_0_.refs_1_, bf16[4096,2048]{1,0:T(8,128)(2,1)S(1)} %get-tuple-element.43.refs_2_.table.refs_1_, ...), custom_call_target="tpu_custom_call" | custom-call | flops 1024 | bytes 1024 | tf_op jit(solution)/shard_map/expand/pallas_call | solution.py:137
  125.3 2.8 %collective-permute-done.33.refs_0_ = bf16[256,512]{1,0:T(8,128)(2,1)S(1)} collective-permute-done((bf16[256,512]{1,0:T(8,128)(2,1)S(1)}, bf16[256,512]{1,0:T(8,128)(2,1)S(1)}, u32[]{:S(2)}, u32[]{:S(2)}) %collective-permute-start.33) | collective-permute-done | bytes 262176 | tf_op jit(solution)/shard_map/along_y1/ppermute | solution.py:259
  128.1 1.6 %finish.1 = f32[512,512]{1,0:T(8,128)} custom-call(s32[10]{0:T(128)S(1)} %pad_add_fusion.at_ref, f32[512,512]{1,0:T(8,128)S(1)} %expand.17.total, bf16[256,512]{1,0:T(8,128)(2,1)S(1)} %collective-permute-done.33.refs_0_, bf16[256,512]{1,0:T(8,128)(2,1)S(1)} %collective-permute-done.34.refs_1_, bf16[256,512]{1,0:T(8,128)(2,1)S(1)} %collective-permute-done.36.refs_2_), custom_call_target="tpu_custom_call" | custom-call | flops 1024 | bytes 1024 | tf_op jit(solution)/shard_map/finish/pallas_call | solution.py:232
  (68 shorter events, 14.1 us)
Async XLA Ops:
  0.0 15.2 %collective-permute-start = (bf16[512,512]{1,0:T(8,128)(2,1)}, bf16[512,512]{1,0:T(8,128)(2,1)S(1)}, u32[]{:S(2)}, u32[]{:S(2)}) collective-permute-start(bf16[512,512]{1,0:T(8,128)(2,1)} %bitcast.6), channel_id=1, source_target_pairs={{0,4},{4,8},{8,12},{12,0},{16,20},{20,24},{24,28},{28,16},{1,5},{5... | collective-permute-start | bytes 1572872 | tf_op jit(solution)/shard_map/along_y1/ppermute | solution.py:259
  1.7 14.0 %collective-permute-start.2 = (bf16[512,512]{1,0:T(8,128)(2,1)}, bf16[512,512]{1,0:T(8,128)(2,1)S(1)}, u32[]{:S(2)}, u32[]{:S(2)}) collective-permute-start(bf16[512,512]{1,0:T(8,128)(2,1)} %bitcast.7), channel_id=1, source_target_pairs={{0,12},{4,0},{8,4},{12,8},{16,28},{20,16},{24,20},{28,24},{1,13},{... | collective-permute-start | bytes 1572872 | tf_op jit(solution)/shard_map/along_y3/ppermute | solution.py:259
  3.2 15.4 %collective-permute-start.5 = (bf16[512,512]{1,0:T(8,128)(2,1)}, bf16[512,512]{1,0:T(8,128)(2,1)S(1)}, u32[]{:S(2)}, u32[]{:S(2)}) collective-permute-start(bf16[512,512]{1,0:T(8,128)(2,1)} %bitcast.8), channel_id=1, source_target_pairs={{0,16},{4,20},{8,24},{12,28},{16,0},{20,4},{24,8},{28,12},{1,17},{... | collective-permute-start | bytes 1572872 | tf_op jit(solution)/shard_map/across_x/ppermute | solution.py:255
  7.1 1.0 copy-start
  15.3 10.5 %collective-permute-start.1 = (bf16[256,512]{1,0:T(8,128)(2,1)S(1)}, bf16[256,512]{1,0:T(8,128)(2,1)S(1)}, u32[]{:S(2)}, u32[]{:S(2)}) collective-permute-start(bf16[256,512]{1,0:T(8,128)(2,1)S(1)} %slice.44), channel_id=1, source_target_pairs={{0,4},{4,8},{8,12},{12,0},{16,20},{20,24},{24,28},{28,16},{1,5},{5... | collective-permute-start | bytes 786440 | tf_op jit(solution)/shard_map/along_y1/ppermute | solution.py:259
  15.7 10.1 %collective-permute-start.3 = (bf16[256,512]{1,0:T(8,128)(2,1)S(1)}, bf16[256,512]{1,0:T(8,128)(2,1)S(1)}, u32[]{:S(2)}, u32[]{:S(2)}) collective-permute-start(bf16[256,512]{1,0:T(8,128)(2,1)S(1)} %slice.45), channel_id=1, source_target_pairs={{0,12},{4,0},{8,4},{12,8},{16,28},{20,16},{24,20},{28,24},{1,13},{... | collective-permute-start | bytes 786440 | tf_op jit(solution)/shard_map/along_y3/ppermute | solution.py:259
  18.7 16.5 %collective-permute-start.6 = (bf16[512,512]{1,0:T(8,128)(2,1)S(1)}, bf16[512,512]{1,0:T(8,128)(2,1)S(1)}, u32[]{:S(2)}, u32[]{:S(2)}) collective-permute-start(bf16[512,512]{1,0:T(8,128)(2,1)S(1)} %collective-permute-done.5.refs_0_), channel_id=1, source_target_pairs={{0,12},{4,0},{8,4},{12,8},{16,28},{20,16},{24,20},{28,24},{1,13},{... | collective-permute-start | bytes 1572872 | tf_op jit(solution)/shard_map/along_y3/ppermute | solution.py:259
  19.9 15.3 %collective-permute-start.7 = (bf16[512,512]{1,0:T(8,128)(2,1)S(1)}, bf16[512,512]{1,0:T(8,128)(2,1)S(1)}, u32[]{:S(2)}, u32[]{:S(2)}) collective-permute-start(bf16[512,512]{1,0:T(8,128)(2,1)S(1)} %collective-permute-done.5.refs_0_), channel_id=1, source_target_pairs={{0,4},{4,8},{8,12},{12,0},{16,20},{20,24},{24,28},{28,16},{1,5},{5... | collective-permute-start | bytes 1572872 | tf_op jit(solution)/shard_map/along_y1/ppermute | solution.py:259
  25.8 12.5 %collective-permute-start.4 = (bf16[512,512]{1,0:T(8,128)(2,1)S(1)}, bf16[512,512]{1,0:T(8,128)(2,1)S(1)}, u32[]{:S(2)}, u32[]{:S(2)}) collective-permute-start(bf16[512,512]{1,0:T(8,128)(2,1)S(1)} %constant_dynamic-update-slice_fusion.refs_1_), channel_id=1, source_target_pairs={{0,16},{4,20},{8,24},{12,28},{16,0},{20,4},{24,8},{28,12},{1,17},{... | collective-permute-start | bytes 1572872 | tf_op jit(solution)/shard_map/across_x/ppermute | solution.py:255
  39.6 2.7 %collective-permute-start.8 = (bf16[256,2048]{1,0:T(8,128)(2,1)S(1)}, bf16[256,2048]{1,0:T(8,128)(2,1)S(1)}, u32[]{:S(2)}, u32[]{:S(2)}) collective-permute-start(bf16[256,2048]{1,0:T(8,128)(2,1)S(1)} %project_last.2), channel_id=1, source_target_pairs={{0,32},{32,0},{64,96},{96,64},{1,33},{33,1},{65,97},{97,65},{2,34}... | collective-permute-start | bytes 3145736 | tf_op jit(solution)/shard_map/other_core/ppermute | solution.py:267
  42.7 18.8 %copy-start.1 = (bf16[256,256]{1,0:T(8,128)(2,1)S(1)}, bf16[256,256]{1,0:T(8,128)(2,1)}, u32[]{:S(2)}) copy-start(bf16[256,256]{1,0:T(8,128)(2,1)} %turn.1) | copy-start | bytes 393220
  42.7 18.8 %copy-start.2 = (f32[2048]{0:T(1024)S(1)}, f32[2048]{0:T(1024)}, u32[]{:S(2)}) copy-start(f32[2048]{0:T(1024)} %param.10) | copy-start | bytes 24580
  42.7 18.8 %copy-start.3 = (f32[256]{0:T(256)S(1)}, f32[256]{0:T(256)}, u32[]{:S(2)}) copy-start(f32[256]{0:T(256)} %param.12) | copy-start | bytes 3076
  42.8 6.4 %collective-permute-start.12 = (bf16[128,512]{1,0:T(8,128)(2,1)S(1)}, bf16[128,512]{1,0:T(8,128)(2,1)S(1)}, u32[]{:S(2)}, u32[]{:S(2)}) collective-permute-start(bf16[128,512]{1,0:T(8,128)(2,1)S(1)} %get-tuple-element.77), channel_id=1, source_target_pairs={{0,64},{32,96},{64,0},{96,32},{1,65},{33,97},{65,1},{97,33},{2,66}... | collective-permute-start | bytes 393224 | tf_op jit(solution)/shard_map/other_x/ppermute | solution.py:271
  44.8 8.4 %collective-permute-start.11 = (bf16[128,512]{1,0:T(8,128)(2,1)S(1)}, bf16[128,512]{1,0:T(8,128)(2,1)S(1)}, u32[]{:S(2)}, u32[]{:S(2)}) collective-permute-start(bf16[128,512]{1,0:T(8,128)(2,1)S(1)} %get-tuple-element.78), channel_id=1, source_target_pairs={{0,64},{32,96},{64,0},{96,32},{1,65},{33,97},{65,1},{97,33},{2,66}... | collective-permute-start | bytes 393224 | tf_op jit(solution)/shard_map/other_x/ppermute | solution.py:271
  45.6 9.2 %collective-permute-start.10 = (bf16[128,512]{1,0:T(8,128)(2,1)S(1)}, bf16[128,512]{1,0:T(8,128)(2,1)S(1)}, u32[]{:S(2)}, u32[]{:S(2)}) collective-permute-start(bf16[128,512]{1,0:T(8,128)(2,1)S(1)} %get-tuple-element.79), channel_id=1, source_target_pairs={{0,64},{32,96},{64,0},{96,32},{1,65},{33,97},{65,1},{97,33},{2,66}... | collective-permute-start | bytes 393224 | tf_op jit(solution)/shard_map/other_x/ppermute | solution.py:271
  46.9 12.1 %collective-permute-start.9 = (bf16[128,512]{1,0:T(8,128)(2,1)S(1)}, bf16[128,512]{1,0:T(8,128)(2,1)S(1)}, u32[]{:S(2)}, u32[]{:S(2)}) collective-permute-start(bf16[128,512]{1,0:T(8,128)(2,1)S(1)} %get-tuple-element.80), channel_id=1, source_target_pairs={{0,64},{32,96},{64,0},{96,32},{1,65},{33,97},{65,1},{97,33},{2,66}... | collective-permute-start | bytes 393224 | tf_op jit(solution)/shard_map/other_x/ppermute | solution.py:271
  49.2 12.3 %collective-permute-start.14 = (bf16[128,512]{1,0:T(8,128)(2,1)S(1)}, bf16[128,512]{1,0:T(8,128)(2,1)S(1)}, u32[]{:S(2)}, u32[]{:S(2)}) collective-permute-start(bf16[128,512]{1,0:T(8,128)(2,1)S(1)} %fusion), channel_id=1, source_target_pairs={{0,2},{1,3},{2,0},{3,1},{4,6},{5,7},{6,4},{7,5},{8,10},{9,11},{10,... | collective-permute-start | bytes 393224 | tf_op jit(solution)/shard_map/along_z2/ppermute | solution.py:263
  53.2 8.3 %collective-permute-start.13 = (bf16[128,512]{1,0:T(8,128)(2,1)S(1)}, bf16[128,512]{1,0:T(8,128)(2,1)S(1)}, u32[]{:S(2)}, u32[]{:S(2)}) collective-permute-start(bf16[128,512]{1,0:T(8,128)(2,1)S(1)} %fusion.1), channel_id=1, source_target_pairs={{0,1},{1,2},{2,3},{3,0},{4,5},{5,6},{6,7},{7,4},{8,9},{9,10},{10,1... | collective-permute-start | bytes 393224 | tf_op jit(solution)/shard_map/along_z1/ppermute | solution.py:263
  54.9 6.6 %collective-permute-start.15 = (bf16[128,512]{1,0:T(8,128)(2,1)S(1)}, bf16[128,512]{1,0:T(8,128)(2,1)S(1)}, u32[]{:S(2)}, u32[]{:S(2)}) collective-permute-start(bf16[128,512]{1,0:T(8,128)(2,1)S(1)} %fusion.2), channel_id=1, source_target_pairs={{0,3},{1,0},{2,1},{3,2},{4,7},{5,4},{6,5},{7,6},{8,11},{9,8},{10,9... | collective-permute-start | bytes 393224 | tf_op jit(solution)/shard_map/along_z3/ppermute | solution.py:263
  62.7 6.5 %collective-permute-start.17 = (bf16[128,512]{1,0:T(8,128)(2,1)S(1)}, bf16[128,512]{1,0:T(8,128)(2,1)S(1)}, u32[]{:S(2)}, u32[]{:S(2)}) collective-permute-start(bf16[128,512]{1,0:T(8,128)(2,1)S(1)} %get-tuple-element.49.refs_0_), channel_id=1, source_target_pairs={{0,64},{32,96},{64,0},{96,32},{1,65},{33,97},{65,1},{97,33},{2,66}... | collective-permute-start | bytes 393224 | tf_op jit(solution)/shard_map/other_x/ppermute | solution.py:271
  64.1 7.0 %collective-permute-start.19 = (bf16[128,512]{1,0:T(8,128)(2,1)S(1)}, bf16[128,512]{1,0:T(8,128)(2,1)S(1)}, u32[]{:S(2)}, u32[]{:S(2)}) collective-permute-start(bf16[128,512]{1,0:T(8,128)(2,1)S(1)} %get-tuple-element.54), channel_id=1, source_target_pairs={{0,1},{1,2},{2,3},{3,0},{4,5},{5,6},{6,7},{7,4},{8,9},{9,10},{10,1... | collective-permute-start | bytes 393224 | tf_op jit(solution)/shard_map/along_z1/ppermute | solution.py:263
  64.4 9.1 %collective-permute-start.18 = (bf16[128,512]{1,0:T(8,128)(2,1)S(1)}, bf16[128,512]{1,0:T(8,128)(2,1)S(1)}, u32[]{:S(2)}, u32[]{:S(2)}) collective-permute-start(bf16[128,512]{1,0:T(8,128)(2,1)S(1)} %get-tuple-element.52), channel_id=1, source_target_pairs={{0,2},{1,3},{2,0},{3,1},{4,6},{5,7},{6,4},{7,5},{8,10},{9,11},{10,... | collective-permute-start | bytes 393224 | tf_op jit(solution)/shard_map/along_z2/ppermute | solution.py:263
  69.2 5.0 %collective-permute-start.16 = (bf16[128,512]{1,0:T(8,128)(2,1)S(1)}, bf16[128,512]{1,0:T(8,128)(2,1)S(1)}, u32[]{:S(2)}, u32[]{:S(2)}) collective-permute-start(bf16[128,512]{1,0:T(8,128)(2,1)S(1)} %get-tuple-element.50), channel_id=1, source_target_pairs={{0,3},{1,0},{2,1},{3,2},{4,7},{5,4},{6,5},{7,6},{8,11},{9,8},{10,9... | collective-permute-start | bytes 393224 | tf_op jit(solution)/shard_map/along_z3/ppermute | solution.py:263
  74.8 2.0 %collective-permute-start.20 = (bf16[128,2048]{1,0:T(8,128)(2,1)S(1)}, bf16[128,2048]{1,0:T(8,128)(2,1)S(1)}, u32[]{:S(2)}, u32[]{:S(2)}) collective-permute-start(bf16[128,2048]{1,0:T(8,128)(2,1)S(1)} %get-tuple-element.56), channel_id=1, source_target_pairs={{0,32},{32,0},{64,96},{96,64},{1,33},{33,1},{65,97},{97,65},{2,34}... | collective-permute-start | bytes 1572872 | tf_op jit(solution)/shard_map/other_core/ppermute | solution.py:267
  74.9 11.5 %collective-permute-start.21 = (bf16[384,512]{1,0:T(8,128)(2,1)S(1)}, bf16[384,512]{1,0:T(8,128)(2,1)S(1)}, u32[]{:S(2)}, u32[]{:S(2)}) collective-permute-start(bf16[384,512]{1,0:T(8,128)(2,1)S(1)} %get-tuple-element.57), channel_id=1, source_target_pairs={{0,64},{32,96},{64,0},{96,32},{1,65},{33,97},{65,1},{97,33},{2,66}... | collective-permute-start | bytes 1179656 | tf_op jit(solution)/shard_map/other_x/ppermute | solution.py:271
  78.7 9.7 %collective-permute-start.22 = (bf16[256,512]{1,0:T(8,128)(2,1)S(1)}, bf16[256,512]{1,0:T(8,128)(2,1)S(1)}, u32[]{:S(2)}, u32[]{:S(2)}) collective-permute-start(bf16[256,512]{1,0:T(8,128)(2,1)S(1)} %get-tuple-element.58), channel_id=1, source_target_pairs={{0,4},{4,8},{8,12},{12,0},{16,20},{20,24},{24,28},{28,16},{1,5},{5... | collective-permute-start | bytes 786440 | tf_op jit(solution)/shard_map/along_y1/ppermute | solution.py:259
  79.2 9.2 %collective-permute-start.23 = (bf16[256,512]{1,0:T(8,128)(2,1)S(1)}, bf16[256,512]{1,0:T(8,128)(2,1)S(1)}, u32[]{:S(2)}, u32[]{:S(2)}) collective-permute-start(bf16[256,512]{1,0:T(8,128)(2,1)S(1)} %get-tuple-element.61), channel_id=1, source_target_pairs={{0,12},{4,0},{8,4},{12,8},{16,28},{20,16},{24,20},{28,24},{1,13},{... | collective-permute-start | bytes 786440 | tf_op jit(solution)/shard_map/along_y3/ppermute | solution.py:259
  89.0 4.0 %collective-permute-start.24 = (bf16[128,2048]{1,0:T(8,128)(2,1)S(1)}, bf16[128,2048]{1,0:T(8,128)(2,1)S(1)}, u32[]{:S(2)}, u32[]{:S(2)}) collective-permute-start(bf16[128,2048]{1,0:T(8,128)(2,1)S(1)} %assemble.3), channel_id=1, source_target_pairs={{0,32},{32,0},{64,96},{96,64},{1,33},{33,1},{65,97},{97,65},{2,34}... | collective-permute-start | bytes 1572872 | tf_op jit(solution)/shard_map/other_core/ppermute | solution.py:267
  89.1 13.7 %collective-permute-start.25 = (bf16[256,512]{1,0:T(8,128)(2,1)S(1)}, bf16[256,512]{1,0:T(8,128)(2,1)S(1)}, u32[]{:S(2)}, u32[]{:S(2)}) collective-permute-start(bf16[256,512]{1,0:T(8,128)(2,1)S(1)} %get-tuple-element.60), channel_id=1, source_target_pairs={{0,16},{4,20},{8,24},{12,28},{16,0},{20,4},{24,8},{28,12},{1,17},{... | collective-permute-start | bytes 786440 | tf_op jit(solution)/shard_map/across_x/ppermute | solution.py:255
  91.9 13.8 %collective-permute-start.26 = (bf16[256,512]{1,0:T(8,128)(2,1)S(1)}, bf16[256,512]{1,0:T(8,128)(2,1)S(1)}, u32[]{:S(2)}, u32[]{:S(2)}) collective-permute-start(bf16[256,512]{1,0:T(8,128)(2,1)S(1)} %get-tuple-element.66), channel_id=1, source_target_pairs={{0,4},{4,8},{8,12},{12,0},{16,20},{20,24},{24,28},{28,16},{1,5},{5... | collective-permute-start | bytes 786440 | tf_op jit(solution)/shard_map/along_y1/ppermute | solution.py:259
  93.2 12.9 %collective-permute-start.27 = (bf16[256,512]{1,0:T(8,128)(2,1)S(1)}, bf16[256,512]{1,0:T(8,128)(2,1)S(1)}, u32[]{:S(2)}, u32[]{:S(2)}) collective-permute-start(bf16[256,512]{1,0:T(8,128)(2,1)S(1)} %get-tuple-element.67), channel_id=1, source_target_pairs={{0,12},{4,0},{8,4},{12,8},{16,28},{20,16},{24,20},{28,24},{1,13},{... | collective-permute-start | bytes 786440 | tf_op jit(solution)/shard_map/along_y3/ppermute | solution.py:259
  99.5 16.3 %collective-permute-start.29 = (bf16[512,512]{1,0:T(8,128)(2,1)S(1)}, bf16[512,512]{1,0:T(8,128)(2,1)S(1)}, u32[]{:S(2)}, u32[]{:S(2)}) collective-permute-start(bf16[512,512]{1,0:T(8,128)(2,1)S(1)} %get-tuple-element.64), channel_id=1, source_target_pairs={{0,4},{4,8},{8,12},{12,0},{16,20},{20,24},{24,28},{28,16},{1,5},{5... | collective-permute-start | bytes 1572872 | tf_op jit(solution)/shard_map/along_y1/ppermute | solution.py:259
  99.6 16.2 %collective-permute-start.30 = (bf16[512,512]{1,0:T(8,128)(2,1)S(1)}, bf16[512,512]{1,0:T(8,128)(2,1)S(1)}, u32[]{:S(2)}, u32[]{:S(2)}) collective-permute-start(bf16[512,512]{1,0:T(8,128)(2,1)S(1)} %get-tuple-element.71), channel_id=1, source_target_pairs={{0,12},{4,0},{8,4},{12,8},{16,28},{20,16},{24,20},{28,24},{1,13},{... | collective-permute-start | bytes 1572872 | tf_op jit(solution)/shard_map/along_y3/ppermute | solution.py:259
  102.8 8.8 %collective-permute-start.28 = (bf16[256,512]{1,0:T(8,128)(2,1)S(1)}, bf16[256,512]{1,0:T(8,128)(2,1)S(1)}, u32[]{:S(2)}, u32[]{:S(2)}) collective-permute-start(bf16[256,512]{1,0:T(8,128)(2,1)S(1)} %expand.11), channel_id=1, source_target_pairs={{0,16},{4,20},{8,24},{12,28},{16,0},{20,4},{24,8},{28,12},{1,17},{... | collective-permute-start | bytes 786440 | tf_op jit(solution)/shard_map/across_x/ppermute | solution.py:255
  105.7 14.2 %collective-permute-start.32 = (bf16[256,512]{1,0:T(8,128)(2,1)S(1)}, bf16[256,512]{1,0:T(8,128)(2,1)S(1)}, u32[]{:S(2)}, u32[]{:S(2)}) collective-permute-start(bf16[256,512]{1,0:T(8,128)(2,1)S(1)} %expand.13), channel_id=1, source_target_pairs={{0,4},{4,8},{8,12},{12,0},{16,20},{20,24},{24,28},{28,16},{1,5},{5... | collective-permute-start | bytes 786440 | tf_op jit(solution)/shard_map/along_y1/ppermute | solution.py:259
  112.9 7.0 %collective-permute-start.35 = (bf16[256,512]{1,0:T(8,128)(2,1)S(1)}, bf16[256,512]{1,0:T(8,128)(2,1)S(1)}, u32[]{:S(2)}, u32[]{:S(2)}) collective-permute-start(bf16[256,512]{1,0:T(8,128)(2,1)S(1)} %expand.15), channel_id=1, source_target_pairs={{0,12},{4,0},{8,4},{12,8},{16,28},{20,16},{24,20},{28,24},{1,13},{... | collective-permute-start | bytes 786440 | tf_op jit(solution)/shard_map/along_y3/ppermute | solution.py:259
  113.5 9.9 %collective-permute-start.31 = (bf16[256,512]{1,0:T(8,128)(2,1)S(1)}, bf16[256,512]{1,0:T(8,128)(2,1)S(1)}, u32[]{:S(2)}, u32[]{:S(2)}) collective-permute-start(bf16[256,512]{1,0:T(8,128)(2,1)S(1)} %expand.14), channel_id=1, source_target_pairs={{0,16},{4,20},{8,24},{12,28},{16,0},{20,4},{24,8},{28,12},{1,17},{... | collective-permute-start | bytes 786440 | tf_op jit(solution)/shard_map/across_x/ppermute | solution.py:255
  117.1 11.0 %collective-permute-start.34 = (bf16[256,512]{1,0:T(8,128)(2,1)S(1)}, bf16[256,512]{1,0:T(8,128)(2,1)S(1)}, u32[]{:S(2)}, u32[]{:S(2)}) collective-permute-start(bf16[256,512]{1,0:T(8,128)(2,1)S(1)} %expand.16), channel_id=1, source_target_pairs={{0,16},{4,20},{8,24},{12,28},{16,0},{20,4},{24,8},{28,12},{1,17},{... | collective-permute-start | bytes 786440 | tf_op jit(solution)/shard_map/across_x/ppermute | solution.py:255
  119.9 8.2 %collective-permute-start.33 = (bf16[256,512]{1,0:T(8,128)(2,1)S(1)}, bf16[256,512]{1,0:T(8,128)(2,1)S(1)}, u32[]{:S(2)}, u32[]{:S(2)}) collective-permute-start(bf16[256,512]{1,0:T(8,128)(2,1)S(1)} %collective-permute-done.32), channel_id=1, source_target_pairs={{0,4},{4,8},{8,12},{12,0},{16,20},{20,24},{24,28},{28,16},{1,5},{5... | collective-permute-start | bytes 786440 | tf_op jit(solution)/shard_map/along_y1/ppermute | solution.py:259
  120.0 8.1 %collective-permute-start.36 = (bf16[256,512]{1,0:T(8,128)(2,1)S(1)}, bf16[256,512]{1,0:T(8,128)(2,1)S(1)}, u32[]{:S(2)}, u32[]{:S(2)}) collective-permute-start(bf16[256,512]{1,0:T(8,128)(2,1)S(1)} %collective-permute-done.35), channel_id=1, source_target_pairs={{0,12},{4,0},{8,4},{12,8},{16,28},{20,16},{24,20},{28,24},{1,13},{... | collective-permute-start | bytes 786440 | tf_op jit(solution)/shard_map/along_y3/ppermute | solution.py:259
